TPU v7x, 32 devices: a whole 2x2x4 slice. The times are simulated.
32 devices in a mesh: dp: 8 (over z, y), tm: 4 (over x, core).
Axes of the slice: x: 2, y: 2, z: 4, core: 2. Of those that a mesh axis runs over, the one named last changes fastest.
Arguments:
- latents: bfloat16 [8, 16, 16, 16, 640], P('dp', 'tm'), may hold values from -60 to 60
- cotangent: bfloat16 [8, 8, 16, 16, 640], P('dp', 'tm'), may hold values from -6 to 6
- timesteps: int32 [8], P('dp'), may hold values from 0 to 999
- spatial_weight: bfloat16 [640, 5760], P('dp'), may hold values from -0.078125 to 0.078125
- temporal_weight: bfloat16 [640, 1920], P('dp'), may hold values from -0.125 to 0.125
- time_weight: bfloat16 [640, 256], P('dp'), may hold values from -0.375 to 0.375
Outputs:
- downsampled: float32 [8, 8, 16, 16, 640], P('dp', 'tm')
- latents_grad: float32 [8, 16, 16, 16, 640], P('dp', 'tm')
- spatial_grad: float32 [640, 5760], P('dp')
- temporal_grad: float32 [640, 1920], P('dp')
- time_grad: float32 [640, 256], P('dp')
All inputs are finite; a program needn't handle non-finite values.
Results may differ from a plain program's by a relative error of at most 0.0041.
Values may be sent and summed in bfloat16 or wider, within the bound.
No kernel may reach another device: no remote copies, remote signals or barrier semaphores. Data moves between devices by JAX's collectives and lax.ppermute only.
A program may use at most 128 MiB of HBM per device.

v0:
```python
import math

import jax
import jax.numpy as jnp
from jax import lax
from jax.sharding import PartitionSpec as P

GROUPS = 32


epsilon = 1e-05
log_base = math.log(10000.0)


def from_behind(x, axis, by):
    count = lax.axis_size(axis)
    pairs = [(i, i + by) for i in range(count) if 0 <= i + by < count]
    return lax.ppermute(x, axis, pairs)


def embedding(diffusion_step, embed_width):
    half_width = embed_width // 2
    frequency = jnp.exp(-log_base * jnp.arange(half_width, dtype=jnp.float32) / half_width)
    angles = diffusion_step.astype(jnp.float32) * frequency
    return jnp.concatenate([jnp.cos(angles), jnp.sin(angles)])


def normalize(frames):
    frame_count, height, breadth, channels = frames.shape
    grouped = frames.astype(jnp.float32).reshape(
        frame_count, height * breadth, GROUPS, channels // GROUPS
    )
    center = jnp.mean(grouped, axis=(1, 3), keepdims=True)
    deviation = grouped - center
    variance = jnp.mean(deviation * deviation, axis=(1, 3), keepdims=True)
    scaled = lax.rsqrt(variance + epsilon)
    return (deviation * scaled, scaled)


def spatial_columns(activation):
    frame_count, height, breadth, channels = activation.shape
    padded = jnp.pad(activation, ((0, 0), (1, 1), (1, 1), (0, 0)))
    shifted_views = [
        padded[:, row_shift : row_shift + height, col_shift : col_shift + breadth, :]
        for row_shift in range(3)
        for col_shift in range(3)
    ]
    return jnp.stack(shifted_views, axis=3).reshape(frame_count * height * breadth, 9, channels)


def spatial_fold(pieces, frame_count, height, breadth):
    channels = pieces.shape[-1]
    layout = pieces.reshape(frame_count, height, breadth, 9, channels)
    total = jnp.zeros((frame_count, height + 2, breadth + 2, channels), jnp.float32)
    for row_shift in range(3):
        for col_shift in range(3):
            placed = jnp.pad(
                layout[:, :, :, 3 * row_shift + col_shift, :],
                ((0, 0), (row_shift, 2 - row_shift), (col_shift, 2 - col_shift), (0, 0)),
            )
            total = total + placed
    return total[:, 1 : height + 1, 1 : breadth + 1, :]


def temporal_columns(extended):
    out_count = (extended.shape[0] - 1) // 2
    taps = [extended[offset : offset + 2 * out_count : 2] for offset in range(3)]
    return jnp.stack(taps, axis=2).reshape(out_count * extended.shape[1], 3, extended.shape[2])


def temporal_back(parts, incoming):
    lead_tap = parts[:, :, 0, :]
    mid_tap = parts[:, :, 1, :]
    tail_tap = parts[:, :, 2, :]
    even_frames = jnp.concatenate([lead_tap[1:], incoming[None]], axis=0) + tail_tap
    merged = jnp.stack([mid_tap, even_frames], axis=1)
    return (merged.reshape(2 * parts.shape[0], parts.shape[1], parts.shape[3]), lead_tap[0])


def spatial_forward(frames, spatial_taps, time_shift):
    frame_count, height, breadth, channels = frames.shape
    normal, scaled = normalize(frames)
    activation = (
        jax.nn.silu(normal).reshape(frame_count, height, breadth, channels).astype(jnp.bfloat16)
    )
    columns = spatial_columns(activation)
    conv_sum = (
        jnp.einsum("rkc,ckq->rq", columns, spatial_taps, preferred_element_type=jnp.float32)
        + time_shift
    )
    hidden = conv_sum.astype(jnp.bfloat16).reshape(frame_count, height * breadth, channels)
    return (hidden, normal, scaled, columns)


def body(latents, cotangent, timesteps, spatial_weight, temporal_weight, time_weight):
    clip_frames = latents[0]
    frame_count, height, breadth, channels = clip_frames.shape
    pixels = height * breadth
    out_count = frame_count // 2
    spatial_full, temporal_full, time_full = (
        lax.all_gather(spatial_weight, "dp", axis=0, tiled=True),
        lax.all_gather(temporal_weight, "dp", axis=0, tiled=True),
        lax.all_gather(time_weight, "dp", axis=0, tiled=True),
    )
    spatial_taps = spatial_full.reshape(channels, 9, channels)
    temporal_taps = temporal_full.reshape(channels, 3, channels)
    embedded = embedding(timesteps[0], time_full.shape[1])
    time_shift = jnp.dot(time_full.astype(jnp.float32), embedded, precision=lax.Precision.HIGHEST)
    hidden, normal, scaled, columns = spatial_forward(clip_frames, spatial_taps, time_shift)
    before = from_behind(hidden[-1], "tm", 1)
    extended = jnp.concatenate([before[None], hidden], axis=0)
    tcols = temporal_columns(extended)
    result = jnp.einsum("rkc,ckq->rq", tcols, temporal_taps, preferred_element_type=jnp.float32)
    downsampled = result.reshape(1, out_count, height, breadth, channels)
    grad_out = cotangent[0].reshape(out_count * pixels, channels)
    parts = jnp.einsum(
        "rq,ckq->rkc", grad_out, temporal_taps, preferred_element_type=jnp.float32
    ).reshape(out_count, pixels, 3, channels)
    local_grad, leaving = temporal_back(parts, jnp.zeros((pixels, channels), jnp.float32))
    arriving = from_behind(leaving, "tm", -1)
    hidden_grad = local_grad.at[-1].add(arriving)
    hidden_back = hidden_grad.astype(jnp.bfloat16).reshape(frame_count * pixels, channels)
    shift_grad = jnp.sum(hidden_grad, axis=(0, 1))
    pieces = jnp.einsum(
        "rq,ckq->rkc", hidden_back, spatial_taps, preferred_element_type=jnp.float32
    )
    activation_grad = spatial_fold(pieces, frame_count, height, breadth)
    sigmoid_value = jax.nn.sigmoid(normal)
    derivative = sigmoid_value * (1.0 + normal * (1.0 - sigmoid_value))
    norm_grad = activation_grad.reshape(normal.shape) * derivative
    mean_one = jnp.mean(norm_grad, axis=(1, 3), keepdims=True)
    mean_two = jnp.mean(norm_grad * normal, axis=(1, 3), keepdims=True)
    input_grad = ((norm_grad - mean_one - normal * mean_two) * scaled).reshape(
        1, frame_count, height, breadth, channels
    )
    row_share = channels // lax.axis_size("dp")
    spatial_part = jnp.einsum(
        "rkc,rq->ckq", columns, hidden_back, preferred_element_type=jnp.float32
    )
    temporal_part = jnp.einsum("rkc,rq->ckq", tcols, grad_out, preferred_element_type=jnp.float32)
    time_part = shift_grad[:, None] * embedded[None, :]
    grad_shard = lax.psum_scatter(
        jnp.concatenate(
            [
                spatial_part.reshape(row_share * lax.axis_size("dp"), 9 * channels),
                temporal_part.reshape(row_share * lax.axis_size("dp"), 3 * channels),
                time_part,
            ],
            axis=1,
        ),
        "dp",
        scatter_dimension=0,
        tiled=True,
    )
    totals = lax.psum(grad_shard, "tm")
    spatial_grad = totals[:, : 9 * channels]
    temporal_grad = totals[:, 9 * channels : 12 * channels]
    time_grad = totals[:, 12 * channels :]
    return (downsampled, input_grad, spatial_grad, temporal_grad, time_grad)


def solution(mesh):
    placed = (
        P("dp", "tm", None, None, None),
        P("dp", "tm", None, None, None),
        P("dp"),
        P("dp", None),
        P("dp", None),
        P("dp", None),
    )
    return jax.shard_map(
        body,
        mesh=mesh,
        in_specs=placed,
        out_specs=(
            P("dp", "tm", None, None, None),
            P("dp", "tm", None, None, None),
            P("dp", None),
            P("dp", None),
            P("dp", None),
        ),
        check_vma=False,
    )
```

profile of v0, /device:TPU:0, one launch (start us, length us, event | category | flops | bytes accessed | tf_op | source)
XLA Modules:
  0.0 723.6 jit_solution(1900016296076289256)
XLA Ops:
  7.2 0.7 all-gather.5.cloned.1.call-update
  8.0 0.7 all-gather.3.cloned.1.call-update
  8.7 1.5 convert_reduce_fusion
  10.7 0.4 multiply_reduce_fusion.1
  12.2 33.4 %all_gather.10 = bf16[640,256]{1,0:T(8,128)(2,1)S(1)} all-gather(bf16[80,256]{1,0:T(8,128)(2,1)S(1)} %copy-done.14), channel_id=1, replica_groups=mesh['dp'=8,'tm'=4] {'dp'}, dimensions={0}, use_global_device_ids=true | all-gather | bytes 368640 | tf_op jit(solution)/shard_map/all_gather | solution.py:103
  45.6 0.4 convolution_reduce_fusion
  46.0 20.7 %all-gather.5.cloned.1.call-done = bf16[640,1920]{1,0:T(8,128)(2,1)} async-done(((bf16[80,1920]{1,0:T(8,128)(2,1)}), bf16[640,1920]{1,0:T(8,128)(2,1)}) %all-gather.5.cloned.1.call-update) | async-done | bytes 2457616 | tf_op jit(solution)/shard_map/all_gather | solution.py:102
  66.7 4.3 copy.34
  71.0 3.4 fusion.18
  74.5 1.5 collective-permute-start.1
  76.6 1.9 collective-permute-done.1
  78.7 0.3 fusion.13
  79.0 1.2 broadcast_multiply_fusion
  80.2 100.1 %all-gather.3.cloned.1.call-done = bf16[640,5760]{1,0:T(8,128)(2,1)} async-done(((bf16[80,5760]{1,0:T(8,128)(2,1)}), bf16[640,5760]{1,0:T(8,128)(2,1)}) %all-gather.3.cloned.1.call-update) | async-done | bytes 7372816 | tf_op jit(solution)/shard_map/all_gather | solution.py:101
  180.3 10.3 %copy.32 = bf16[640,5760]{0,1:T(8,128)(2,1)} copy(bf16[640,5760]{1,0:T(8,128)(2,1)} %all-gather.3.cloned.1.call-done) | data formatting | bytes 14745600 | tf_op jit(solution)/shard_map/all_gather | solution.py:101
  190.6 15.7 %fusion.16 = f32[1024,640,9]{1,0,2:T(8,128)} fusion(bf16[1024,640,1]{1,0,2:T(8,128)(2,1)S(1)} %bitcast.165, bf16[640,9,640]{0,2,1:T(8,128)(2,1)} %bitcast.137), kind=kOutput, calls=%fused_computation.78 | convolution fusion | flops 7549747200 | bytes 32276480 | tf_op jit(solution)/shard_map/rq,ckq->rkc/dot_general | solution.py:124
  206.2 13.8 %slice_bitcast_fusion.8 = (f32[4,16,16,640]{3,2,1,0:T(8,128)}, f32[4,16,16,640]{3,2,1,0:T(8,128)S(1)}, f32[4,16,16,640]{3,2,1,0:T(8,128)S(1)}, f32[4,16,16,640]{...) fusion(f32[4,16,16,9,640]{4,2,1,0,3:T(8,128)} %bitcast.132), kind=kLoop, calls=%fused_computation.24 | loop fusion | bytes 47185920 | tf_op jit(solution)/shard_map/squeeze | solution.py:58
  220.1 4.2 pad_add_fusion
  224.3 0.6 copy-done.3
  224.9 0.8 copy-done.4
  225.7 3.8 multiply_multiply_fusion
  229.4 1.0 fusion.12
  230.5 3.0 pad_slice_fusion
  234.7 0.8 constant_dynamic-update-slice_fusion.4
  235.6 4.4 copy-done.13
  239.9 1.2 constant_dynamic-update-slice_fusion.3
  241.1 1.2 constant_dynamic-update-slice_fusion.2
  242.3 1.2 constant_dynamic-update-slice_fusion.1
  243.5 1.2 constant_dynamic-update-slice_fusion
  244.6 12.7 %fusion.3 = bf16[1024,640]{1,0:T(8,128)(2,1)S(1)} fusion(bf16[1024,9,640]{2,0,1:T(8,128)(2,1)} %constant_dynamic-update-slice_fusion, bf16[640,9,640]{0,2,1:T(8,128)(2,1)S(1)} %bitcast.140, f32[640]{0:T(1024)S(1)} %convolution_reduce_fusion), kind=kOutput, calls=%fused_computation.31 | convolution fusion | flops 7551057920 | bytes 20482560 | tf_op jit(solution)/shard_map/rkc,ckq->rq/dot_general | solution.py:88
  257.4 0.8 slice.149
  258.1 2.1 collective-permute-start
  260.2 15.0 %fusion.17 = f32[640,9,640]{2,0,1:T(8,128)} fusion(bf16[1024,640,1]{1,0,2:T(8,128)(2,1)S(1)} %bitcast.166, bf16[1024,9,640]{2,0,1:T(8,128)(2,1)} %constant_dynamic-update-slice_fusion), kind=kOutput, calls=%fused_computation.79 | convolution fusion | flops 7549747200 | bytes 27852800 | tf_op jit(solution)/shard_map/rkc,rq->ckq/dot_general | solution.py:137
  275.2 15.1 %copy.44 = f32[640,5760]{1,0:T(8,128)} copy(f32[640,5760]{0,1:T(8,128)} %bitcast.133) | data formatting | bytes 29491200 | tf_op jit(solution)/shard_map/reshape | solution.py:145
  290.5 1.4 pad_maximum_fusion.3
  291.9 3.9 fusion.11
  295.8 6.0 copy.45
  301.8 15.2 %pad_maximum_fusion = f32[640,7936]{1,0:T(8,128)} fusion(f32[640,256]{1,0:T(8,128)S(1)} %copy-done.9, f32[640,1920]{1,0:T(8,128)} %copy.45, f32[640,5760]{1,0:T(8,128)} %copy.44), kind=kLoop, calls=%fused_computation | loop fusion | flops 10158080 | bytes 40632320 | tf_op jit(solution)/shard_map/concatenate | solution.py:143
  317.9 332.6 %reduce-scatter.2.cloned.1.call-done = f32[80,7936]{1,0:T(8,128)} async-done(((f32[640,7936]{1,0:T(8,128)}), f32[80,7936]{1,0:T(8,128)}) %reduce-scatter.2.cloned.1.call-update) | async-done | bytes 2539536 | tf_op jit(solution)/shard_map/reduce_scatter | solution.py:142
  650.5 4.7 fusion.2
  655.3 0.3 pad_maximum_fusion.2
  655.5 1.4 copy-done.10
  656.9 1.8 fusion.15
  658.9 1.1 copy.46
  660.0 50.8 %all-reduce.13.cloned.1.call-done = f32[80,7936]{1,0:T(8,128)} async-done(((f32[80,7936]{1,0:T(8,128)}), f32[80,7936]{1,0:T(8,128)}) %all-reduce.13.cloned.1.call-update) | async-done | bytes 2539536 | tf_op jit(solution)/shard_map/psum | solution.py:155
  710.8 2.9 slice.165
  713.6 1.9 slice.166
  715.6 1.5 slice.167
  (75 shorter events, 4.2 us)
Async XLA Ops:
  7.2 63.8 %copy-start = (bf16[1,2,16,16,640]{4,3,2,1,0:T(8,128)(2,1)S(1)}, bf16[1,2,16,16,640]{4,3,2,1,0:T(8,128)(2,1)}, u32[]{:S(2)}) copy-start(bf16[1,2,16,16,640]{4,3,2,1,0:T(8,128)(2,1)} %param.9) | copy-start | bytes 1966084
  7.2 3.5 copy-start.1
  7.2 5.0 copy-start.14
  7.2 59.5 %all-gather.5.cloned.1.call-start = ((), (), s32[]{:S(2)}) async-start(), calls=%async_computation.2 | async-start | bytes 2764800 | tf_op jit(solution)/shard_map/all_gather | solution.py:102
  7.9 172.4 %all-gather.3.cloned.1.call-start = ((), (), s32[]{:S(2)}) async-start(), calls=%async_computation.1 | async-start | bytes 8294400 | tf_op jit(solution)/shard_map/all_gather | solution.py:101
  8.7 641.8 %reduce-scatter.2.cloned.1.call-start = ((), (), s32[]{:S(2)}) async-start(), calls=%async_computation.3 | async-start | bytes 22855680 | tf_op jit(solution)/shard_map/reduce_scatter | solution.py:142
  74.5 4.0 collective-permute-start.1
  79.0 111.6 %copy-start.11 = (bf16[4,256,640]{2,1,0:T(8,128)(2,1)}, bf16[4,256,640]{2,1,0:T(8,128)(2,1)S(1)}, u32[]{:S(2)}) copy-start(bf16[4,256,640]{2,1,0:T(8,128)(2,1)S(1)} %get-tuple-element.38) | copy-start | bytes 3932164
  220.0 4.3 copy-start.2
  220.0 4.8 copy-start.3
  220.0 5.6 copy-start.4
  234.7 9.9 %slice-start = ((s8[7372800]{0:T(1024)(128)(4,1)}), s8[4194304]{0:T(1024)(128)(4,1)S(1)}, s32[]{:S(2)}) async-start(s8[7372800]{0:T(1024)(128)(4,1)} %bitcast.138), calls=%async_computation.5 | async-start | bytes 8388608
  235.6 4.4 copy-start.13
  239.9 4.7 slice-start.1
  244.6 15.6 %copy-start.12 = (bf16[4,256,640]{2,1,0:T(8,128)(2,1)S(1)}, bf16[4,256,640]{2,1,0:T(8,128)(2,1)}, u32[]{:S(2)}) copy-start(bf16[4,256,640]{2,1,0:T(8,128)(2,1)} %copy-done.11) | copy-start | bytes 3932164
  258.1 32.3 %collective-permute-start = (bf16[256,640]{1,0:T(8,128)(2,1)}, bf16[256,640]{1,0:T(8,128)(2,1)}, u32[]{:S(2)}, u32[]{:S(2)}) collective-permute-start(bf16[256,640]{1,0:T(8,128)(2,1)} %slice.149), channel_id=1, source_target_pairs={{0,1},{1,2},{2,3},{4,5},{5,6},{6,7},{8,9},{9,10},{10,11},{12,13},{... | collective-permute-start | bytes 983048 | tf_op jit(solution)/shard_map/ppermute | solution.py:18
  290.4 5.4 copy-start.5
  290.5 5.4 copy-start.7
  295.8 6.0 copy-start.9
  317.0 393.8 %all-reduce.13.cloned.1.call-start = ((), (), s32[]{:S(2)}) async-start(), calls=%async_computation.4 | async-start | bytes 5079040 | tf_op jit(solution)/shard_map/psum | solution.py:155
  650.5 4.7 copy-start.6
  650.5 4.7 copy-start.8
  655.3 1.7 copy-start.10
Sparse Core Ops, SparseCore 0:
  10.2 56.4 all-gather.4
  68.9 111.3 all-gather.2
  317.1 333.2 reduce-scatter.1
  652.9 57.8 all-reduce.12
where the time goes:
time: 725 us; the launch traced here: 724 us
  waiting for transfers between devices  508 us (70%)
  local copies, waits for them, and re-layouts  75.6 us (10%)
  matrix products  52.9 us (7%)
  other arithmetic  35.7 us (5%)
  blocking collectives  33.4 us (5%)
  between operations  14.9 us (2%)
    reduce_scatter x1, waiting for transfers between devices, body(): lax.psum_scatter(jnp.concatenate([spatial_part.reshape(row_share * lax.ax...  333 us
    all_gather x1, waiting for transfers between devices, body(): lax.all_gather(spatial_weight, 'dp', axis=0, tiled=True)  100 us
    psum x1, waiting for transfers between devices, body(): totals = lax.psum(grad_shard, 'tm')  50.8 us
    all_gather x1, blocking collectives, body(): lax.all_gather(time_weight, 'dp', axis=0, tiled=True)  33.4 us
    all_gather x1, waiting for transfers between devices, body(): lax.all_gather(temporal_weight, 'dp', axis=0, tiled=True)  20.7 us
    dot_general x1, matrix products, body(): jnp.einsum('rq,ckq->rkc', hidden_back, spatial_taps, preferred_element_ty...  15.7 us
    concatenate x1, other arithmetic, body(): jnp.concatenate([spatial_part.reshape(row_share * lax.axis_size('dp'), 9...  15.2 us
    reshape x1, local copies, waits for them, and re-layouts, body(): spatial_part.reshape(row_share * lax.axis_size('dp'), 9 * channels)  15.1 us
  transfers between devices with their start and end apart: 6, of which 5 were waited for; matrix products, arithmetic and copies ran while one was open for 7% of the time, Pallas kernels for 0%

commit v1 on v0

v1 whole, which is shorter than its diff:
```python
import math

import jax
import jax.numpy as jnp
from jax import lax
from jax.experimental import pallas as pl
from jax.experimental.pallas import tpu as pltpu
from jax.sharding import PartitionSpec as P

GROUPS = 32


epsilon = 1e-05
log_base = math.log(10000.0)
bf16 = jnp.bfloat16
f32 = jnp.float32
VMEM_BYTES = 56 * 1024 * 1024


def embedding(diffusion_step, embed_width):
    half_width = embed_width // 2
    frequency = jnp.exp(-log_base * jnp.arange(half_width, dtype=jnp.float32) / half_width)
    angles = diffusion_step.astype(jnp.float32) * frequency
    return jnp.concatenate([jnp.cos(angles), jnp.sin(angles)])


def normalize(frames):
    frame_count, height, breadth, channels = frames.shape
    grouped = frames.astype(jnp.float32).reshape(
        frame_count, height * breadth, GROUPS, channels // GROUPS
    )
    center = jnp.mean(grouped, axis=(1, 3), keepdims=True)
    deviation = grouped - center
    variance = jnp.mean(deviation * deviation, axis=(1, 3), keepdims=True)
    scaled = lax.rsqrt(variance + epsilon)
    return (deviation * scaled, scaled)


def column_views(frames):
    breadth = frames.shape[2]
    padded = jnp.pad(frames, ((0, 0), (1, 1), (1, 1), (0, 0)))
    return jnp.stack([padded[:, :, s : s + breadth, :] for s in range(3)])


def flip(x, axis, mask):
    count = lax.axis_size(axis)
    return lax.ppermute(x, axis, [(i, i ^ mask) for i in range(count)])


def bits_of(count):
    return [1 << i for i in range(count.bit_length() - 1)]


def after(x, *others):
    return lax.optimization_barrier((x,) + others)[0]


def ordered(mine, other, upper, axis):
    low = jnp.where(upper, other, mine)
    high = jnp.where(upper, mine, other)
    return jnp.concatenate([low, high], axis=axis)


def gather_dp(piece, spots):
    count = lax.axis_size("dp")
    masks = bits_of(count)[::-1]
    index = lax.axis_index("dp")
    x = piece.reshape((1,) * len(masks) + piece.shape)
    arrivals = []
    for spot in spots:
        mask = masks[spot]
        got = flip(x, "dp", mask)
        arrivals.append(got)
        x = ordered(x, got, (index & mask) != 0, spot)
    return x, arrivals


def half_of(length):
    return -(-((length + 1) // 2) // 8) * 8


def split_rows(x, upper, rows_axis):
    length = x.shape[rows_axis]
    half = half_of(length)
    low = lax.slice_in_dim(x, 0, half, axis=rows_axis)
    high = lax.slice_in_dim(x, length - half, length, axis=rows_axis)
    return jnp.where(upper, high, low), jnp.where(upper, low, high)


def reduce_stage(x, kind):
    axis, mask, spot = kind
    upper = (lax.axis_index(axis) & mask) != 0
    if axis == "dp":
        low = lax.slice_in_dim(x, 0, 1, axis=spot)
        high = lax.slice_in_dim(x, 1, 2, axis=spot)
        keep, send = jnp.where(upper, high, low), jnp.where(upper, low, high)
    else:
        keep, send = split_rows(x, upper, x.ndim - 2)
    got = flip(send.astype(bf16), axis, mask)
    return keep + got.astype(f32)


def join_rows(x, length, kind):
    axis, mask, _ = kind
    upper = (lax.axis_index(axis) & mask) != 0
    got = flip(x, axis, mask)
    half = x.shape[0]
    low = jnp.where(upper, got, x)
    high = jnp.where(upper, x, got)
    return jnp.concatenate([low, high[2 * half - length :]], axis=0)


def reduce_all(x, order):
    count = lax.axis_size("dp")
    nbits = len(bits_of(count))
    rows = x.shape[1]
    x = x.reshape((2,) * nbits + x.shape[1:])
    lengths = []
    for kind in order:
        if kind[0] == "tm":
            lengths.append((x.shape[-2], kind))
        x = reduce_stage(x, kind)
    x = x.reshape(x.shape[-2:])
    for length, kind in lengths[::-1]:
        x = join_rows(x, length, kind)
    return x


def matmul_nt(a, b):
    return lax.dot_general(a, b, (((1,), (1,)), ((), ())), preferred_element_type=f32)


def matmul_tn(a, b):
    return lax.dot_general(a, b, (((0,), (0,)), ((), ())), preferred_element_type=f32)


def conv_kernel(back, views_ref, lo_a, hi_a, lo_b, hi_b, mid, shift_ref, out_ref, acc_ref):
    step = pl.program_id(0)
    rows, channels = acc_ref.shape
    height = views_ref.shape[3]

    def part(tap, w):
        r, s = tap // 3, tap % 3
        if back:
            r, s = 2 - r, 2 - s
        x = views_ref[s, :, pl.ds(r, height)].reshape(rows, channels)
        if back:
            return matmul_nt(x, w)
        return jnp.dot(x, w, preferred_element_type=f32)

    @pl.when(step == 0)
    def _():
        acc_ref[...] = part(4, mid[...]) + shift_ref[...]

    acc_ref[...] += part(step, lo_a[...])
    acc_ref[...] += part(5 + step, hi_a[...])
    acc_ref[...] += part(2 + step, lo_b[...])
    acc_ref[...] += part(7 + step, hi_b[...])

    @pl.when(step == 1)
    def _():
        out_ref[...] = acc_ref[...].astype(out_ref.dtype)


def conv(views, taps, shift, back, out_dtype):
    _, frames, _, breadth, channels = views.shape
    rows = frames * (views.shape[2] - 2) * breadth
    w_spec = pl.BlockSpec((channels, channels), lambda i: (0, i))
    return pl.pallas_call(
        lambda *refs: conv_kernel(back, *refs),
        grid=(2,),
        in_specs=[
            pl.BlockSpec(views.shape, lambda i: (0, 0, 0, 0, 0), pipeline_mode=pl.Buffered(1)),
            w_spec,
            w_spec,
            w_spec,
            w_spec,
            pl.BlockSpec((channels, channels), lambda i: (0, 0), pipeline_mode=pl.Buffered(1)),
            pl.BlockSpec((1, channels), lambda i: (0, 0)),
        ],
        out_specs=pl.BlockSpec((rows, channels), lambda i: (0, 0), pipeline_mode=pl.Buffered(1)),
        out_shape=jax.ShapeDtypeStruct((rows, channels), out_dtype),
        scratch_shapes=[pltpu.VMEM((rows, channels), f32)],
        compiler_params=pltpu.CompilerParams(vmem_limit_bytes=VMEM_BYTES),
        name="conv_back" if back else "conv_fwd",
    )(views, *taps, shift)


def hidden_grad_kernel(cot_ref, next_ref, w_ref, back_ref, sum_ref):
    outs = cot_ref.shape[0]
    channels = w_ref.shape[0]
    total = jnp.zeros((1, channels), f32)
    for o in range(outs):
        even = matmul_nt(cot_ref[o], w_ref[:, channels : 2 * channels])
        later = cot_ref[o + 1] if o + 1 < outs else next_ref[...]
        odd = matmul_nt(cot_ref[o], w_ref[:, 2 * channels :]) + matmul_nt(
            later, w_ref[:, :channels]
        )
        back_ref[2 * o] = even.astype(bf16)
        back_ref[2 * o + 1] = odd.astype(bf16)
        total += jnp.sum(even + odd, axis=0, keepdims=True)
    sum_ref[...] = total


def hidden_gradient(cot, following, temporal):
    outs, pixels, channels = cot.shape
    return pl.pallas_call(
        hidden_grad_kernel,
        out_shape=(
            jax.ShapeDtypeStruct((2 * outs, pixels, channels), bf16),
            jax.ShapeDtypeStruct((1, channels), f32),
        ),
        compiler_params=pltpu.CompilerParams(vmem_limit_bytes=VMEM_BYTES),
        name="hidden_grad",
    )(cot, following, temporal)


def weight_grad_kernel(first, views_ref, back_ref, out_ref):
    tap = first + pl.program_id(0)
    rows, channels = back_ref.shape
    height = views_ref.shape[3]
    shards, share, _ = out_ref.shape
    x = views_ref[tap % 3, :, pl.ds(tap // 3, height)].reshape(rows, channels)
    out_ref[...] = matmul_tn(x, back_ref[...]).reshape(shards, share, channels)


def weight_grad(views, hidden_back, first, taps, shards):
    rows, channels = hidden_back.shape
    share = channels // shards
    return pl.pallas_call(
        lambda *refs: weight_grad_kernel(first, *refs),
        grid=(taps,),
        in_specs=[
            pl.BlockSpec(views.shape, lambda i: (0, 0, 0, 0, 0), pipeline_mode=pl.Buffered(1)),
            pl.BlockSpec((rows, channels), lambda i: (0, 0), pipeline_mode=pl.Buffered(1)),
        ],
        out_specs=pl.BlockSpec((shards, share, channels), lambda i: (0, i, 0)),
        out_shape=jax.ShapeDtypeStruct((shards, taps * share, channels), f32),
        compiler_params=pltpu.CompilerParams(vmem_limit_bytes=VMEM_BYTES),
        name="weight_grad",
    )(views, hidden_back)


def body(latents, cotangent, timesteps, spatial_weight, temporal_weight, time_weight):
    clip_frames = latents[0]
    frame_count, height, breadth, channels = clip_frames.shape
    pixels = height * breadth
    out_count = frame_count // 2
    dp = lax.axis_size("dp")
    tm = lax.axis_size("tm")
    share = channels // dp
    dp_masks = bits_of(dp)[::-1]
    nbits = len(dp_masks)
    dp_index = lax.axis_index("dp")
    tm_index = lax.axis_index("tm")
    core = tm_index & 1
    side = (tm_index >> 1) & 1
    on_side = side != 0
    on_core = core != 0

    cot = cotangent[0].reshape(out_count, pixels, channels)
    following = lax.ppermute(cot[0], "tm", [(i + 1, i) for i in range(tm - 1)])

    half = share // 2
    wide = jnp.concatenate([temporal_weight, time_weight], axis=1)
    spots = list(range(nbits))
    piece = lax.dynamic_slice_in_dim(wide, core * half, half, axis=0)
    got, arrivals = gather_dp(piece, spots)
    got = ordered(got, flip(got, "tm", 1), on_core, got.ndim - 2)
    wide_full = got.reshape(channels, wide.shape[1])
    temporal_full = wide_full[:, : 3 * channels]
    time_full = wide_full[:, 3 * channels :]

    my_rows = lax.dynamic_slice_in_dim(spatial_weight, core * half, half, axis=0)
    gate = arrivals[-2]

    def spatial_taps(first, across):
        nonlocal gate
        start = first * channels + (side * 5 * channels if across else 0)
        cols = (2 if across else 1) * channels
        chunk = lax.dynamic_slice_in_dim(my_rows, start, cols, axis=1)
        got, arrivals = gather_dp(after(chunk, gate), spots)
        gate = arrivals[-2]
        if not across:
            whole = ordered(got, flip(got, "tm", 1), on_core, got.ndim - 2)
            return (whole.reshape(channels, cols),)
        other = flip(got, "tm", 2)
        both = jnp.stack([jnp.where(on_side, other, got), jnp.where(on_side, got, other)])
        whole = ordered(both, flip(both, "tm", 1), on_core, both.ndim - 2)
        whole = whole.reshape(2, channels, cols)
        return whole[0], whole[1]

    lo_a, hi_a = spatial_taps(0, True)
    lo_b, hi_b = spatial_taps(2, True)
    (mid,) = spatial_taps(4, False)
    taps = (lo_a, hi_a, lo_b, hi_b, mid)

    normal, scaled = normalize(clip_frames)
    activation = jax.nn.silu(normal).reshape(frame_count, height, breadth, channels).astype(bf16)
    views = column_views(activation)

    hidden_back, shift_sum = hidden_gradient(cot, following, temporal_full)
    flat_back = hidden_back.reshape(frame_count * pixels, channels)

    bit = {"y": ("dp", dp_masks[-1], nbits - 1)}
    z_kinds = [("dp", m, i) for i, m in list(enumerate(dp_masks))[:-1]][::-1]
    y_kinds = [bit["y"]]
    core_kind = [("tm", 1, None)]
    x_kinds = [("tm", m, None) for m in bits_of(tm)[1:]]
    orders = [
        core_kind + y_kinds + z_kinds + x_kinds,
        core_kind + z_kinds + x_kinds + y_kinds,
        core_kind + x_kinds + y_kinds + z_kinds,
    ]
    spatial_rows = []
    for i in range(3):
        grad = weight_grad(views, flat_back, 3 * i, 3, dp)
        total = reduce_all(grad, orders[i])
        spatial_rows.append(total.reshape(3, share, channels))

    embedded = embedding(timesteps[0], time_full.shape[1])
    time_shift = jnp.dot(time_full.astype(f32), embedded, precision=lax.Precision.HIGHEST)
    hidden = conv(views, taps, time_shift[None], False, bf16).reshape(
        frame_count, pixels, channels
    )
    before = lax.ppermute(hidden[-1], "tm", [(i, i + 1) for i in range(tm - 1)])
    evens = hidden[0::2].reshape(out_count * pixels, channels)
    odds = hidden[1::2].reshape(out_count * pixels, channels)
    leads = jnp.concatenate([before[None], hidden[1:-1:2]], axis=0).reshape(
        out_count * pixels, channels
    )
    flat_cot = cot.reshape(out_count * pixels, channels)
    columns = (leads, evens, odds)
    temporal_rows = []
    for k in range(3):
        grad = lax.dot_general(
            columns[k], flat_cot, (((0,), (0,)), ((), ())), preferred_element_type=f32
        )
        temporal_rows.append(reduce_all(grad.reshape(dp, share, channels), orders[k]))
    result = sum(
        jnp.dot(
            columns[k],
            temporal_full[:, k * channels : (k + 1) * channels],
            preferred_element_type=f32,
        )
        for k in range(3)
    )
    downsampled = result.reshape(1, out_count, height, breadth, channels)

    back_views = column_views(flat_back.reshape(frame_count, height, breadth, channels))
    zero_shift = jnp.zeros((1, channels), f32)
    activation_grad = conv(back_views, taps, zero_shift, True, f32)
    sigmoid_value = jax.nn.sigmoid(normal)
    derivative = sigmoid_value * (1.0 + normal * (1.0 - sigmoid_value))
    norm_grad = activation_grad.reshape(normal.shape) * derivative
    mean_one = jnp.mean(norm_grad, axis=(1, 3), keepdims=True)
    mean_two = jnp.mean(norm_grad * normal, axis=(1, 3), keepdims=True)
    input_grad = ((norm_grad - mean_one - normal * mean_two) * scaled).reshape(
        1, frame_count, height, breadth, channels
    )

    sums = shift_sum
    for mask in bits_of(tm):
        sums = sums + flip(sums, "tm", mask)
    pairs = jnp.concatenate([sums, embedded[None]], axis=1)
    for mask in bits_of(dp):
        pairs = jnp.concatenate([pairs, flip(pairs, "dp", mask)], axis=0)
    mine = lax.dynamic_slice_in_dim(pairs[:, :channels], dp_index * share, share, axis=1)
    time_grad = lax.dot_general(
        mine,
        pairs[:, channels:],
        (((0,), (0,)), ((), ())),
        precision=lax.Precision.HIGHEST,
        preferred_element_type=f32,
    )

    spatial_grad = jnp.concatenate(
        [part[i] for part in spatial_rows for i in range(3)], axis=1
    )
    temporal_grad = jnp.concatenate(temporal_rows, axis=1)
    return (downsampled, input_grad, spatial_grad, temporal_grad, time_grad)


def solution(mesh):
    placed = (
        P("dp", "tm", None, None, None),
        P("dp", "tm", None, None, None),
        P("dp"),
        P("dp", None),
        P("dp", None),
        P("dp", None),
    )
    return jax.shard_map(
        body,
        mesh=mesh,
        in_specs=placed,
        out_specs=(
            P("dp", "tm", None, None, None),
            P("dp", "tm", None, None, None),
            P("dp", None),
            P("dp", None),
            P("dp", None),
        ),
        check_vma=False,
    )
```

time: 725 us -> 382 us (0.53)
  waiting for transfers between devices: 508 us -> 126 us
  Pallas kernels: 0 us -> 60.7 us
  starting transfers between devices: 3.69 us -> 60.7 us
  matrix products: 52.9 us -> 14.5 us
  blocking collectives: 33.4 us -> 0 us
  other arithmetic: 35.7 us -> 53.7 us
  local copies, waits for them, and re-layouts: 75.6 us -> 60.1 us
  between operations: 14.9 us -> 2.9 us
    reduce_scatter x1 -> x0, waiting for transfers between devices: 333 us -> none  [body(): lax.psum_scatter(jnp.concatenate([spatial_part.reshape(row_share * lax.ax...]
    ppermute x2 -> x67, waiting for transfers between devices: 1.95 us -> 126 us  [the longest x65 126 us: flip(): return lax.ppermute(x, axis, [(i, i ^ mask) for i in range(count)])]
    all_gather x2 -> x0, waiting for transfers between devices: 121 us -> none  [the longest x1 100 us: body(): lax.all_gather(spatial_weight, 'dp', axis=0, tiled=True)]
    pallas_call x0 -> x6, Pallas kernels: none -> 60.7 us  [the longest x2 32.6 us: conv(): pl.pallas_call(lambda *refs: conv_kernel(back, *refs), grid=(2,), in_spec...]
    ppermute x2 -> x67, starting transfers between devices: 3.53 us -> 60.7 us  [the longest x65 57 us: flip(): return lax.ppermute(x, axis, [(i, i ^ mask) for i in range(count)])]
    psum x1 -> x0, waiting for transfers between devices: 50.8 us -> none  [body(): totals = lax.psum(grad_shard, 'tm')]
    dot_general x7 -> x8, matrix products: 52.9 us -> 14.5 us  [the longest x3 6.82 us: body(): jnp.dot(columns[k], temporal_full[:, k * channels:(k + 1) * channels], pr...]
    all_gather x1 -> x0, blocking collectives: 33.4 us -> none  [body(): lax.all_gather(time_weight, 'dp', axis=0, tiled=True)]
  transfers between devices with their start and end apart: 6 -> 67, of which waited for: 5 -> 25; matrix products, arithmetic and copies ran while one was open for 7% -> 32% of each run, Pallas kernels for 0% -> 16%
where the time goes in v1:
time: 382 us; the launch traced here: 378 us
  waiting for transfers between devices  126 us (33%)
  starting transfers between devices  60.7 us (16%)
  Pallas kernels  60.7 us (16%)
  local copies, waits for them, and re-layouts  60.1 us (16%)
  other arithmetic  53.7 us (14%)
  matrix products  14.5 us (4%)
    ppermute x65, waiting for transfers between devices, flip(): return lax.ppermute(x, axis, [(i, i ^ mask) for i in range(count)])  126 us
    ppermute x65, starting transfers between devices, flip(): return lax.ppermute(x, axis, [(i, i ^ mask) for i in range(count)])  57 us
    pallas_call x2, Pallas kernels, conv(): pl.pallas_call(lambda *refs: conv_kernel(back, *refs), grid=(2,), in_spec...  32.6 us
    convert_element_type x2, local copies, waits for them, and re-layouts, normalize(): frames.astype(jnp.float32)  32.5 us
    pallas_call x3, Pallas kernels, weight_grad(): pl.pallas_call(lambda *refs: weight_grad_kernel(first, *refs), grid=(taps...  23 us
    convert_element_type x30, other arithmetic, reduce_stage(): got = flip(send.astype(bf16), axis, mask)  9.02 us
  transfers between devices with their start and end apart: 67, of which 25 were waited for; matrix products, arithmetic and copies ran while one was open for 32% of the time, Pallas kernels for 16%

profile of v1, /device:TPU:0, one launch (start us, length us, event | category | flops | bytes accessed | tf_op | source)
XLA Modules:
  0.0 378.2 jit_solution(8251426361260065649)
XLA Ops:
  1.7 4.1 %collective-permute-start = (bf16[1,1,1,40,2176]{4,3,2,1,0:T(8,128)(2,1)S(1)}, bf16[1,1,1,40,2176]{4,3,2,1,0:T(8,128)(2,1)S(1)}, u32[]{:S(2)}, u32[]{:S(2)}) collective-permute-start(bf16[1,1,1,40,2176]{4,3,2,1,0:T(8,128)(2,1)S(1)} %fusion.19), channel_id=1, source_target_pairs={{0,16},{4,20},{8,24},{12,28},{16,0},{20,4},{24,8},{28,12},{1,17},{... | collective-permute-start | bytes 522248 | tf_op jit(solution)/shard_map/ppermute | solution.py:47
  15.8 2.6 fusion.3
  18.6 21.1 %reshape.182 = f32[4,256,32,20]{3,2,1,0:T(8,128)} reshape(bf16[1,4,16,16,640]{4,3,2,1,0:T(8,128)(2,1)S(1)} %copy-done) | data formatting | bytes 3932160 | tf_op jit(solution)/shard_map/convert_element_type | solution.py:29
  40.3 11.4 %copy.32 = f32[4,256,32,20]{1,0,3,2:T(4,128)} copy(f32[4,256,32,20]{3,2,1,0:T(8,128)} %reshape.182) | data formatting | bytes 5242880 | tf_op jit(solution)/shard_map/convert_element_type | solution.py:29
  53.7 3.1 collective-permute-start.2
  56.8 5.6 %collective-permute-done.2 = bf16[1,1,1,40,1280]{4,3,2,1,0:T(8,128)(2,1)S(1)} collective-permute-done((bf16[1,1,1,40,1280]{4,3,2,1,0:T(8,128)(2,1)S(1)}, bf16[1,1,1,40,1280]{4,3,2,1,0:T(8,128)(2,1)S(1)}, u32[]{:S(2)}, u32[]{:S(2)}) %collective-permute-start.2) | collective-permute-done | bytes 102432 | tf_op jit(solution)/shard_map/ppermute | solution.py:47
  62.6 3.7 pad_maximum_fusion.refs_0_
  66.3 3.1 collective-permute-done.3
  69.5 6.7 %collective-permute-done.7 = bf16[1,1,1,40,1280]{4,3,2,1,0:T(8,128)(2,1)S(1)} collective-permute-done((bf16[1,1,1,40,1280]{4,3,2,1,0:T(8,128)(2,1)S(1)}, bf16[1,1,1,40,1280]{4,3,2,1,0:T(8,128)(2,1)S(1)}, u32[]{:S(2)}, u32[]{:S(2)}) %collective-permute-start.7) | collective-permute-done | bytes 102432 | tf_op jit(solution)/shard_map/ppermute | solution.py:47
  78.0 4.6 %collective-permute-done.8 = bf16[2,1,1,40,1280]{4,3,2,1,0:T(8,128)(2,1)S(1)} collective-permute-done((bf16[2,1,1,40,1280]{4,3,2,1,0:T(8,128)(2,1)S(1)}, bf16[2,1,1,40,1280]{4,3,2,1,0:T(8,128)(2,1)S(1)}, u32[]{:S(2)}, u32[]{:S(2)}) %collective-permute-start.8) | collective-permute-done | bytes 204832 | tf_op jit(solution)/shard_map/ppermute | solution.py:47
  85.0 3.0 collective-permute-done.12
  88.1 7.0 %collective-permute-done.16 = bf16[2,2,1,40,2176]{4,3,2,1,0:T(8,128)(2,1)S(1)} collective-permute-done((bf16[2,2,1,40,2176]{4,3,2,1,0:T(8,128)(2,1)S(1)}, bf16[2,2,1,40,2176]{4,3,2,1,0:T(8,128)(2,1)S(1)}, u32[]{:S(2)}, u32[]{:S(2)}) %collective-permute-start.16) | collective-permute-done | bytes 696352 | tf_op jit(solution)/shard_map/ppermute | solution.py:47
  97.1 18.2 %collective-permute-done.14 = bf16[2,2,1,40,640]{4,3,2,1,0:T(8,128)(2,1)S(1)} collective-permute-done((bf16[2,2,1,40,640]{4,3,2,1,0:T(8,128)(2,1)S(1)}, bf16[2,2,1,40,640]{4,3,2,1,0:T(8,128)(2,1)S(1)}, u32[]{:S(2)}, u32[]{:S(2)}) %collective-permute-start.14) | collective-permute-done | bytes 204832 | tf_op jit(solution)/shard_map/ppermute | solution.py:47
  115.6 3.2 collective-permute-start.5
  120.2 17.8 %collective-permute-done.5 = bf16[2,2,2,40,1280]{4,3,2,1,0:T(8,128)(2,1)S(1)} collective-permute-done((bf16[2,2,2,40,1280]{4,3,2,1,0:T(8,128)(2,1)S(1)}, bf16[2,2,2,40,1280]{4,3,2,1,0:T(8,128)(2,1)S(1)}, u32[]{:S(2)}, u32[]{:S(2)}) %collective-permute-start.5) | collective-permute-done | bytes 819232 | tf_op jit(solution)/shard_map/ppermute | solution.py:47
  139.4 15.9 %collective-permute-done.10 = bf16[2,2,2,40,1280]{4,3,2,1,0:T(8,128)(2,1)S(1)} collective-permute-done((bf16[2,2,2,40,1280]{4,3,2,1,0:T(8,128)(2,1)S(1)}, bf16[2,2,2,40,1280]{4,3,2,1,0:T(8,128)(2,1)S(1)}, u32[]{:S(2)}, u32[]{:S(2)}) %collective-permute-start.10) | collective-permute-done | bytes 819232 | tf_op jit(solution)/shard_map/ppermute | solution.py:47
  160.6 5.1 %hidden_grad.1 = (bf16[4,256,640]{2,1,0:T(8,128)(2,1)}, f32[1,640]{1,0:T(1,128)}) custom-call(bf16[2,256,640]{2,1,0:T(8,128)(2,1)} %bitcast.128, bf16[256,640]{1,0:T(8,128)(2,1)} %collective-permute-done.19.next_ref, bf16[640,1920]{1,0:T(8,128)(2,1)} %slice.427.w_ref), custom_call_target="tpu_custom_call" | custom-call | tf_op jit(solution)/shard_map/hidden_grad/pallas_call | solution.py:207
  165.7 7.6 %weight_grad.5 = f32[8,240,640]{2,1,0:T(8,128)} custom-call(bf16[3,4,18,16,640]{4,3,2,1,0:T(8,128)(2,1)} %pad_maximum_fusion.refs_0_, bf16[1024,640]{1,0:T(8,128)(2,1)} %bitcast.116), custom_call_target="tpu_custom_call" | custom-call | tf_op jit(solution)/shard_map/weight_grad/pallas_call | solution.py:230
  173.3 7.6 %weight_grad.4 = f32[8,240,640]{2,1,0:T(8,128)} custom-call(bf16[3,4,18,16,640]{4,3,2,1,0:T(8,128)(2,1)} %pad_maximum_fusion.refs_0_, bf16[1024,640]{1,0:T(8,128)(2,1)} %bitcast.117), custom_call_target="tpu_custom_call" | custom-call | tf_op jit(solution)/shard_map/weight_grad/pallas_call | solution.py:230
  180.8 7.9 %weight_grad.3 = f32[8,240,640]{2,1,0:T(8,128)} custom-call(bf16[3,4,18,16,640]{4,3,2,1,0:T(8,128)(2,1)} %pad_maximum_fusion.refs_0_, bf16[1024,640]{1,0:T(8,128)(2,1)} %bitcast.118), custom_call_target="tpu_custom_call" | custom-call | tf_op jit(solution)/shard_map/weight_grad/pallas_call | solution.py:230
  189.3 2.8 select_convert_fusion
  201.6 2.5 pad_maximum_fusion.1.refs_0_
  204.3 2.4 fusion.13.refs_6_
  206.6 2.2 collective-permute-done.66
  220.2 1.9 pad_maximum_fusion.4
  222.1 1.9 broadcast_select_fusion
  224.0 2.0 pad_maximum_fusion.3
  226.0 16.0 %conv_fwd.1 = bf16[1024,640]{1,0:T(8,128)(2,1)} custom-call(bf16[3,4,18,16,640]{4,3,2,1,0:T(8,128)(2,1)} %pad_maximum_fusion.refs_0_, bf16[640,1280]{1,0:T(8,128)(2,1)} %bitcast.122, bf16[640,1280]{1,0:T(8,128)(2,1)} %bitcast.120, bf16[640,1280]{1,0:T(8,128)(2,1)} %bitcast.126, bf16[640,1280]{1,0:T(8,128)(2,1)} %bitcast.124, bf16[640,640]{1,0:T(8,128)(2,1)} %bitcast.133, ...), custom_call_target="tpu_custom_call" | custom-call | tf_op jit(solution)/shard_map/conv_fwd/pallas_call | solution.py:169
  242.0 2.1 fusion.37
  244.0 2.5 collective-permute-start.18
  251.7 1.9 fusion.40
  254.2 16.6 %conv_back.1 = f32[1024,640]{1,0:T(8,128)} custom-call(bf16[3,4,18,16,640]{4,3,2,1,0:T(8,128)(2,1)} %pad_maximum_fusion.1.refs_0_, bf16[640,1280]{1,0:T(8,128)(2,1)} %bitcast.123, bf16[640,1280]{1,0:T(8,128)(2,1)} %bitcast.121, bf16[640,1280]{1,0:T(8,128)(2,1)} %bitcast.127, bf16[640,1280]{1,0:T(8,128)(2,1)} %bitcast.125, bf16[640,640]{1,0:T(8,128)(2,1)} %bitcast.134, ...), custom_call_target="tpu_custom_call" | custom-call | tf_op jit(solution)/shard_map/conv_back/pallas_call | solution.py:169
  270.7 3.2 copy.30
  274.0 4.2 %reshape.170 = f32[4,256,32,20]{1,0,3,2:T(4,128)} reshape(f32[1024,640]{0,1:T(8,128)} %copy.30) | data formatting | bytes 5242880 | tf_op jit(solution)/shard_map/reshape | solution.py:355
  278.1 5.1 %fusion.35 = (f32[4,32]{0,1:T(8,128)S(1)}, f32[4,32]{0,1:T(8,128)S(1)}) fusion(f32[4,32]{0,1:T(8,128)S(1)} %copy.33, f32[4,256,32,20]{1,0,3,2:T(4,128)} %copy.32, f32[4,32]{0,1:T(8,128)S(1)} %copy.31, f32[4,256,32,20]{1,0,3,2:T(4,128)} %reshape.170), kind=kLoop, calls=%fused_computation.225 | loop fusion | flops 8519424 | bytes 5244928 | tf_op jit(solution)/shard_map/reduce_sum | solution.py:356
  283.8 4.7 %subtract_multiply_fusion = f32[1,4,16,16,640]{4,3,2,1,0:T(8,128)} fusion(f32[1,4,16,16,640]{4,3,2,1,0:T(8,128)} %bitcast.110, bf16[1,4,16,16,640]{4,3,2,1,0:T(8,128)(2,1)S(1)} %copy-done, f32[4,640]{1,0:T(4,128)S(1)} %mul.115, f32[4,640]{1,0:T(4,128)S(1)} %sub.57, f32[4,640]{1,0:T(4,128)S(1)} %mul.95, f32[4,640]{1,0:T(4,128)S(1)} %sub.47), kind=kLoop, calls=%fused_computation.9 | loop fusion | flops 9830400 | bytes 6594560 | tf_op jit(solution)/shard_map/mul | solution.py:358
  289.4 2.9 fusion.10
  295.9 2.1 convolution_add_fusion.1
  312.0 16.0 %collective-permute-done.50 = bf16[1,1,2,40,640]{4,3,2,1,0:T(8,128)(2,1)S(1)} collective-permute-done((bf16[1,1,2,40,640]{4,3,2,1,0:T(8,128)(2,1)S(1)}, bf16[1,1,2,40,640]{4,3,2,1,0:T(8,128)(2,1)S(1)}, u32[]{:S(2)}, u32[]{:S(2)}) %collective-permute-start.50) | collective-permute-done | bytes 102432 | tf_op jit(solution)/shard_map/ppermute | solution.py:47
  336.0 2.3 collective-permute-done.52
  339.4 3.4 collective-permute-done.58
  344.1 3.7 collective-permute-done.59
  350.2 1.8 collective-permute-done.60
  352.1 2.2 collective-permute-start.31
  356.6 2.0 collective-permute-start.25
  360.0 1.9 collective-permute-start.44
  361.9 3.7 collective-permute-done.44
  367.8 1.9 collective-permute-done.45
  (342 shorter events, 100.3 us)
Async XLA Ops:
  1.7 12.3 %collective-permute-start = (bf16[1,1,1,40,2176]{4,3,2,1,0:T(8,128)(2,1)S(1)}, bf16[1,1,1,40,2176]{4,3,2,1,0:T(8,128)(2,1)S(1)}, u32[]{:S(2)}, u32[]{:S(2)}) collective-permute-start(bf16[1,1,1,40,2176]{4,3,2,1,0:T(8,128)(2,1)S(1)} %fusion.19), channel_id=1, source_target_pairs={{0,16},{4,20},{8,24},{12,28},{16,0},{20,4},{24,8},{28,12},{1,17},{... | collective-permute-start | bytes 522248 | tf_op jit(solution)/shard_map/ppermute | solution.py:47
  7.5 153.1 %collective-permute-start.19 = (bf16[256,640]{1,0:T(8,128)(2,1)}, bf16[256,640]{1,0:T(8,128)(2,1)}, u32[]{:S(2)}, u32[]{:S(2)}) collective-permute-start(bf16[256,640]{1,0:T(8,128)(2,1)} %bitcast.28), channel_id=1, source_target_pairs={{1,0},{2,1},{3,2},{5,4},{6,5},{7,6},{9,8},{10,9},{11,10},{13,12},{... | collective-permute-start | bytes 983048 | tf_op jit(solution)/shard_map/ppermute | solution.py:262
  14.8 38.9 %collective-permute-start.1 = (bf16[2,1,1,40,2176]{4,3,2,1,0:T(8,128)(2,1)}, bf16[2,1,1,40,2176]{4,3,2,1,0:T(8,128)(2,1)S(1)}, u32[]{:S(2)}, u32[]{:S(2)}) collective-permute-start(bf16[2,1,1,40,2176]{4,3,2,1,0:T(8,128)(2,1)} %pad_maximum_fusion.16), channel_id=1, source_target_pairs={{0,8},{4,12},{8,0},{12,4},{16,24},{20,28},{24,16},{28,20},{1,9},{5... | collective-permute-start | bytes 1044488 | tf_op jit(solution)/shard_map/ppermute | solution.py:47
  53.7 8.8 %collective-permute-start.2 = (bf16[1,1,1,40,1280]{4,3,2,1,0:T(8,128)(2,1)S(1)}, bf16[1,1,1,40,1280]{4,3,2,1,0:T(8,128)(2,1)S(1)}, u32[]{:S(2)}, u32[]{:S(2)}) collective-permute-start(bf16[1,1,1,40,1280]{4,3,2,1,0:T(8,128)(2,1)S(1)} %bitcast.146), channel_id=1, source_target_pairs={{0,16},{4,20},{8,24},{12,28},{16,0},{20,4},{24,8},{28,12},{1,17},{... | collective-permute-start | bytes 307208 | tf_op jit(solution)/shard_map/ppermute | solution.py:47
  62.5 6.9 %collective-permute-start.3 = (bf16[2,1,1,40,1280]{4,3,2,1,0:T(8,128)(2,1)S(1)}, bf16[2,1,1,40,1280]{4,3,2,1,0:T(8,128)(2,1)S(1)}, u32[]{:S(2)}, u32[]{:S(2)}) collective-permute-start(bf16[2,1,1,40,1280]{4,3,2,1,0:T(8,128)(2,1)S(1)} %pad_maximum_fusion.23), channel_id=1, source_target_pairs={{0,8},{4,12},{8,0},{12,4},{16,24},{20,28},{24,16},{28,20},{1,9},{5... | collective-permute-start | bytes 614408 | tf_op jit(solution)/shard_map/ppermute | solution.py:47
  69.4 6.8 %collective-permute-start.7 = (bf16[1,1,1,40,1280]{4,3,2,1,0:T(8,128)(2,1)S(1)}, bf16[1,1,1,40,1280]{4,3,2,1,0:T(8,128)(2,1)S(1)}, u32[]{:S(2)}, u32[]{:S(2)}) collective-permute-start(bf16[1,1,1,40,1280]{4,3,2,1,0:T(8,128)(2,1)S(1)} %bitcast.145), channel_id=1, source_target_pairs={{0,16},{4,20},{8,24},{12,28},{16,0},{20,4},{24,8},{28,12},{1,17},{... | collective-permute-start | bytes 307208 | tf_op jit(solution)/shard_map/ppermute | solution.py:47
  76.3 6.4 %collective-permute-start.8 = (bf16[2,1,1,40,1280]{4,3,2,1,0:T(8,128)(2,1)S(1)}, bf16[2,1,1,40,1280]{4,3,2,1,0:T(8,128)(2,1)S(1)}, u32[]{:S(2)}, u32[]{:S(2)}) collective-permute-start(bf16[2,1,1,40,1280]{4,3,2,1,0:T(8,128)(2,1)S(1)} %pad_maximum_fusion.24), channel_id=1, source_target_pairs={{0,8},{4,12},{8,0},{12,4},{16,24},{20,28},{24,16},{28,20},{1,9},{5... | collective-permute-start | bytes 614408 | tf_op jit(solution)/shard_map/ppermute | solution.py:47
  76.4 18.6 %collective-permute-start.16 = (bf16[2,2,1,40,2176]{4,3,2,1,0:T(8,128)(2,1)S(1)}, bf16[2,2,1,40,2176]{4,3,2,1,0:T(8,128)(2,1)S(1)}, u32[]{:S(2)}, u32[]{:S(2)}) collective-permute-start(bf16[2,2,1,40,2176]{4,3,2,1,0:T(8,128)(2,1)S(1)} %pad_maximum_fusion.11), channel_id=1, source_target_pairs={{0,4},{4,0},{8,12},{12,8},{16,20},{20,16},{24,28},{28,24},{1,5},{5... | collective-permute-start | bytes 2088968 | tf_op jit(solution)/shard_map/ppermute | solution.py:47
  82.8 32.7 %collective-permute-start.4 = (bf16[2,2,1,40,1280]{4,3,2,1,0:T(8,128)(2,1)S(1)}, bf16[2,2,1,40,1280]{4,3,2,1,0:T(8,128)(2,1)S(1)}, u32[]{:S(2)}, u32[]{:S(2)}) collective-permute-start(bf16[2,2,1,40,1280]{4,3,2,1,0:T(8,128)(2,1)S(1)} %pad_maximum_fusion.13), channel_id=1, source_target_pairs={{0,4},{4,0},{8,12},{12,8},{16,20},{20,16},{24,28},{28,24},{1,5},{5... | collective-permute-start | bytes 1228808 | tf_op jit(solution)/shard_map/ppermute | solution.py:47
  84.4 34.4 %collective-permute-start.9 = (bf16[2,2,1,40,1280]{4,3,2,1,0:T(8,128)(2,1)S(1)}, bf16[2,2,1,40,1280]{4,3,2,1,0:T(8,128)(2,1)S(1)}, u32[]{:S(2)}, u32[]{:S(2)}) collective-permute-start(bf16[2,2,1,40,1280]{4,3,2,1,0:T(8,128)(2,1)S(1)} %pad_maximum_fusion.14), channel_id=1, source_target_pairs={{0,4},{4,0},{8,12},{12,8},{16,20},{20,16},{24,28},{28,24},{1,5},{5... | collective-permute-start | bytes 1228808 | tf_op jit(solution)/shard_map/ppermute | solution.py:47
  88.0 7.3 %collective-permute-start.13 = (bf16[2,1,1,40,640]{4,3,2,1,0:T(8,128)(2,1)S(1)}, bf16[2,1,1,40,640]{4,3,2,1,0:T(8,128)(2,1)S(1)}, u32[]{:S(2)}, u32[]{:S(2)}) collective-permute-start(bf16[2,1,1,40,640]{4,3,2,1,0:T(8,128)(2,1)S(1)} %pad_maximum_fusion.26), channel_id=1, source_target_pairs={{0,8},{4,12},{8,0},{12,4},{16,24},{20,28},{24,16},{28,20},{1,9},{5... | collective-permute-start | bytes 307208 | tf_op jit(solution)/shard_map/ppermute | solution.py:47
  95.3 20.0 %collective-permute-start.14 = (bf16[2,2,1,40,640]{4,3,2,1,0:T(8,128)(2,1)S(1)}, bf16[2,2,1,40,640]{4,3,2,1,0:T(8,128)(2,1)S(1)}, u32[]{:S(2)}, u32[]{:S(2)}) collective-permute-start(bf16[2,2,1,40,640]{4,3,2,1,0:T(8,128)(2,1)S(1)} %pad_maximum_fusion.25), channel_id=1, source_target_pairs={{0,4},{4,0},{8,12},{12,8},{16,20},{20,16},{24,28},{28,24},{1,5},{5... | collective-permute-start | bytes 614408 | tf_op jit(solution)/shard_map/ppermute | solution.py:47
  97.0 60.6 %collective-permute-start.17 = (bf16[2,2,2,40,2176]{4,3,2,1,0:T(8,128)(2,1)S(1)}, bf16[2,2,2,40,2176]{4,3,2,1,0:T(8,128)(2,1)S(1)}, u32[]{:S(2)}, u32[]{:S(2)}) collective-permute-start(bf16[2,2,2,40,2176]{4,3,2,1,0:T(8,128)(2,1)S(1)} %pad_maximum_fusion.7), channel_id=1, source_target_pairs={{0,1},{1,0},{2,3},{3,2},{4,5},{5,4},{6,7},{7,6},{8,9},{9,8},{10,11... | collective-permute-start | bytes 4177928 | tf_op jit(solution)/shard_map/ppermute | solution.py:47
  115.6 22.3 %collective-permute-start.5 = (bf16[2,2,2,40,1280]{4,3,2,1,0:T(8,128)(2,1)S(1)}, bf16[2,2,2,40,1280]{4,3,2,1,0:T(8,128)(2,1)S(1)}, u32[]{:S(2)}, u32[]{:S(2)}) collective-permute-start(bf16[2,2,2,40,1280]{4,3,2,1,0:T(8,128)(2,1)S(1)} %pad_maximum_fusion.8), channel_id=1, source_target_pairs={{0,2},{1,3},{2,0},{3,1},{4,6},{5,7},{6,4},{7,5},{8,10},{9,11},{10,... | collective-permute-start | bytes 2457608 | tf_op jit(solution)/shard_map/ppermute | solution.py:47
  119.0 36.3 %collective-permute-start.10 = (bf16[2,2,2,40,1280]{4,3,2,1,0:T(8,128)(2,1)S(1)}, bf16[2,2,2,40,1280]{4,3,2,1,0:T(8,128)(2,1)S(1)}, u32[]{:S(2)}, u32[]{:S(2)}) collective-permute-start(bf16[2,2,2,40,1280]{4,3,2,1,0:T(8,128)(2,1)S(1)} %pad_maximum_fusion.9), channel_id=1, source_target_pairs={{0,2},{1,3},{2,0},{3,1},{4,6},{5,7},{6,4},{7,5},{8,10},{9,11},{10,... | collective-permute-start | bytes 2457608 | tf_op jit(solution)/shard_map/ppermute | solution.py:47
  139.4 79.1 %collective-permute-start.6 = (bf16[2,2,2,2,40,1280]{5,4,3,2,1,0:T(8,128)(2,1)}, bf16[2,2,2,2,40,1280]{5,4,3,2,1,0:T(8,128)(2,1)}, u32[]{:S(2)}, u32[]{:S(2)}) collective-permute-start(bf16[2,2,2,2,40,1280]{5,4,3,2,1,0:T(8,128)(2,1)} %pad_maximum_fusion.5), channel_id=1, source_target_pairs={{0,1},{1,0},{2,3},{3,2},{4,5},{5,4},{6,7},{7,6},{8,9},{9,8},{10,11... | collective-permute-start | bytes 4915208 | tf_op jit(solution)/shard_map/ppermute | solution.py:47
  157.6 64.5 %collective-permute-start.11 = (bf16[2,2,2,2,40,1280]{5,4,3,2,1,0:T(8,128)(2,1)}, bf16[2,2,2,2,40,1280]{5,4,3,2,1,0:T(8,128)(2,1)}, u32[]{:S(2)}, u32[]{:S(2)}) collective-permute-start(bf16[2,2,2,2,40,1280]{5,4,3,2,1,0:T(8,128)(2,1)} %pad_maximum_fusion.6), channel_id=1, source_target_pairs={{0,1},{1,0},{2,3},{3,2},{4,5},{5,4},{6,7},{7,6},{8,9},{9,8},{10,11... | collective-permute-start | bytes 4915208 | tf_op jit(solution)/shard_map/ppermute | solution.py:47
  192.1 17.8 %collective-permute-start.34 = (bf16[2,2,2,120,640]{4,3,2,1,0:T(8,128)(2,1)S(1)}, bf16[2,2,2,120,640]{4,3,2,1,0:T(8,128)(2,1)S(1)}, u32[]{:S(2)}, u32[]{:S(2)}) collective-permute-start(bf16[2,2,2,120,640]{4,3,2,1,0:T(8,128)(2,1)S(1)} %select_convert_fusion), channel_id=1, source_target_pairs={{0,1},{1,0},{2,3},{3,2},{4,5},{5,4},{6,7},{7,6},{8,9},{9,8},{10,11... | collective-permute-start | bytes 3686408 | tf_op jit(solution)/shard_map/ppermute | solution.py:47
  198.8 14.2 %collective-permute-start.20 = (bf16[2,2,2,120,640]{4,3,2,1,0:T(8,128)(2,1)S(1)}, bf16[2,2,2,120,640]{4,3,2,1,0:T(8,128)(2,1)S(1)}, u32[]{:S(2)}, u32[]{:S(2)}) collective-permute-start(bf16[2,2,2,120,640]{4,3,2,1,0:T(8,128)(2,1)S(1)} %select_convert_fusion.2), channel_id=1, source_target_pairs={{0,1},{1,0},{2,3},{3,2},{4,5},{5,4},{6,7},{7,6},{8,9},{9,8},{10,11... | collective-permute-start | bytes 3686408 | tf_op jit(solution)/shard_map/ppermute | solution.py:47
  208.9 7.1 %collective-permute-start.27 = (bf16[2,2,2,120,640]{4,3,2,1,0:T(8,128)(2,1)S(1)}, bf16[2,2,2,120,640]{4,3,2,1,0:T(8,128)(2,1)S(1)}, u32[]{:S(2)}, u32[]{:S(2)}) collective-permute-start(bf16[2,2,2,120,640]{4,3,2,1,0:T(8,128)(2,1)S(1)} %select_convert_fusion.1), channel_id=1, source_target_pairs={{0,1},{1,0},{2,3},{3,2},{4,5},{5,4},{6,7},{7,6},{8,9},{9,8},{10,11... | collective-permute-start | bytes 3686408 | tf_op jit(solution)/shard_map/ppermute | solution.py:47
  211.3 95.4 %collective-permute-start.35 = (bf16[2,2,2,64,640]{4,3,2,1,0:T(8,128)(2,1)}, bf16[2,2,2,64,640]{4,3,2,1,0:T(8,128)(2,1)}, u32[]{:S(2)}, u32[]{:S(2)}) collective-permute-start(bf16[2,2,2,64,640]{4,3,2,1,0:T(8,128)(2,1)} %select_convert_fusion.3), channel_id=1, source_target_pairs={{0,2},{1,3},{2,0},{3,1},{4,6},{5,7},{6,4},{7,5},{8,10},{9,11},{10,... | collective-permute-start | bytes 1966088 | tf_op jit(solution)/shard_map/ppermute | solution.py:47
  214.5 87.2 %collective-permute-start.21 = (bf16[2,2,1,120,640]{4,3,2,1,0:T(8,128)(2,1)}, bf16[2,2,1,120,640]{4,3,2,1,0:T(8,128)(2,1)}, u32[]{:S(2)}, u32[]{:S(2)}) collective-permute-start(bf16[2,2,1,120,640]{4,3,2,1,0:T(8,128)(2,1)} %select_convert_fusion.5), channel_id=1, source_target_pairs={{0,4},{4,0},{8,12},{12,8},{16,20},{20,16},{24,28},{28,24},{1,5},{5... | collective-permute-start | bytes 1843208 | tf_op jit(solution)/shard_map/ppermute | solution.py:47
  217.4 87.0 %collective-permute-start.28 = (bf16[2,1,2,120,640]{4,3,2,1,0:T(8,128)(2,1)}, bf16[2,1,2,120,640]{4,3,2,1,0:T(8,128)(2,1)}, u32[]{:S(2)}, u32[]{:S(2)}) collective-permute-start(bf16[2,1,2,120,640]{4,3,2,1,0:T(8,128)(2,1)} %select_convert_fusion.4), channel_id=1, source_target_pairs={{0,8},{4,12},{8,0},{12,4},{16,24},{20,28},{24,16},{28,20},{1,9},{5... | collective-permute-start | bytes 1843208 | tf_op jit(solution)/shard_map/ppermute | solution.py:47
  244.0 48.3 %collective-permute-start.18 = (bf16[256,640]{1,0:T(8,128)(2,1)}, bf16[256,640]{1,0:T(8,128)(2,1)}, u32[]{:S(2)}, u32[]{:S(2)}) collective-permute-start(bf16[256,640]{1,0:T(8,128)(2,1)} %get-tuple-element.38), channel_id=1, source_target_pairs={{0,1},{1,2},{2,3},{4,5},{5,6},{6,7},{8,9},{9,10},{10,11},{12,13},{... | collective-permute-start | bytes 983048 | tf_op jit(solution)/shard_map/ppermute | solution.py:326
  251.6 48.3 %collective-permute-start.55 = (bf16[2,2,2,40,640]{4,3,2,1,0:T(8,128)(2,1)}, bf16[2,2,2,40,640]{4,3,2,1,0:T(8,128)(2,1)}, u32[]{:S(2)}, u32[]{:S(2)}) collective-permute-start(bf16[2,2,2,40,640]{4,3,2,1,0:T(8,128)(2,1)} %select_convert_fusion.6), channel_id=1, source_target_pairs={{0,1},{1,0},{2,3},{3,2},{4,5},{5,4},{6,7},{7,6},{8,9},{9,8},{10,11... | collective-permute-start | bytes 1228808 | tf_op jit(solution)/shard_map/ppermute | solution.py:47
  292.4 8.9 %collective-permute-start.48 = (bf16[2,2,2,40,640]{4,3,2,1,0:T(8,128)(2,1)}, bf16[2,2,2,40,640]{4,3,2,1,0:T(8,128)(2,1)S(1)}, u32[]{:S(2)}, u32[]{:S(2)}) collective-permute-start(bf16[2,2,2,40,640]{4,3,2,1,0:T(8,128)(2,1)} %select_convert_fusion.7), channel_id=1, source_target_pairs={{0,1},{1,0},{2,3},{3,2},{4,5},{5,4},{6,7},{7,6},{8,9},{9,8},{10,11... | collective-permute-start | bytes 1228808 | tf_op jit(solution)/shard_map/ppermute | solution.py:47
  299.9 28.6 %collective-permute-start.41 = (bf16[2,2,2,40,640]{4,3,2,1,0:T(8,128)(2,1)S(1)}, bf16[2,2,2,40,640]{4,3,2,1,0:T(8,128)(2,1)S(1)}, u32[]{:S(2)}, u32[]{:S(2)}) collective-permute-start(bf16[2,2,2,40,640]{4,3,2,1,0:T(8,128)(2,1)S(1)} %select_convert_fusion.8), channel_id=1, source_target_pairs={{0,1},{1,0},{2,3},{3,2},{4,5},{5,4},{6,7},{7,6},{8,9},{9,8},{10,11... | collective-permute-start | bytes 1228808 | tf_op jit(solution)/shard_map/ppermute | solution.py:47
  301.2 9.0 %collective-permute-start.56 = (bf16[2,2,2,24,640]{4,3,2,1,0:T(8,128)(2,1)S(1)}, bf16[2,2,2,24,640]{4,3,2,1,0:T(8,128)(2,1)S(1)}, u32[]{:S(2)}, u32[]{:S(2)}) collective-permute-start(bf16[2,2,2,24,640]{4,3,2,1,0:T(8,128)(2,1)S(1)} %select_convert_fusion.12), channel_id=1, source_target_pairs={{0,2},{1,3},{2,0},{3,1},{4,6},{5,7},{6,4},{7,5},{8,10},{9,11},{10,... | collective-permute-start | bytes 737288 | tf_op jit(solution)/shard_map/ppermute | solution.py:47
  301.7 8.0 %collective-permute-start.49 = (bf16[2,1,2,40,640]{4,3,2,1,0:T(8,128)(2,1)S(1)}, bf16[2,1,2,40,640]{4,3,2,1,0:T(8,128)(2,1)S(1)}, u32[]{:S(2)}, u32[]{:S(2)}) collective-permute-start(bf16[2,1,2,40,640]{4,3,2,1,0:T(8,128)(2,1)S(1)} %select_convert_fusion.13), channel_id=1, source_target_pairs={{0,8},{4,12},{8,0},{12,4},{16,24},{20,28},{24,16},{28,20},{1,9},{5... | collective-permute-start | bytes 614408 | tf_op jit(solution)/shard_map/ppermute | solution.py:47
  304.4 25.6 %collective-permute-start.22 = (bf16[2,1,1,120,640]{4,3,2,1,0:T(8,128)(2,1)S(1)}, bf16[2,1,1,120,640]{4,3,2,1,0:T(8,128)(2,1)S(1)}, u32[]{:S(2)}, u32[]{:S(2)}) collective-permute-start(bf16[2,1,1,120,640]{4,3,2,1,0:T(8,128)(2,1)S(1)} %select_convert_fusion.11), channel_id=1, source_target_pairs={{0,8},{4,12},{8,0},{12,4},{16,24},{20,28},{24,16},{28,20},{1,9},{5... | collective-permute-start | bytes 921608 | tf_op jit(solution)/shard_map/ppermute | solution.py:47
  306.7 25.0 %collective-permute-start.29 = (bf16[1,1,2,120,640]{4,3,2,1,0:T(8,128)(2,1)S(1)}, bf16[1,1,2,120,640]{4,3,2,1,0:T(8,128)(2,1)S(1)}, u32[]{:S(2)}, u32[]{:S(2)}) collective-permute-start(bf16[1,1,2,120,640]{4,3,2,1,0:T(8,128)(2,1)S(1)} %select_convert_fusion.10), channel_id=1, source_target_pairs={{0,16},{4,20},{8,24},{12,28},{16,0},{20,4},{24,8},{28,12},{1,17},{... | collective-permute-start | bytes 921608 | tf_op jit(solution)/shard_map/ppermute | solution.py:47
  309.6 28.7 %collective-permute-start.36 = (bf16[2,2,1,64,640]{4,3,2,1,0:T(8,128)(2,1)S(1)}, bf16[2,2,1,64,640]{4,3,2,1,0:T(8,128)(2,1)S(1)}, u32[]{:S(2)}, u32[]{:S(2)}) collective-permute-start(bf16[2,2,1,64,640]{4,3,2,1,0:T(8,128)(2,1)S(1)} %select_convert_fusion.9), channel_id=1, source_target_pairs={{0,4},{4,0},{8,12},{12,8},{16,20},{20,16},{24,28},{28,24},{1,5},{5... | collective-permute-start | bytes 983048 | tf_op jit(solution)/shard_map/ppermute | solution.py:47
  310.3 17.7 %collective-permute-start.50 = (bf16[1,1,2,40,640]{4,3,2,1,0:T(8,128)(2,1)S(1)}, bf16[1,1,2,40,640]{4,3,2,1,0:T(8,128)(2,1)S(1)}, u32[]{:S(2)}, u32[]{:S(2)}) collective-permute-start(bf16[1,1,2,40,640]{4,3,2,1,0:T(8,128)(2,1)S(1)} %select_convert_fusion.19), channel_id=1, source_target_pairs={{0,16},{4,20},{8,24},{12,28},{16,0},{20,4},{24,8},{28,12},{1,17},{... | collective-permute-start | bytes 307208 | tf_op jit(solution)/shard_map/ppermute | solution.py:47
  327.9 6.4 %collective-permute-start.57 = (bf16[2,2,1,24,640]{4,3,2,1,0:T(8,128)(2,1)S(1)}, bf16[2,2,1,24,640]{4,3,2,1,0:T(8,128)(2,1)S(1)}, u32[]{:S(2)}, u32[]{:S(2)}) collective-permute-start(bf16[2,2,1,24,640]{4,3,2,1,0:T(8,128)(2,1)S(1)} %select_convert_fusion.18), channel_id=1, source_target_pairs={{0,4},{4,0},{8,12},{12,8},{16,20},{20,16},{24,28},{28,24},{1,5},{5... | collective-permute-start | bytes 368648 | tf_op jit(solution)/shard_map/ppermute | solution.py:47
  330.0 24.4 %collective-permute-start.42 = (bf16[2,2,1,40,640]{4,3,2,1,0:T(8,128)(2,1)S(1)}, bf16[2,2,1,40,640]{4,3,2,1,0:T(8,128)(2,1)S(1)}, u32[]{:S(2)}, u32[]{:S(2)}) collective-permute-start(bf16[2,2,1,40,640]{4,3,2,1,0:T(8,128)(2,1)S(1)} %select_convert_fusion.14), channel_id=1, source_target_pairs={{0,4},{4,0},{8,12},{12,8},{16,20},{20,16},{24,28},{28,24},{1,5},{5... | collective-permute-start | bytes 614408 | tf_op jit(solution)/shard_map/ppermute | solution.py:47
  331.7 17.1 %collective-permute-start.23 = (bf16[1,1,1,120,640]{4,3,2,1,0:T(8,128)(2,1)S(1)}, bf16[1,1,1,120,640]{4,3,2,1,0:T(8,128)(2,1)S(1)}, u32[]{:S(2)}, u32[]{:S(2)}) collective-permute-start(bf16[1,1,1,120,640]{4,3,2,1,0:T(8,128)(2,1)S(1)} %select_convert_fusion.17), channel_id=1, source_target_pairs={{0,16},{4,20},{8,24},{12,28},{16,0},{20,4},{24,8},{28,12},{1,17},{... | collective-permute-start | bytes 460808 | tf_op jit(solution)/shard_map/ppermute | solution.py:47
  332.8 16.1 %collective-permute-start.30 = (bf16[1,1,2,64,640]{4,3,2,1,0:T(8,128)(2,1)S(1)}, bf16[1,1,2,64,640]{4,3,2,1,0:T(8,128)(2,1)S(1)}, u32[]{:S(2)}, u32[]{:S(2)}) collective-permute-start(bf16[1,1,2,64,640]{4,3,2,1,0:T(8,128)(2,1)S(1)} %select_convert_fusion.16), channel_id=1, source_target_pairs={{0,2},{1,3},{2,0},{3,1},{4,6},{5,7},{6,4},{7,5},{8,10},{9,11},{10,... | collective-permute-start | bytes 491528 | tf_op jit(solution)/shard_map/ppermute | solution.py:47
  338.3 9.4 %collective-permute-start.53 = (f32[24,640]{1,0:T(8,128)S(1)}, f32[24,640]{1,0:T(8,128)S(1)}, u32[]{:S(2)}, u32[]{:S(2)}) collective-permute-start(f32[24,640]{1,0:T(8,128)S(1)} %add_bitcast_fusion.4), channel_id=1, source_target_pairs={{0,2},{1,3},{2,0},{3,1},{4,6},{5,7},{6,4},{7,5},{8,10},{9,11},{10,... | collective-permute-start | bytes 184328 | tf_op jit(solution)/shard_map/ppermute | solution.py:47
  347.8 8.7 %collective-permute-start.37 = (bf16[2,1,1,64,640]{4,3,2,1,0:T(8,128)(2,1)S(1)}, bf16[2,1,1,64,640]{4,3,2,1,0:T(8,128)(2,1)S(1)}, u32[]{:S(2)}, u32[]{:S(2)}) collective-permute-start(bf16[2,1,1,64,640]{4,3,2,1,0:T(8,128)(2,1)S(1)} %select_convert_fusion.15), channel_id=1, source_target_pairs={{0,8},{4,12},{8,0},{12,4},{16,24},{20,28},{24,16},{28,20},{1,9},{5... | collective-permute-start | bytes 491528 | tf_op jit(solution)/shard_map/ppermute | solution.py:47
  348.8 5.8 %collective-permute-start.54 = (f32[40,640]{1,0:T(8,128)S(1)}, f32[40,640]{1,0:T(8,128)S(1)}, u32[]{:S(2)}, u32[]{:S(2)}) collective-permute-start(f32[40,640]{1,0:T(8,128)S(1)} %pad_maximum_fusion.28), channel_id=1, source_target_pairs={{0,1},{1,0},{2,3},{3,2},{4,5},{5,4},{6,7},{7,6},{8,9},{9,8},{10,11... | collective-permute-start | bytes 307208 | tf_op jit(solution)/shard_map/ppermute | solution.py:47
  349.0 7.6 %collective-permute-start.24 = (bf16[1,1,1,64,640]{4,3,2,1,0:T(8,128)(2,1)S(1)}, bf16[1,1,1,64,640]{4,3,2,1,0:T(8,128)(2,1)S(1)}, u32[]{:S(2)}, u32[]{:S(2)}) collective-permute-start(bf16[1,1,1,64,640]{4,3,2,1,0:T(8,128)(2,1)S(1)} %select_convert_fusion.23), channel_id=1, source_target_pairs={{0,2},{1,3},{2,0},{3,1},{4,6},{5,7},{6,4},{7,5},{8,10},{9,11},{10,... | collective-permute-start | bytes 245768 | tf_op jit(solution)/shard_map/ppermute | solution.py:47
  352.1 6.6 %collective-permute-start.31 = (bf16[1,1,1,64,640]{4,3,2,1,0:T(8,128)(2,1)S(1)}, bf16[1,1,1,64,640]{4,3,2,1,0:T(8,128)(2,1)S(1)}, u32[]{:S(2)}, u32[]{:S(2)}) collective-permute-start(bf16[1,1,1,64,640]{4,3,2,1,0:T(8,128)(2,1)S(1)} %select_convert_fusion.22), channel_id=1, source_target_pairs={{0,4},{4,0},{8,12},{12,8},{16,20},{20,16},{24,28},{28,24},{1,5},{5... | collective-permute-start | bytes 245768 | tf_op jit(solution)/shard_map/ppermute | solution.py:47
  354.4 7.5 %collective-permute-start.61 = (f32[40,640]{1,0:T(8,128)S(1)}, f32[40,640]{1,0:T(8,128)S(1)}, u32[]{:S(2)}, u32[]{:S(2)}) collective-permute-start(f32[40,640]{1,0:T(8,128)S(1)} %pad_maximum_fusion.29), channel_id=1, source_target_pairs={{0,1},{1,0},{2,3},{3,2},{4,5},{5,4},{6,7},{7,6},{8,9},{9,8},{10,11... | collective-permute-start | bytes 307208 | tf_op jit(solution)/shard_map/ppermute | solution.py:47
  356.5 10.6 %collective-permute-start.38 = (bf16[1,1,1,64,640]{4,3,2,1,0:T(8,128)(2,1)S(1)}, bf16[1,1,1,64,640]{4,3,2,1,0:T(8,128)(2,1)S(1)}, u32[]{:S(2)}, u32[]{:S(2)}) collective-permute-start(bf16[1,1,1,64,640]{4,3,2,1,0:T(8,128)(2,1)S(1)} %select_convert_fusion.21), channel_id=1, source_target_pairs={{0,16},{4,20},{8,24},{12,28},{16,0},{20,4},{24,8},{28,12},{1,17},{... | collective-permute-start | bytes 245768 | tf_op jit(solution)/shard_map/ppermute | solution.py:47
  356.6 14.8 %collective-permute-start.25 = (f32[64,640]{1,0:T(8,128)S(1)}, f32[64,640]{1,0:T(8,128)S(1)}, u32[]{:S(2)}, u32[]{:S(2)}) collective-permute-start(f32[64,640]{1,0:T(8,128)S(1)} %add_bitcast_fusion.2), channel_id=1, source_target_pairs={{0,2},{1,3},{2,0},{3,1},{4,6},{5,7},{6,4},{7,5},{8,10},{9,11},{10,... | collective-permute-start | bytes 491528 | tf_op jit(solution)/shard_map/ppermute | solution.py:47
  358.7 12.9 %collective-permute-start.32 = (f32[64,640]{1,0:T(8,128)S(1)}, f32[64,640]{1,0:T(8,128)S(1)}, u32[]{:S(2)}, u32[]{:S(2)}) collective-permute-start(f32[64,640]{1,0:T(8,128)S(1)} %add_bitcast_fusion.1), channel_id=1, source_target_pairs={{0,2},{1,3},{2,0},{3,1},{4,6},{5,7},{6,4},{7,5},{8,10},{9,11},{10,... | collective-permute-start | bytes 491528 | tf_op jit(solution)/shard_map/ppermute | solution.py:47
  360.0 5.5 %collective-permute-start.44 = (bf16[1,1,1,40,640]{4,3,2,1,0:T(8,128)(2,1)S(1)}, bf16[1,1,1,40,640]{4,3,2,1,0:T(8,128)(2,1)S(1)}, u32[]{:S(2)}, u32[]{:S(2)}) collective-permute-start(bf16[1,1,1,40,640]{4,3,2,1,0:T(8,128)(2,1)S(1)} %select_convert_fusion.26), channel_id=1, source_target_pairs={{0,16},{4,20},{8,24},{12,28},{16,0},{20,4},{24,8},{28,12},{1,17},{... | collective-permute-start | bytes 153608 | tf_op jit(solution)/shard_map/ppermute | solution.py:47
  367.1 6.9 %collective-permute-start.39 = (f32[64,640]{1,0:T(8,128)S(1)}, f32[64,640]{1,0:T(8,128)S(1)}, u32[]{:S(2)}, u32[]{:S(2)}) collective-permute-start(f32[64,640]{1,0:T(8,128)S(1)} %add_bitcast_fusion), channel_id=1, source_target_pairs={{0,2},{1,3},{2,0},{3,1},{4,6},{5,7},{6,4},{7,5},{8,10},{9,11},{10,... | collective-permute-start | bytes 491528 | tf_op jit(solution)/shard_map/ppermute | solution.py:47
  (48 other events, 190.2 us)

commit v2 on v0

v2 whole, which is shorter than its diff:
```python
import math

import jax
import jax.numpy as jnp
from jax import lax
from jax.experimental import pallas as pl
from jax.experimental.pallas import tpu as pltpu
from jax.sharding import Mesh
from jax.sharding import PartitionSpec as P

GROUPS = 32


epsilon = 1e-05
log_base = math.log(10000.0)
bf16 = jnp.bfloat16
f32 = jnp.float32
VMEM_BYTES = 56 * 1024 * 1024


def embedding(diffusion_step, embed_width):
    half_width = embed_width // 2
    frequency = jnp.exp(-log_base * jnp.arange(half_width, dtype=jnp.float32) / half_width)
    angles = diffusion_step.astype(jnp.float32) * frequency
    return jnp.concatenate([jnp.cos(angles), jnp.sin(angles)])


def flip(x, axis, mask=1):
    count = lax.axis_size(axis)
    return lax.ppermute(x, axis, [(i, i ^ mask) for i in range(count)])


def bits_of(count):
    return [1 << i for i in range(count.bit_length() - 1)]


def params():
    return pltpu.CompilerParams(vmem_limit_bytes=VMEM_BYTES)


def whole(shape):
    return pl.BlockSpec(shape, lambda *_: (0,) * len(shape), pipeline_mode=pl.Buffered(1))


def half_of(length):
    return -(-((length + 1) // 2) // 8) * 8


def is_upper(axis, mask):
    return (lax.axis_index(axis) & mask) != 0


def split_rows(x, upper):
    length = x.shape[-2]
    half = half_of(length)
    low = lax.slice_in_dim(x, 0, half, axis=x.ndim - 2)
    high = lax.slice_in_dim(x, length - half, length, axis=x.ndim - 2)
    return jnp.where(upper, high, low), jnp.where(upper, low, high)


def join_rows(x, length, axis, mask):
    upper = is_upper(axis, mask)
    got = flip(x, axis, mask)
    half = x.shape[0]
    low = jnp.where(upper, got, x)
    high = jnp.where(upper, x, got)
    return jnp.concatenate([low, high[2 * half - length :]], axis=0)


def reduce_all(keep, send):
    shards, taps, half, cols = keep.shape
    x = keep + flip(send, "core").astype(f32)
    x = x.reshape(shards, taps * half, cols)
    lengths = []
    for mask in bits_of(lax.axis_size("x")):
        lengths.append((x.shape[-2], mask))
        mine, other = split_rows(x, is_upper("x", mask))
        x = mine + flip(other.astype(bf16), "x", mask).astype(f32)
    x = lax.all_to_all(x.astype(bf16), "dp", 0, 0)
    x = jnp.sum(x.astype(f32), axis=0)
    for length, mask in lengths[::-1]:
        x = join_rows(x, length, "x", mask)
    x = x.reshape(taps, half, cols)
    got = flip(x, "core")
    upper = is_upper("core", 1)
    return jnp.concatenate([jnp.where(upper, got, x), jnp.where(upper, x, got)], axis=1)


def matmul_nt(a, b):
    return lax.dot_general(a, b, (((1,), (1,)), ((), ())), preferred_element_type=f32)


def matmul_tn(a, b):
    return lax.dot_general(a, b, (((0,), (0,)), ((), ())), preferred_element_type=f32)


def matmul(a, b):
    return jnp.dot(a, b, preferred_element_type=f32)


def group_mean(sums, same_ref, count):
    padded = jnp.broadcast_to(sums, (8, sums.shape[1]))
    total = jnp.dot(
        padded, same_ref[...], precision=lax.Precision.HIGHEST, preferred_element_type=f32
    )
    return total[:1] * (1.0 / count)


def write_views(ref, frame, values, breadth):
    pixels, channels = values.shape
    height = pixels // breadth
    column = lax.broadcasted_iota(jnp.int32, (pixels, channels), 0) & (breadth - 1)
    left = jnp.where(column == 0, 0.0, pltpu.roll(values, 1, 0))
    right = jnp.where(column == breadth - 1, 0.0, pltpu.roll(values, pixels - 1, 0))
    edge = jnp.zeros((1, breadth, channels), bf16)
    for s, moved in enumerate((left, values, right)):
        ref[s, frame, 0:1] = edge
        ref[s, frame, 1 : height + 1] = moved.astype(bf16).reshape(height, breadth, channels)
        ref[s, frame, height + 1 : height + 2] = edge


def norm_kernel(count, breadth, x_ref, same_ref, views_ref, mean_ref, scale_ref):
    for frame in range(x_ref.shape[0]):
        x = x_ref[frame].astype(f32)
        center = group_mean(jnp.sum(x, axis=0, keepdims=True), same_ref, count)
        deviation = x - center
        squares = jnp.sum(deviation * deviation, axis=0, keepdims=True)
        scaled = lax.rsqrt(group_mean(squares, same_ref, count) + epsilon)
        normal = deviation * scaled
        mean_ref[frame] = center
        scale_ref[frame] = scaled
        write_views(views_ref, frame, normal / (1.0 + jnp.exp(-normal)), breadth)


def normalize(frames, same, breadth):
    count, pixels, channels = frames.shape
    height = pixels // breadth
    return pl.pallas_call(
        lambda *refs: norm_kernel(pixels * (channels // GROUPS), breadth, *refs),
        out_shape=(
            jax.ShapeDtypeStruct((3, count, height + 2, breadth, channels), bf16),
            jax.ShapeDtypeStruct((count, 1, channels), f32),
            jax.ShapeDtypeStruct((count, 1, channels), f32),
        ),
        compiler_params=params(),
        name="norm",
    )(frames, same)


def turn_kernel(views_ref, out_ref):
    tap = pl.program_id(0)
    _, channels, rows = out_ref.shape
    height = views_ref.shape[2] - 2
    x = views_ref[tap % 3, :, pl.ds(tap // 3, height)].reshape(rows, channels)
    out_ref[0] = x.T


def turned_columns(views):
    _, frames, high, breadth, channels = views.shape
    rows = frames * (high - 2) * breadth
    return pl.pallas_call(
        turn_kernel,
        grid=(9,),
        in_specs=[whole(views.shape)],
        out_specs=pl.BlockSpec((1, channels, rows), lambda i: (i, 0, 0)),
        out_shape=jax.ShapeDtypeStruct((9, channels, rows), bf16),
        compiler_params=params(),
        name="turn",
    )(views)


def hidden_grad_kernel(breadth, cot_ref, next_ref, w_ref, back_ref, views_ref, sum_ref):
    outs = cot_ref.shape[0]
    channels = w_ref.shape[0]
    total = jnp.zeros((1, channels), f32)
    for o in range(outs):
        later = cot_ref[o + 1] if o + 1 < outs else next_ref[...]
        even = matmul_nt(cot_ref[o], w_ref[:, channels : 2 * channels])
        odd = matmul_nt(cot_ref[o], w_ref[:, 2 * channels : 3 * channels]) + matmul_nt(
            later, w_ref[:, :channels]
        )
        for frame, values in ((2 * o, even), (2 * o + 1, odd)):
            back_ref[frame] = values.astype(bf16)
            write_views(views_ref, frame, values, breadth)
            total += jnp.sum(values, axis=0, keepdims=True)
    sum_ref[...] = total


def hidden_gradient(cot, following, temporal, breadth):
    outs, pixels, channels = cot.shape
    return pl.pallas_call(
        lambda *refs: hidden_grad_kernel(breadth, *refs),
        out_shape=(
            jax.ShapeDtypeStruct((2 * outs, pixels, channels), bf16),
            jax.ShapeDtypeStruct((3, 2 * outs, pixels // breadth + 2, breadth, channels), bf16),
            jax.ShapeDtypeStruct((1, channels), f32),
        ),
        compiler_params=params(),
        name="hidden_grad",
    )(cot, following, temporal)


def store_halves(core_ref, grad, keep_ref, send_ref, slot):
    shards, _, half, channels = keep_ref.shape
    grad = grad.reshape(shards, 2 * half, channels)
    low, high = grad[:, :half], grad[:, half:]

    @pl.when(core_ref[0] == 0)
    def _():
        keep_ref[:, slot] = low
        send_ref[:, slot] = high.astype(bf16)

    @pl.when(core_ref[0] != 0)
    def _():
        keep_ref[:, slot] = high
        send_ref[:, slot] = low.astype(bf16)


def weight_grad_kernel(core_ref, x_ref, back_ref, keep_ref, send_ref):
    store_halves(core_ref, matmul(x_ref[0], back_ref[...]), keep_ref, send_ref, 0)


def weight_grad(turned, hidden_back, shards, core):
    taps = turned.shape[0]
    rows, channels = hidden_back.shape
    half = channels // shards // 2
    out_spec = pl.BlockSpec((shards, 1, half, channels), lambda i: (0, i, 0, 0))
    return pl.pallas_call(
        weight_grad_kernel,
        grid=(taps,),
        in_specs=[
            pl.BlockSpec(memory_space=pltpu.SMEM),
            pl.BlockSpec((1, channels, rows), lambda i: (i, 0, 0)),
            whole((rows, channels)),
        ],
        out_specs=(out_spec, out_spec),
        out_shape=(
            jax.ShapeDtypeStruct((shards, taps, half, channels), f32),
            jax.ShapeDtypeStruct((shards, taps, half, channels), bf16),
        ),
        compiler_params=params(),
        name="weight_grad",
    )(core, turned, hidden_back)


def temporal_grad_kernel(core_ref, hidden_ref, before_ref, cot_ref, keep_ref, send_ref):
    for k in range(3):
        grad = 0.0
        for o in range(cot_ref.shape[0]):
            frame = 2 * o + k - 1
            x = before_ref[...] if frame < 0 else hidden_ref[frame]
            grad += matmul_tn(x, cot_ref[o])
        store_halves(core_ref, grad, keep_ref, send_ref, k)


def temporal_grad_parts(hidden, before, cot, shards, core):
    channels = cot.shape[2]
    half = channels // shards // 2
    vmem = pl.BlockSpec(memory_space=pltpu.VMEM)
    return pl.pallas_call(
        temporal_grad_kernel,
        in_specs=[pl.BlockSpec(memory_space=pltpu.SMEM), vmem, vmem, vmem],
        out_shape=(
            jax.ShapeDtypeStruct((shards, 3, half, channels), f32),
            jax.ShapeDtypeStruct((shards, 3, half, channels), bf16),
        ),
        compiler_params=params(),
        name="temporal_grad",
    )(core, hidden, before, cot)


def temporal_kernel(hidden_ref, before_ref, w_ref, out_ref):
    channels = w_ref.shape[0]
    for o in range(out_ref.shape[0]):
        total = 0.0
        for k in range(3):
            frame = 2 * o + k - 1
            x = before_ref[...] if frame < 0 else hidden_ref[frame]
            total += matmul(x, w_ref[:, k * channels : (k + 1) * channels])
        out_ref[o] = total


def temporal_forward(hidden, before, temporal):
    frames, pixels, channels = hidden.shape
    return pl.pallas_call(
        temporal_kernel,
        out_shape=jax.ShapeDtypeStruct((frames // 2, pixels, channels), f32),
        compiler_params=params(),
        name="temporal",
    )(hidden, before, temporal)


def conv_forward_kernel(views_ref, w_ref, shift_ref, out_ref, acc_ref):
    tap = pl.program_id(0)
    rows, channels = acc_ref.shape
    height = views_ref.shape[2] - 2
    x = views_ref[tap % 3, :, pl.ds(tap // 3, height)].reshape(rows, channels)

    @pl.when(tap == 0)
    def _():
        acc_ref[...] = jnp.broadcast_to(shift_ref[...], (rows, channels))

    acc_ref[...] += matmul(x, w_ref[...])

    @pl.when(tap == 8)
    def _():
        out_ref[...] = acc_ref[...].astype(bf16).reshape(out_ref.shape)


def conv_forward(views, spatial, shift):
    _, frames, high, breadth, channels = views.shape
    pixels = (high - 2) * breadth
    return pl.pallas_call(
        conv_forward_kernel,
        grid=(9,),
        in_specs=[
            whole(views.shape),
            pl.BlockSpec((channels, channels), lambda i: (0, i)),
            whole((1, channels)),
        ],
        out_specs=whole((frames, pixels, channels)),
        out_shape=jax.ShapeDtypeStruct((frames, pixels, channels), bf16),
        scratch_shapes=[pltpu.VMEM((frames * pixels, channels), f32)],
        compiler_params=params(),
        name="conv_forward",
    )(views, spatial, shift)


def conv_back_kernel(
    count, views_ref, w_ref, x_ref, mean_ref, scale_ref, same_ref, out_ref, acc_ref
):
    tap = pl.program_id(0)
    rows, channels = acc_ref.shape
    height = views_ref.shape[2] - 2
    x = views_ref[2 - tap % 3, :, pl.ds(2 - tap // 3, height)].reshape(rows, channels)

    @pl.when(tap == 0)
    def _():
        acc_ref[...] = matmul_nt(x, w_ref[...])

    @pl.when(tap != 0)
    def _():
        acc_ref[...] += matmul_nt(x, w_ref[...])

    @pl.when(tap == 8)
    def _():
        frames, pixels, _ = x_ref.shape
        for frame in range(frames):
            scaled = scale_ref[frame]
            normal = (x_ref[frame].astype(f32) - mean_ref[frame]) * scaled
            gate = 1.0 / (1.0 + jnp.exp(-normal))
            slope = gate * (1.0 + normal * (1.0 - gate))
            grad = acc_ref[frame * pixels : (frame + 1) * pixels] * slope
            one = group_mean(jnp.sum(grad, axis=0, keepdims=True), same_ref, count)
            two = group_mean(jnp.sum(grad * normal, axis=0, keepdims=True), same_ref, count)
            out_ref[frame] = (grad - one - normal * two) * scaled


def conv_back(views, spatial, frames, mean, scale, same):
    count, pixels, channels = frames.shape
    return pl.pallas_call(
        lambda *refs: conv_back_kernel(pixels * (channels // GROUPS), *refs),
        grid=(9,),
        in_specs=[
            whole(views.shape),
            pl.BlockSpec((channels, channels), lambda i: (0, i)),
            whole(frames.shape),
            whole(mean.shape),
            whole(scale.shape),
            whole(same.shape),
        ],
        out_specs=whole(frames.shape),
        out_shape=jax.ShapeDtypeStruct(frames.shape, f32),
        scratch_shapes=[pltpu.VMEM((count * pixels, channels), f32)],
        compiler_params=params(),
        name="conv_back",
    )(views, spatial, frames, mean, scale, same)


def neighbours(x_size, step):
    count = 2 * x_size
    return [(i, i + step) for i in range(count) if 0 <= i + step < count]


def body(latents, cotangent, timesteps, spatial_weight, temporal_weight, time_weight):
    clip_frames = latents[0]
    frame_count, height, breadth, channels = clip_frames.shape
    pixels = height * breadth
    out_count = frame_count // 2
    dp = lax.axis_size("dp")
    x_size = lax.axis_size("x")
    share = channels // dp
    half = share // 2
    core = lax.axis_index("core")
    core_scalar = core[None].astype(jnp.int32)
    frames = clip_frames.reshape(frame_count, pixels, channels)

    cot = cotangent[0].reshape(out_count, pixels, channels)
    following = lax.ppermute(cot[0], ("x", "core"), neighbours(x_size, -1))

    wide = jnp.concatenate([temporal_weight, time_weight], axis=1)
    wide_mine = lax.dynamic_slice_in_dim(wide, core * half, half, axis=0)
    wide_full = lax.all_gather(wide_mine, ("dp", "core"), axis=0, tiled=True)
    spatial_mine = lax.dynamic_slice_in_dim(spatial_weight, core * half, half, axis=0)
    spatial_full = lax.all_gather(spatial_mine, ("dp", "core"), axis=0, tiled=True)

    group = lax.broadcasted_iota(jnp.int32, (channels, channels), 0) // (channels // GROUPS)
    same = (group == group.T).astype(f32)
    views, mean, scale = normalize(frames, same, breadth)
    turned = turned_columns(views)

    hidden_back, back_views, shift_sum = hidden_gradient(cot, following, wide_full, breadth)
    flat_back = hidden_back.reshape(frame_count * pixels, channels)
    spatial_rows = reduce_all(*weight_grad(turned, flat_back, dp, core_scalar))

    time_full = wide_full[:, 3 * channels :]
    embedded = embedding(timesteps[0], time_full.shape[1])
    time_shift = jnp.dot(time_full.astype(f32), embedded, precision=lax.Precision.HIGHEST)
    hidden = conv_forward(views, spatial_full, time_shift[None])
    before = lax.ppermute(hidden[-1], ("x", "core"), neighbours(x_size, 1))
    temporal_rows = reduce_all(*temporal_grad_parts(hidden, before, cot, dp, core_scalar))
    result = temporal_forward(hidden, before, wide_full)
    downsampled = result.reshape(1, out_count, height, breadth, channels)

    input_grad = conv_back(back_views, spatial_full, frames, mean, scale, same)
    input_grad = input_grad.reshape(1, frame_count, height, breadth, channels)

    sums = shift_sum + flip(shift_sum, "core")
    for mask in bits_of(x_size):
        sums = sums + flip(sums, "x", mask)
    pairs = jnp.concatenate([sums, embedded[None]], axis=1)
    for mask in bits_of(dp):
        pairs = jnp.concatenate([pairs, flip(pairs, "dp", mask)], axis=0)
    mine = lax.dynamic_slice_in_dim(
        pairs[:, :channels], lax.axis_index("dp") * share, share, axis=1
    )
    time_grad = lax.dot_general(
        mine,
        pairs[:, channels:],
        (((0,), (0,)), ((), ())),
        precision=lax.Precision.HIGHEST,
        preferred_element_type=f32,
    )

    spatial_grad = jnp.concatenate([spatial_rows[i] for i in range(9)], axis=1)
    temporal_grad = jnp.concatenate([temporal_rows[i] for i in range(3)], axis=1)
    return (downsampled, input_grad, spatial_grad, temporal_grad, time_grad)


def solution(mesh):
    dp, tm = mesh.devices.shape
    fine = Mesh(mesh.devices.reshape(dp, tm // 2, 2), ("dp", "x", "core"))
    placed = (
        P("dp", ("x", "core"), None, None, None),
        P("dp", ("x", "core"), None, None, None),
        P("dp"),
        P("dp", None),
        P("dp", None),
        P("dp", None),
    )
    return jax.shard_map(
        body,
        mesh=fine,
        in_specs=placed,
        out_specs=(
            P("dp", ("x", "core"), None, None, None),
            P("dp", ("x", "core"), None, None, None),
            P("dp", None),
            P("dp", None),
            P("dp", None),
        ),
        check_vma=False,
    )
```

time: 725 us -> 293 us (0.40)
  waiting for transfers between devices: 508 us -> 119 us
  Pallas kernels: 0 us -> 97.8 us
  local copies, waits for them, and re-layouts: 75.6 us -> 2.6 us
  matrix products: 52.9 us -> 2.92 us
  blocking collectives: 33.4 us -> 0 us
  starting transfers between devices: 3.69 us -> 31 us
  other arithmetic: 35.7 us -> 23.2 us
    reduce_scatter x1 -> x0, waiting for transfers between devices: 333 us -> none  [body(): lax.psum_scatter(jnp.concatenate([spatial_part.reshape(row_share * lax.ax...]
    pallas_call x0 -> x8, Pallas kernels: none -> 97.8 us  [the longest x1 25.3 us: conv_back(): pl.pallas_call(lambda *refs: conv_back_kernel(pixels * (channels // GROUP...]
    all_gather x2, waiting for transfers between devices: 121 us -> 23.3 us  [the longest x1 23.3 us: body(): wide_full = lax.all_gather(wide_mine, ('dp', 'core'), axis=0, tiled=True)]
    ppermute x2 -> x15, waiting for transfers between devices: 1.95 us -> 87 us  [the longest x13 85.8 us: flip(): return lax.ppermute(x, axis, [(i, i ^ mask) for i in range(count)])]
    psum x1 -> x0, waiting for transfers between devices: 50.8 us -> none  [body(): totals = lax.psum(grad_shard, 'tm')]
    dot_general x7 -> x2, matrix products: 52.9 us -> 2.92 us  [the longest x1 1.94 us: body(): jnp.dot(time_full.astype(f32), embedded, precision=lax.Precision.HIGHEST)]
    all_gather x1 -> x0, blocking collectives: 33.4 us -> none  [body(): lax.all_gather(time_weight, 'dp', axis=0, tiled=True)]
    reshape x2 -> x0, local copies, waits for them, and re-layouts: 21.2 us -> none  [the longest x1 15.1 us: body(): spatial_part.reshape(row_share * lax.axis_size('dp'), 9 * channels)]
  transfers between devices with their start and end apart: 6 -> 19, of which waited for: 5 -> 11; matrix products, arithmetic and copies ran while one was open for 7% -> 8% of each run, Pallas kernels for 0% -> 34%
where the time goes in v2:
time: 293 us; the launch traced here: 292 us
  waiting for transfers between devices  119 us (41%)
  Pallas kernels  97.8 us (33%)
  starting transfers between devices  31 us (11%)
  other arithmetic  23.2 us (8%)
  between operations  15 us (5%)
    ppermute x13, waiting for transfers between devices, flip(): return lax.ppermute(x, axis, [(i, i ^ mask) for i in range(count)])  85.8 us
    pallas_call x1, Pallas kernels, conv_back(): pl.pallas_call(lambda *refs: conv_back_kernel(pixels * (channels // GROUP...  25.3 us
    all_gather x1, waiting for transfers between devices, body(): wide_full = lax.all_gather(wide_mine, ('dp', 'core'), axis=0, tiled=True)  23.3 us
    ppermute x13, starting transfers between devices, flip(): return lax.ppermute(x, axis, [(i, i ^ mask) for i in range(count)])  20 us
    pallas_call x1, Pallas kernels, conv_forward(): pl.pallas_call(conv_forward_kernel, grid=(9,), in_specs=[whole(views.shap...  16.8 us
    pallas_call x1, Pallas kernels, weight_grad(): pl.pallas_call(weight_grad_kernel, grid=(taps,), in_specs=[pl.BlockSpec(m...  16.5 us
    pallas_call x1, Pallas kernels, normalize(): pl.pallas_call(lambda *refs: norm_kernel(pixels * (channels // GROUPS), b...  11.4 us
    pallas_call x1, Pallas kernels, turned_columns(): pl.pallas_call(turn_kernel, grid=(9,), in_specs=[whole(views.shape)], out...  9.73 us
  transfers between devices with their start and end apart: 19, of which 11 were waited for; matrix products, arithmetic and copies ran while one was open for 8% of the time, Pallas kernels for 34%

profile of v2, /device:TPU:0, one launch (start us, length us, event | category | flops | bytes accessed | tf_op | source)
XLA Modules:
  0.0 291.6 jit_solution(14834531797290244611)
XLA Ops:
  7.2 1.7 fusion.34
  9.0 0.8 constant_dynamic-slice_fusion
  9.9 1.3 collective-permute-start.1
  11.2 1.5 fusion.refs_1_.refs_5_
  12.7 11.4 %norm.1 = (bf16[3,4,18,16,640]{4,3,2,1,0:T(8,128)(2,1)}, f32[4,1,640]{2,1,0:T(1,128)}, f32[4,1,640]{2,1,0:T(1,128)}) custom-call(bf16[4,256,640]{2,1,0:T(8,128)(2,1)} %bitcast.63, f32[640,640]{1,0:T(8,128)} %fusion.refs_1_.refs_5_), custom_call_target="tpu_custom_call" | custom-call | tf_op jit(solution)/shard_map/norm/pallas_call | solution.py:138
  24.2 9.7 %turn.1.x_ref = bf16[9,640,1024]{2,1,0:T(8,128)(2,1)} custom-call(bf16[3,4,18,16,640]{4,3,2,1,0:T(8,128)(2,1)} %get-tuple-element.15.views_ref), custom_call_target="tpu_custom_call" | custom-call | tf_op jit(solution)/shard_map/turn/pallas_call | solution.py:161
  33.9 23.3 %all-gather.5.cloned.1.call-done.w_ref.refs_2_ = bf16[640,2176]{1,0:T(8,128)(2,1)} async-done(((bf16[40,2176]{1,0:T(8,128)(2,1)}), bf16[640,2176]{1,0:T(8,128)(2,1)}) %all-gather.5.cloned.1.call-update) | async-done | bytes 2785296 | tf_op jit(solution)/shard_map/all_gather | solution.py:403
  57.3 6.8 %hidden_grad.1 = (bf16[4,256,640]{2,1,0:T(8,128)(2,1)}, bf16[3,4,18,16,640]{4,3,2,1,0:T(8,128)(2,1)}, f32[1,640]{1,0:T(1,128)}) custom-call(bf16[2,256,640]{2,1,0:T(8,128)(2,1)} %bitcast.65, bf16[256,640]{1,0:T(8,128)(2,1)} %copy-done.5, bf16[640,2176]{1,0:T(8,128)(2,1)} %all-gather.5.cloned.1.call-done.w_ref.refs_2_), custom_call_target="tpu_custom_call" | custom-call | tf_op jit(solution)/shard_map/hidden_grad/pallas_call | solution.py:191
  64.1 16.5 %weight_grad.1 = (f32[8,9,40,640]{3,2,1,0:T(8,128)}, bf16[8,9,40,640]{3,2,1,0:T(8,128)(2,1)}) custom-call(s32[1]{0:T(128)} %bitcast.8.core_ref, bf16[9,640,1024]{2,1,0:T(8,128)(2,1)} %turn.1.x_ref, bf16[1024,640]{1,0:T(8,128)(2,1)} %bitcast.70), custom_call_target="tpu_custom_call" | custom-call | tf_op jit(solution)/shard_map/weight_grad/pallas_call | solution.py:228
  80.8 6.5 %collective-permute-done.2 = bf16[8,9,40,640]{3,2,1,0:T(8,128)(2,1)} collective-permute-done((bf16[8,9,40,640]{3,2,1,0:T(8,128)(2,1)}, bf16[8,9,40,640]{3,2,1,0:T(8,128)(2,1)}, u32[]{:S(2)}, u32[]{:S(2)}) %collective-permute-start.2) | collective-permute-done | bytes 3686432 | tf_op jit(solution)/shard_map/ppermute | solution.py:30
  87.3 5.6 %convert_add_fusion = f32[8,9,40,640]{3,2,1,0:T(8,128)S(1)} fusion(f32[8,9,40,640]{3,2,1,0:T(8,128)} %get-tuple-element.20, bf16[8,9,40,640]{3,2,1,0:T(8,128)(2,1)} %collective-permute-done.2), kind=kLoop, calls=%fused_computation | loop fusion | flops 3686400 | bytes 18432000 | tf_op jit(solution)/shard_map/add | solution.py:72
  93.3 1.3 collective-permute-start.3
  94.7 42.0 %collective-permute-done.3 = bf16[8,184,640]{2,1,0:T(8,128)(2,1)S(1)} collective-permute-done((bf16[8,184,640]{2,1,0:T(8,128)(2,1)S(1)}, bf16[8,184,640]{2,1,0:T(8,128)(2,1)S(1)}, u32[]{:S(2)}, u32[]{:S(2)}) %collective-permute-start.3) | collective-permute-done | bytes 1884192 | tf_op jit(solution)/shard_map/ppermute | solution.py:30
  136.7 2.0 add_convert_fusion
  138.7 3.6 %all-to-all-start = ((bf16[8,184,640]{2,1,0:T(8,128)(2,1)}), bf16[8,184,640]{2,1,0:T(8,128)(2,1)S(1)}, u32[]{:S(2)}, u32[]{:S(2)}) async-start(bf16[8,184,640]{2,1,0:T(8,128)(2,1)} %add_convert_fusion), calls=%async_computation | async-start | bytes 3768320 | tf_op jit(solution)/shard_map/all_to_all | solution.py:79
  143.0 1.9 fusion.1.shift_ref
  144.9 16.8 %conv_forward.1.hidden_ref = bf16[4,256,640]{2,1,0:T(8,128)(2,1)} custom-call(bf16[3,4,18,16,640]{4,3,2,1,0:T(8,128)(2,1)} %get-tuple-element.15.views_ref, bf16[640,5760]{1,0:T(8,128)(2,1)} %all-gather.3.cloned.1.call-done.w_ref.refs_1_, f32[1,640]{1,0:T(1,128)} %fusion.1.shift_ref), custom_call_target="tpu_custom_call" | custom-call | tf_op jit(solution)/shard_map/conv_forward/pallas_call | solution.py:313
  161.7 1.0 slice_bitcast_fusion
  162.7 1.4 collective-permute-start
  164.1 1.2 collective-permute-done.before_ref
  165.4 0.7 copy-done.4
  166.1 6.1 %temporal_grad.1 = (f32[8,3,40,640]{3,2,1,0:T(8,128)}, bf16[8,3,40,640]{3,2,1,0:T(8,128)(2,1)}) custom-call(s32[1]{0:T(128)} %bitcast.8.core_ref, bf16[4,256,640]{2,1,0:T(8,128)(2,1)} %conv_forward.1.hidden_ref, bf16[256,640]{1,0:T(8,128)(2,1)} %copy-done.4, bf16[2,256,640]{2,1,0:T(8,128)(2,1)} %bitcast.66), custom_call_target="tpu_custom_call" | custom-call | tf_op jit(solution)/shard_map/temporal_grad/pallas_call | solution.py:260
  172.2 4.8 %collective-permute-start.6 = (bf16[8,3,40,640]{3,2,1,0:T(8,128)(2,1)}, bf16[8,3,40,640]{3,2,1,0:T(8,128)(2,1)}, u32[]{:S(2)}, u32[]{:S(2)}) collective-permute-start(bf16[8,3,40,640]{3,2,1,0:T(8,128)(2,1)} %get-tuple-element.23), channel_id=1, source_target_pairs={{0,1},{1,0},{2,3},{3,2},{4,5},{5,4},{6,7},{7,6},{8,9},{9,8},{10,11... | collective-permute-start | bytes 3686408 | tf_op jit(solution)/shard_map/ppermute | solution.py:30
  177.0 8.8 %all-to-all-done = bf16[8,184,640]{2,1,0:T(8,128)(2,1)S(1)} async-done(((bf16[8,184,640]{2,1,0:T(8,128)(2,1)}), bf16[8,184,640]{2,1,0:T(8,128)(2,1)S(1)}, u32[]{:S(2)}, u32[]{:S(2)}) %all-to-all-start) | async-done | bytes 1884192 | tf_op jit(solution)/shard_map/all_to_all | solution.py:79
  186.1 1.6 collective-permute-start.4
  187.7 9.7 %collective-permute-done.4 = f32[184,640]{1,0:T(8,128)S(1)} collective-permute-done((f32[184,640]{1,0:T(8,128)S(1)}, f32[184,640]{1,0:T(8,128)S(1)}, u32[]{:S(2)}, u32[]{:S(2)}) %collective-permute-start.4) | collective-permute-done | bytes 471072 | tf_op jit(solution)/shard_map/ppermute | solution.py:30
  197.5 1.6 convert_add_fusion.1
  199.2 1.8 collective-permute-start.7
  201.7 1.6 collective-permute-done.10
  203.8 10.1 %collective-permute-done.11 = f32[1,640]{1,0:T(1,128)S(1)} collective-permute-done((f32[1,640]{1,0:T(1,128)S(1)}, f32[1,640]{1,0:T(1,128)S(1)}, u32[]{:S(2)}, u32[]{:S(2)}) %collective-permute-start.11) | collective-permute-done | bytes 2592 | tf_op jit(solution)/shard_map/ppermute | solution.py:30
  213.9 2.2 collective-permute-start.12
  216.1 1.6 collective-permute-done.12
  217.7 2.2 collective-permute-start.13
  219.9 1.1 add_convert_fusion.1
  221.0 4.6 %all-to-all-start.1 = ((bf16[8,64,640]{2,1,0:T(8,128)(2,1)}), bf16[8,64,640]{2,1,0:T(8,128)(2,1)S(1)}, u32[]{:S(2)}, u32[]{:S(2)}) async-start(bf16[8,64,640]{2,1,0:T(8,128)(2,1)} %add_convert_fusion.1), calls=%async_computation.1 | async-start | bytes 1310720 | tf_op jit(solution)/shard_map/all_to_all | solution.py:79
  225.6 3.0 %collective-permute-start.14 = (f32[4,896]{1,0:T(4,128)S(1)}, f32[4,896]{1,0:T(4,128)S(1)}, u32[]{:S(2)}, u32[]{:S(2)}) collective-permute-start(f32[4,896]{1,0:T(4,128)S(1)} %pad_maximum_fusion.6), channel_id=1, source_target_pairs={{0,16},{4,20},{8,24},{12,28},{16,0},{20,4},{24,8},{28,12},{1,17},{... | collective-permute-start | bytes 43016 | tf_op jit(solution)/shard_map/ppermute | solution.py:30
  228.6 11.9 %collective-permute-done.14 = f32[4,896]{1,0:T(4,128)S(1)} collective-permute-done((f32[4,896]{1,0:T(4,128)S(1)}, f32[4,896]{1,0:T(4,128)S(1)}, u32[]{:S(2)}, u32[]{:S(2)}) %collective-permute-start.14) | collective-permute-done | bytes 14368 | tf_op jit(solution)/shard_map/ppermute | solution.py:30
  240.5 1.0 fusion.35
  241.5 25.3 %conv_back.1 = f32[4,256,640]{2,1,0:T(8,128)} custom-call(bf16[3,4,18,16,640]{4,3,2,1,0:T(8,128)(2,1)} %get-tuple-element.16.refs_0_, bf16[640,5760]{1,0:T(8,128)(2,1)} %all-gather.3.cloned.1.call-done.w_ref.refs_1_, bf16[4,256,640]{2,1,0:T(8,128)(2,1)} %bitcast.64, f32[4,1,640]{2,1,0:T(1,128)} %get-tuple-element.17.refs_3_, ...), custom_call_target="tpu_custom_call" | custom-call | tf_op jit(solution)/shard_map/conv_back/pallas_call | solution.py:361
  266.8 5.2 %temporal.1 = f32[2,256,640]{2,1,0:T(8,128)} custom-call(bf16[4,256,640]{2,1,0:T(8,128)(2,1)} %conv_forward.1.hidden_ref, bf16[256,640]{1,0:T(8,128)(2,1)} %copy-done.4, bf16[640,2176]{1,0:T(8,128)(2,1)} %all-gather.5.cloned.1.call-done.w_ref.refs_2_), custom_call_target="tpu_custom_call" | custom-call | tf_op jit(solution)/shard_map/temporal/pallas_call | solution.py:285
  272.0 1.3 broadcast_select_fusion
  273.3 0.7 fusion.12
  274.0 0.7 fusion.15
  274.7 0.7 fusion.18
  276.2 1.6 collective-permute-start.8
  279.2 2.4 collective-permute-done.8
  281.7 0.7 fusion.30
  283.9 0.9 pad_maximum_fusion.1
  (59 shorter events, 6.3 us)
Async XLA Ops:
  7.2 1.9 copy-start
  7.2 2.7 copy-start.2
  7.2 50.1 %all-gather.5.cloned.1.call-start = ((), (), s32[]{:S(2)}) async-start(), calls=%async_computation.3 | async-start | bytes 2959360 | tf_op jit(solution)/shard_map/all_gather | solution.py:403
  9.0 136.0 %all-gather.3.cloned.1.call-start = ((), (), s32[]{:S(2)}) async-start(), calls=%async_computation.2 | async-start | bytes 7833600 | tf_op jit(solution)/shard_map/all_gather | solution.py:405
  9.9 24.0 %collective-permute-start.1 = (bf16[256,640]{1,0:T(8,128)(2,1)S(1)}, bf16[256,640]{1,0:T(8,128)(2,1)S(1)}, u32[]{:S(2)}, u32[]{:S(2)}) collective-permute-start(bf16[256,640]{1,0:T(8,128)(2,1)S(1)} %bitcast.74), channel_id=1, source_target_pairs={{1,0},{2,1},{3,2},{5,4},{6,5},{7,6},{9,8},{10,9},{11,10},{13,12},{... | collective-permute-start | bytes 983048 | tf_op jit(solution)/shard_map/ppermute | solution.py:399
  33.9 23.3 %copy-start.5 = (bf16[256,640]{1,0:T(8,128)(2,1)}, bf16[256,640]{1,0:T(8,128)(2,1)S(1)}, u32[]{:S(2)}) copy-start(bf16[256,640]{1,0:T(8,128)(2,1)S(1)} %collective-permute-done.1.refs_1_) | copy-start | bytes 983044
  80.5 6.8 %collective-permute-start.2 = (bf16[8,9,40,640]{3,2,1,0:T(8,128)(2,1)}, bf16[8,9,40,640]{3,2,1,0:T(8,128)(2,1)}, u32[]{:S(2)}, u32[]{:S(2)}) collective-permute-start(bf16[8,9,40,640]{3,2,1,0:T(8,128)(2,1)} %get-tuple-element.21), channel_id=1, source_target_pairs={{0,1},{1,0},{2,3},{3,2},{4,5},{5,4},{6,7},{7,6},{8,9},{9,8},{10,11... | collective-permute-start | bytes 11059208 | tf_op jit(solution)/shard_map/ppermute | solution.py:30
  93.3 43.3 %collective-permute-start.3 = (bf16[8,184,640]{2,1,0:T(8,128)(2,1)S(1)}, bf16[8,184,640]{2,1,0:T(8,128)(2,1)S(1)}, u32[]{:S(2)}, u32[]{:S(2)}) collective-permute-start(bf16[8,184,640]{2,1,0:T(8,128)(2,1)S(1)} %select_convert_fusion), channel_id=1, source_target_pairs={{0,2},{2,0},{1,3},{3,1},{4,6},{6,4},{5,7},{7,5},{8,10},{10,8},{9,1... | collective-permute-start | bytes 5652488 | tf_op jit(solution)/shard_map/ppermute | solution.py:30
  138.7 47.1 %all-to-all-start = ((bf16[8,184,640]{2,1,0:T(8,128)(2,1)}), bf16[8,184,640]{2,1,0:T(8,128)(2,1)S(1)}, u32[]{:S(2)}, u32[]{:S(2)}) async-start(bf16[8,184,640]{2,1,0:T(8,128)(2,1)} %add_convert_fusion), calls=%async_computation | async-start | bytes 3768320 | tf_op jit(solution)/shard_map/all_to_all | solution.py:79
  162.7 2.6 collective-permute-start
  165.4 0.7 copy-start.4
  172.2 25.3 %collective-permute-start.6 = (bf16[8,3,40,640]{3,2,1,0:T(8,128)(2,1)}, bf16[8,3,40,640]{3,2,1,0:T(8,128)(2,1)}, u32[]{:S(2)}, u32[]{:S(2)}) collective-permute-start(bf16[8,3,40,640]{3,2,1,0:T(8,128)(2,1)} %get-tuple-element.23), channel_id=1, source_target_pairs={{0,1},{1,0},{2,3},{3,2},{4,5},{5,4},{6,7},{7,6},{8,9},{9,8},{10,11... | collective-permute-start | bytes 3686408 | tf_op jit(solution)/shard_map/ppermute | solution.py:30
  185.8 11.7 %copy-start.3 = (f32[8,3,40,640]{3,2,1,0:T(8,128)S(1)}, f32[8,3,40,640]{3,2,1,0:T(8,128)}, u32[]{:S(2)}) copy-start(f32[8,3,40,640]{3,2,1,0:T(8,128)} %get-tuple-element.22) | copy-start | bytes 7372804
  186.1 11.4 %collective-permute-start.4 = (f32[184,640]{1,0:T(8,128)S(1)}, f32[184,640]{1,0:T(8,128)S(1)}, u32[]{:S(2)}, u32[]{:S(2)}) collective-permute-start(f32[184,640]{1,0:T(8,128)S(1)} %convert_reduce_fusion), channel_id=1, source_target_pairs={{0,2},{2,0},{1,3},{3,1},{4,6},{6,4},{5,7},{7,5},{8,10},{10,8},{9,1... | collective-permute-start | bytes 1413128 | tf_op jit(solution)/shard_map/ppermute | solution.py:30
  199.2 2.0 copy-start.6
  199.2 20.7 %collective-permute-start.7 = (bf16[8,64,640]{2,1,0:T(8,128)(2,1)S(1)}, bf16[8,64,640]{2,1,0:T(8,128)(2,1)S(1)}, u32[]{:S(2)}, u32[]{:S(2)}) collective-permute-start(bf16[8,64,640]{2,1,0:T(8,128)(2,1)S(1)} %select_convert_fusion.1), channel_id=1, source_target_pairs={{0,2},{2,0},{1,3},{3,1},{4,6},{6,4},{5,7},{7,5},{8,10},{10,8},{9,1... | collective-permute-start | bytes 1966088 | tf_op jit(solution)/shard_map/ppermute | solution.py:30
  201.2 70.9 %collective-permute-start.5 = (f32[9,40,640]{2,1,0:T(8,128)S(1)}, f32[9,40,640]{2,1,0:T(8,128)}, u32[]{:S(2)}, u32[]{:S(2)}) collective-permute-start(f32[9,40,640]{2,1,0:T(8,128)S(1)} %bitcast.67), channel_id=1, source_target_pairs={{0,1},{1,0},{2,3},{3,2},{4,5},{5,4},{6,7},{7,6},{8,9},{9,8},{10,11... | collective-permute-start | bytes 2764808 | tf_op jit(solution)/shard_map/ppermute | solution.py:30
  201.2 2.1 collective-permute-start.10
  203.3 10.5 %collective-permute-start.11 = (f32[1,640]{1,0:T(1,128)S(1)}, f32[1,640]{1,0:T(1,128)S(1)}, u32[]{:S(2)}, u32[]{:S(2)}) collective-permute-start(f32[1,640]{1,0:T(1,128)S(1)} %add.32), channel_id=1, source_target_pairs={{0,2},{2,0},{1,3},{3,1},{4,6},{6,4},{5,7},{7,5},{8,10},{10,8},{9,1... | collective-permute-start | bytes 7688 | tf_op jit(solution)/shard_map/ppermute | solution.py:30
  213.9 3.8 %collective-permute-start.12 = (f32[1,896]{1,0:T(1,128)S(1)}, f32[1,896]{1,0:T(1,128)S(1)}, u32[]{:S(2)}, u32[]{:S(2)}) collective-permute-start(f32[1,896]{1,0:T(1,128)S(1)} %pad_maximum_fusion.8), channel_id=1, source_target_pairs={{0,4},{4,0},{8,12},{12,8},{16,20},{20,16},{24,28},{28,24},{1,5},{5... | collective-permute-start | bytes 10760 | tf_op jit(solution)/shard_map/ppermute | solution.py:30
  217.7 7.9 %collective-permute-start.13 = (f32[2,896]{1,0:T(2,128)S(1)}, f32[2,896]{1,0:T(2,128)S(1)}, u32[]{:S(2)}, u32[]{:S(2)}) collective-permute-start(f32[2,896]{1,0:T(2,128)S(1)} %pad_maximum_fusion.7), channel_id=1, source_target_pairs={{0,8},{4,12},{8,0},{12,4},{16,24},{20,28},{24,16},{28,20},{1,9},{5... | collective-permute-start | bytes 21512 | tf_op jit(solution)/shard_map/ppermute | solution.py:30
  221.0 55.1 %all-to-all-start.1 = ((bf16[8,64,640]{2,1,0:T(8,128)(2,1)}), bf16[8,64,640]{2,1,0:T(8,128)(2,1)S(1)}, u32[]{:S(2)}, u32[]{:S(2)}) async-start(bf16[8,64,640]{2,1,0:T(8,128)(2,1)} %add_convert_fusion.1), calls=%async_computation.1 | async-start | bytes 1310720 | tf_op jit(solution)/shard_map/all_to_all | solution.py:79
  225.6 14.9 %collective-permute-start.14 = (f32[4,896]{1,0:T(4,128)S(1)}, f32[4,896]{1,0:T(4,128)S(1)}, u32[]{:S(2)}, u32[]{:S(2)}) collective-permute-start(f32[4,896]{1,0:T(4,128)S(1)} %pad_maximum_fusion.6), channel_id=1, source_target_pairs={{0,16},{4,20},{8,24},{12,28},{16,0},{20,4},{24,8},{28,12},{1,17},{... | collective-permute-start | bytes 43016 | tf_op jit(solution)/shard_map/ppermute | solution.py:30
  276.2 5.4 %collective-permute-start.8 = (f32[64,640]{1,0:T(8,128)S(1)}, f32[64,640]{1,0:T(8,128)S(1)}, u32[]{:S(2)}, u32[]{:S(2)}) collective-permute-start(f32[64,640]{1,0:T(8,128)S(1)} %convert_reduce_fusion.1), channel_id=1, source_target_pairs={{0,2},{2,0},{1,3},{3,1},{4,6},{6,4},{5,7},{7,5},{8,10},{10,8},{9,1... | collective-permute-start | bytes 491528 | tf_op jit(solution)/shard_map/ppermute | solution.py:30
  281.7 2.2 collective-permute-start.9
  283.1 1.7 copy-start.1
Sparse Core Ops, SparseCore 0:
  10.8 46.4 all-gather.4
  60.0 66.9 all-gather.2

commit v3 on v2

v3 whole, which is shorter than its diff:
```python
import math

import jax
import jax.numpy as jnp
from jax import lax
from jax.experimental import pallas as pl
from jax.experimental.pallas import tpu as pltpu
from jax.sharding import Mesh
from jax.sharding import PartitionSpec as P

GROUPS = 32


epsilon = 1e-05
log_base = math.log(10000.0)
bf16 = jnp.bfloat16
f32 = jnp.float32
VMEM_BYTES = 56 * 1024 * 1024


def embedding(diffusion_step, embed_width):
    half_width = embed_width // 2
    frequency = jnp.exp(-log_base * jnp.arange(half_width, dtype=jnp.float32) / half_width)
    angles = diffusion_step.astype(jnp.float32) * frequency
    return jnp.concatenate([jnp.cos(angles), jnp.sin(angles)])


def flip(x, axis, mask=1):
    count = lax.axis_size(axis)
    return lax.ppermute(x, axis, [(i, i ^ mask) for i in range(count)])


def bits_of(count):
    return [1 << i for i in range(count.bit_length() - 1)]


def params():
    return pltpu.CompilerParams(vmem_limit_bytes=VMEM_BYTES)


def whole(shape):
    return pl.BlockSpec(shape, lambda *_: (0,) * len(shape), pipeline_mode=pl.Buffered(1))


def is_upper(axis, mask):
    return (lax.axis_index(axis) & mask) != 0


def after(x, *others):
    return lax.optimization_barrier((x,) + others)[0]


def ordered(mine, other, upper, axis):
    low = jnp.where(upper, other, mine)
    high = jnp.where(upper, mine, other)
    return jnp.concatenate([low, high], axis=axis)


def gather_temporal(weight, fillers):
    share, wide = weight.shape
    channels = wide // 3
    half = share // 2
    side = lax.axis_index("x") & 1
    x = lax.dynamic_slice(
        weight, (lax.axis_index("core") * half, side * channels), (half, 2 * channels)
    )
    masks = bits_of(lax.axis_size("dp"))[::-1]
    x = x.reshape((1,) * len(masks) + x.shape)
    for spot, mask in enumerate(masks):
        got = flip(x, "dp", mask)
        if mask == 1:
            got = after(got, fillers[0](x))
        x = ordered(x, got, is_upper("dp", mask), spot)
    upper = side != 0
    low, high = x[..., :channels], x[..., channels:]
    outer = jnp.where(upper, high, low)
    other = after(flip(outer, "x", 1), fillers[1](outer))
    x = jnp.concatenate(
        [jnp.where(upper, other, low), jnp.where(upper, low, high), jnp.where(upper, high, other)],
        axis=-1,
    )
    x = ordered(x, flip(x, "core"), is_upper("core", 1), x.ndim - 2)
    return x.reshape(share * lax.axis_size("dp"), wide)


class Chain:
    def __init__(self, keep, send):
        shards, taps, half, cols = keep.shape
        dp_masks = bits_of(shards)[::-1]
        x_masks = bits_of(lax.axis_size("x"))[::-1]
        nd, nx = len(dp_masks), len(x_masks)
        shape = (2,) * (nd + nx) + (taps >> nx, half, cols)
        self.got = flip(send, "core").reshape(shape)
        self.keep = keep.reshape(shape)
        self.stages = [("x", m, nd + i) for i, m in list(enumerate(x_masks))[::-1]]
        self.stages += [("dp", m, i) for i, m in list(enumerate(dp_masks))[::-1]]

    def launch(self):
        axis, mask, spot = self.stages.pop(0)
        bit = is_upper(axis, mask).astype(jnp.int32)

        def pick(which):
            kept = lax.dynamic_index_in_dim(self.keep, which, spot)
            return kept + lax.dynamic_index_in_dim(self.got, which, spot).astype(f32)

        other = pick(1 - bit).astype(bf16)
        self.keep, self.got = pick(bit), flip(other, axis, mask)
        return other

    def land(self, token):
        self.keep, self.got = lax.optimization_barrier((self.keep, self.got, token))[:2]

    def finish(self):
        while self.stages:
            self.launch()
        x = self.keep + self.got.astype(f32)
        return x.reshape(x.shape[-3:])


def join_x(x, token=None):
    for mask in bits_of(lax.axis_size("x")):
        got = flip(x, "x", mask)
        if token is not None:
            x, got = lax.optimization_barrier((x, got, token))[:2]
        x = ordered(x, got, is_upper("x", mask), 1)
    return x


def join_core(x):
    return ordered(x, flip(x, "core"), is_upper("core", 1), 2)


def matmul_nt(a, b):
    return lax.dot_general(a, b, (((1,), (1,)), ((), ())), preferred_element_type=f32)


def matmul_tn(a, b):
    return lax.dot_general(a, b, (((0,), (0,)), ((), ())), preferred_element_type=f32)


def matmul(a, b):
    return jnp.dot(a, b, preferred_element_type=f32)


def group_mean(sums, same_ref, count):
    filled = -(-len(sums) // 8) * 8
    padded = jnp.concatenate(sums + [sums[0]] * (filled - len(sums)), axis=0)
    total = jnp.dot(
        padded, same_ref[...], precision=lax.Precision.HIGHEST, preferred_element_type=f32
    )
    return total * (1.0 / count)


def write_views(ref, frame, values, breadth):
    pixels, channels = values.shape
    height = pixels // breadth
    column = lax.broadcasted_iota(jnp.int32, (pixels, channels), 0) & (breadth - 1)
    left = jnp.where(column == 0, 0.0, pltpu.roll(values, 1, 0))
    right = jnp.where(column == breadth - 1, 0.0, pltpu.roll(values, pixels - 1, 0))
    edge = jnp.zeros((1, breadth, 3 * channels), bf16)
    ref[frame, 0:1] = edge
    ref[frame, height + 1 : height + 2] = edge
    for s, moved in enumerate((left, values, right)):
        ref[frame, 1 : height + 1, :, s * channels : (s + 1) * channels] = moved.astype(
            bf16
        ).reshape(height, breadth, channels)


def rows_of(views_ref, r):
    frames, high, breadth, wide = views_ref.shape
    return views_ref[:, pl.ds(r, high - 2)].reshape(frames * (high - 2) * breadth, wide)


def norm_kernel(count, breadth, x_ref, same_ref, views_ref, mean_ref, scale_ref):
    frames = range(x_ref.shape[0])
    sums = [jnp.sum(x_ref[f].astype(f32), axis=0, keepdims=True) for f in frames]
    centers = group_mean(sums, same_ref, count)
    squares = []
    for f in frames:
        deviation = x_ref[f].astype(f32) - centers[f : f + 1]
        squares.append(jnp.sum(deviation * deviation, axis=0, keepdims=True))
    scales = lax.rsqrt(group_mean(squares, same_ref, count) + epsilon)
    for f in frames:
        center, scaled = centers[f : f + 1], scales[f : f + 1]
        normal = (x_ref[f].astype(f32) - center) * scaled
        mean_ref[f] = center
        scale_ref[f] = scaled
        write_views(views_ref, f, normal / (1.0 + jnp.exp(-normal)), breadth)


def normalize(frames, same, breadth):
    count, pixels, channels = frames.shape
    height = pixels // breadth
    return pl.pallas_call(
        lambda *refs: norm_kernel(pixels * (channels // GROUPS), breadth, *refs),
        out_shape=(
            jax.ShapeDtypeStruct((count, height + 2, breadth, 3 * channels), bf16),
            jax.ShapeDtypeStruct((count, 1, channels), f32),
            jax.ShapeDtypeStruct((count, 1, channels), f32),
        ),
        compiler_params=params(),
        name="norm",
    )(frames, same)


def turn_kernel(views_ref, out_ref):
    out_ref[0] = rows_of(views_ref, pl.program_id(0)).T


def turned_columns(views):
    frames, high, breadth, wide = views.shape
    rows = frames * (high - 2) * breadth
    return pl.pallas_call(
        turn_kernel,
        grid=(3,),
        in_specs=[whole(views.shape)],
        out_specs=pl.BlockSpec((1, wide, rows), lambda i: (i, 0, 0)),
        out_shape=jax.ShapeDtypeStruct((3, wide, rows), bf16),
        compiler_params=params(),
        name="turn",
    )(views)


def hidden_grad_kernel(breadth, cot_ref, next_ref, w_ref, back_ref, views_ref, sum_ref):
    outs = cot_ref.shape[0]
    channels = w_ref.shape[0]
    total = jnp.zeros((1, channels), f32)
    for o in range(outs):
        later = cot_ref[o + 1] if o + 1 < outs else next_ref[...]
        even = matmul_nt(cot_ref[o], w_ref[:, channels : 2 * channels])
        odd = matmul_nt(cot_ref[o], w_ref[:, 2 * channels : 3 * channels]) + matmul_nt(
            later, w_ref[:, :channels]
        )
        for frame, values in ((2 * o, even), (2 * o + 1, odd)):
            back_ref[frame] = values.astype(bf16)
            write_views(views_ref, frame, values, breadth)
            total += jnp.sum(values, axis=0, keepdims=True)
    sum_ref[...] = total


def hidden_gradient(cot, following, temporal, breadth):
    outs, pixels, channels = cot.shape
    return pl.pallas_call(
        lambda *refs: hidden_grad_kernel(breadth, *refs),
        out_shape=(
            jax.ShapeDtypeStruct((2 * outs, pixels, channels), bf16),
            jax.ShapeDtypeStruct((2 * outs, pixels // breadth + 2, breadth, 3 * channels), bf16),
            jax.ShapeDtypeStruct((1, channels), f32),
        ),
        compiler_params=params(),
        name="hidden_grad",
    )(cot, following, temporal)


def store_halves(core_ref, grad, keep_ref, send_ref, slot):
    shards, _, half, channels = keep_ref.shape
    grad = grad.reshape(shards, 2 * half, channels)
    low, high = grad[:, :half], grad[:, half:]

    @pl.when(core_ref[0] == 0)
    def _():
        keep_ref[:, slot] = low
        send_ref[:, slot] = high.astype(bf16)

    @pl.when(core_ref[0] != 0)
    def _():
        keep_ref[:, slot] = high
        send_ref[:, slot] = low.astype(bf16)


def weight_grad_kernel(core_ref, x_ref, back_ref, keep_ref, send_ref):
    store_halves(core_ref, matmul(x_ref[0], back_ref[...]), keep_ref, send_ref, 0)


def weight_grad(turned, hidden_back, first, shards, core):
    rows, channels = hidden_back.shape
    half = channels // shards // 2
    out_spec = pl.BlockSpec((shards, 1, half, channels), lambda i: (0, i, 0, 0))
    return pl.pallas_call(
        weight_grad_kernel,
        grid=(4,),
        in_specs=[
            pl.BlockSpec(memory_space=pltpu.SMEM),
            pl.BlockSpec((1, channels, rows), lambda i: (first + i, 0, 0)),
            whole((rows, channels)),
        ],
        out_specs=(out_spec, out_spec),
        out_shape=(
            jax.ShapeDtypeStruct((shards, 4, half, channels), f32),
            jax.ShapeDtypeStruct((shards, 4, half, channels), bf16),
        ),
        compiler_params=params(),
        name="weight_grad",
    )(core, turned, hidden_back)


def last_grad_kernel(
    core_ref, x_ref, back_ref, hidden_ref, before_ref, cot_ref, keep_ref, send_ref
):
    store_halves(core_ref, matmul(x_ref[0], back_ref[...]), keep_ref, send_ref, 0)
    for k in range(3):
        grad = 0.0
        for o in range(cot_ref.shape[0]):
            frame = 2 * o + k - 1
            x = before_ref[...] if frame < 0 else hidden_ref[frame]
            grad += matmul_tn(x, cot_ref[o])
        store_halves(core_ref, grad, keep_ref, send_ref, 1 + k)


def last_grad(turned, hidden_back, hidden, before, cot, shards, core):
    rows, channels = hidden_back.shape
    half = channels // shards // 2
    shape = (shards, 4, half, channels)
    return pl.pallas_call(
        last_grad_kernel,
        grid=(1,),
        in_specs=[
            pl.BlockSpec(memory_space=pltpu.SMEM),
            pl.BlockSpec((1, channels, rows), lambda i: (8, 0, 0)),
            whole((rows, channels)),
            whole(hidden.shape),
            whole(before.shape),
            whole(cot.shape),
        ],
        out_specs=(whole(shape), whole(shape)),
        out_shape=(jax.ShapeDtypeStruct(shape, f32), jax.ShapeDtypeStruct(shape, bf16)),
        compiler_params=params(),
        name="last_grad",
    )(core, turned, hidden_back, hidden, before, cot)


def temporal_kernel(hidden_ref, before_ref, w_ref, out_ref):
    channels = w_ref.shape[0]
    for o in range(out_ref.shape[0]):
        total = 0.0
        for k in range(3):
            frame = 2 * o + k - 1
            x = before_ref[...] if frame < 0 else hidden_ref[frame]
            total += matmul(x, w_ref[:, k * channels : (k + 1) * channels])
        out_ref[o] = total


def temporal_forward(hidden, before, temporal):
    frames, pixels, channels = hidden.shape
    return pl.pallas_call(
        temporal_kernel,
        out_shape=jax.ShapeDtypeStruct((frames // 2, pixels, channels), f32),
        compiler_params=params(),
        name="temporal",
    )(hidden, before, temporal)


def conv_forward_kernel(views_ref, w_ref, shift_ref, out_ref, acc_ref, tall_ref):
    r = pl.program_id(0)
    rows, channels = acc_ref.shape
    for s in range(3):
        tall_ref[s * channels : (s + 1) * channels] = w_ref[:, s * channels : (s + 1) * channels]
    part = matmul(rows_of(views_ref, r), tall_ref[...])

    @pl.when(r == 0)
    def _():
        acc_ref[...] = part + shift_ref[...]

    @pl.when(r == 1)
    def _():
        acc_ref[...] += part

    @pl.when(r == 2)
    def _():
        out_ref[...] = (acc_ref[...] + part).astype(bf16).reshape(out_ref.shape)


def conv_forward(views, spatial, shift):
    frames, high, breadth, wide = views.shape
    channels = wide // 3
    pixels = (high - 2) * breadth
    return pl.pallas_call(
        conv_forward_kernel,
        grid=(3,),
        in_specs=[
            whole(views.shape),
            pl.BlockSpec((channels, wide), lambda i: (0, i)),
            whole((1, channels)),
        ],
        out_specs=whole((frames, pixels, channels)),
        out_shape=jax.ShapeDtypeStruct((frames, pixels, channels), bf16),
        scratch_shapes=[
            pltpu.VMEM((frames * pixels, channels), f32),
            pltpu.VMEM((wide, channels), bf16),
        ],
        compiler_params=params(),
        name="conv_forward",
    )(views, spatial, shift)


def back_part(views_ref, w_ref, r):
    channels = w_ref.shape[0]
    x = rows_of(views_ref, 2 - r)
    x = jnp.concatenate(
        [x[:, (2 - s) * channels : (3 - s) * channels] for s in range(3)], axis=1
    )
    return matmul_nt(x, w_ref[...])


def conv_back_kernel(views_ref, w_ref, acc_ref):
    r = pl.program_id(0)
    part = back_part(views_ref, w_ref, r)

    @pl.when(r == 0)
    def _():
        acc_ref[...] = part

    @pl.when(r != 0)
    def _():
        acc_ref[...] += part


def conv_back_start(views, spatial):
    frames, high, breadth, wide = views.shape
    channels = wide // 3
    rows = frames * (high - 2) * breadth
    return pl.pallas_call(
        conv_back_kernel,
        grid=(2,),
        in_specs=[whole(views.shape), pl.BlockSpec((channels, wide), lambda i: (0, i))],
        out_specs=whole((rows, channels)),
        out_shape=jax.ShapeDtypeStruct((rows, channels), f32),
        compiler_params=params(),
        name="conv_back_start",
    )(views, spatial)


def conv_back_end_kernel(
    count, views_ref, w_ref, part_ref, x_ref, mean_ref, scale_ref, same_ref, out_ref, acc_ref
):
    acc_ref[...] = part_ref[...] + back_part(views_ref, w_ref, 2)
    frames, pixels, _ = x_ref.shape

    def parts(f):
        normal = (x_ref[f].astype(f32) - mean_ref[f]) * scale_ref[f]
        gate = 1.0 / (1.0 + jnp.exp(-normal))
        slope = gate * (1.0 + normal * (1.0 - gate))
        return normal, slope

    sums = []
    for f in range(frames):
        normal, slope = parts(f)
        grad = acc_ref[f * pixels : (f + 1) * pixels] * slope
        acc_ref[f * pixels : (f + 1) * pixels] = grad
        sums.append(jnp.sum(grad, axis=0, keepdims=True))
        sums.append(jnp.sum(grad * normal, axis=0, keepdims=True))
    means = group_mean(sums, same_ref, count)
    for f in range(frames):
        normal = (x_ref[f].astype(f32) - mean_ref[f]) * scale_ref[f]
        one, two = means[2 * f : 2 * f + 1], means[2 * f + 1 : 2 * f + 2]
        grad = acc_ref[f * pixels : (f + 1) * pixels]
        out_ref[f] = (grad - one - normal * two) * scale_ref[f]


def conv_back_end(views, spatial, part, frames, mean, scale, same):
    count, pixels, channels = frames.shape
    return pl.pallas_call(
        lambda *refs: conv_back_end_kernel(pixels * (channels // GROUPS), *refs),
        grid=(1,),
        in_specs=[
            whole(views.shape),
            pl.BlockSpec((channels, 3 * channels), lambda i: (0, 2)),
            whole(part.shape),
            whole(frames.shape),
            whole(mean.shape),
            whole(scale.shape),
            whole(same.shape),
        ],
        out_specs=whole(frames.shape),
        out_shape=jax.ShapeDtypeStruct(frames.shape, f32),
        scratch_shapes=[pltpu.VMEM((count * pixels, channels), f32)],
        compiler_params=params(),
        name="conv_back_end",
    )(views, spatial, part, frames, mean, scale, same)


def neighbours(x_size, step):
    count = 2 * x_size
    return [(i, i + step) for i in range(count) if 0 <= i + step < count]


def body(latents, cotangent, timesteps, spatial_weight, temporal_weight, time_weight):
    clip_frames = latents[0]
    frame_count, height, breadth, channels = clip_frames.shape
    pixels = height * breadth
    out_count = frame_count // 2
    dp = lax.axis_size("dp")
    x_size = lax.axis_size("x")
    share = channels // dp
    half = share // 2
    core = lax.axis_index("core")
    core_scalar = core[None].astype(jnp.int32)
    frames = clip_frames.reshape(frame_count, pixels, channels)

    cot = cotangent[0].reshape(out_count, pixels, channels)
    following = lax.ppermute(cot[0], ("x", "core"), neighbours(x_size, -1))

    spatial = jnp.concatenate([spatial_weight, time_weight], axis=1)
    spatial_mine = lax.dynamic_slice_in_dim(spatial, core * half, half, axis=0)
    spatial_full = lax.all_gather(spatial_mine, ("dp", "core"), axis=0, tiled=True)
    group = lax.broadcasted_iota(jnp.int32, (channels, channels), 0) // (channels // GROUPS)
    same = (group == group.T).astype(f32)
    held = {}

    def activate(token):
        held["views"], held["mean"], held["scale"] = normalize(
            after(frames, token), same, breadth
        )
        return held["mean"]

    def turn(token):
        held["turned"] = turned_columns(after(held["views"], token))
        return held["turned"][0, :8, :128]

    temporal_full = gather_temporal(temporal_weight, (activate, turn))
    views, mean, scale = held["views"], held["mean"], held["scale"]
    turned = held["turned"].reshape(9, channels, frame_count * pixels)

    embedded = embedding(timesteps[0], time_weight.shape[1])
    hidden_back, back_views, shift_sum = hidden_gradient(cot, following, temporal_full, breadth)
    flat_back = hidden_back.reshape(frame_count * pixels, channels)
    sums = shift_sum
    arriving = flip(sums, "core")

    one = weight_grad(turned, flat_back, 0, dp, core_scalar)
    chain_a = Chain(*one)
    sums = sums + after(arriving, one[1])
    out_a = chain_a.launch()
    for mask in bits_of(x_size):
        arriving = flip(sums, "x", mask)
        sums = sums + after(arriving, out_a)
    pairs = jnp.concatenate([sums, embedded[None]], axis=1)
    two = weight_grad(turned, after(flat_back, out_a), 4, dp, core_scalar)
    chain_a.land(two[1])
    chain_b = Chain(*two)
    out_b = chain_b.launch()
    out_a = chain_a.launch()

    time_full = spatial_full[:, 9 * channels :]
    time_shift = jnp.dot(time_full.astype(f32), embedded, precision=lax.Precision.HIGHEST)
    hidden = conv_forward(views, spatial_full, after(time_shift, out_a, out_b)[None])
    chain_a.land(hidden)
    chain_b.land(hidden)
    before = lax.ppermute(hidden[-1], ("x", "core"), neighbours(x_size, 1))
    out_a = chain_a.launch()
    out_b = chain_b.launch()
    for mask in bits_of(dp):
        pairs = jnp.concatenate([pairs, flip(pairs, "dp", mask)], axis=0)
    last = last_grad(
        turned, flat_back, after(hidden, out_a, out_b), before, cot, dp, core_scalar
    )
    chain_a.land(last[1])
    chain_b.land(last[1])
    chain_c = Chain(*last)
    out_c = chain_c.launch()
    out_a = chain_a.launch()
    out_b = chain_b.launch()

    part = conv_back_start(after(back_views, out_a, out_b, out_c), spatial_full)
    chain_a.land(part)
    chain_b.land(part)
    chain_c.land(part)
    out_c = chain_c.launch()
    first = chain_a.finish()
    out_b = chain_b.launch() if chain_b.stages else out_c
    input_grad = conv_back_end(
        after(back_views, out_c, out_b), spatial_full, part, frames, mean, scale, same
    )
    chain_b.land(input_grad)
    chain_c.land(input_grad)
    out_c = chain_c.launch()
    rows = jnp.stack([first, chain_b.finish()])

    downsampled = temporal_forward(after(hidden, out_c, rows), before, temporal_full)
    chain_c.land(downsampled)
    rows = join_x(rows, downsampled)
    last_rows = join_core(join_x(chain_c.finish()[None]))[0]
    rows = join_core(rows)
    downsampled = downsampled.reshape(1, out_count, height, breadth, channels)
    input_grad = input_grad.reshape(1, frame_count, height, breadth, channels)

    mine = lax.dynamic_slice_in_dim(
        pairs[:, :channels], lax.axis_index("dp") * share, share, axis=1
    )
    time_grad = lax.dot_general(
        mine,
        pairs[:, channels:],
        (((0,), (0,)), ((), ())),
        precision=lax.Precision.HIGHEST,
        preferred_element_type=f32,
    )

    spatial_grad = jnp.concatenate(
        [rows[i, j] for i in range(2) for j in range(4)] + [last_rows[0]], axis=1
    )
    temporal_grad = jnp.concatenate([last_rows[1 + k] for k in range(3)], axis=1)
    return (downsampled, input_grad, spatial_grad, temporal_grad, time_grad)


def solution(mesh):
    dp, tm = mesh.devices.shape
    fine = Mesh(mesh.devices.reshape(dp, tm // 2, 2), ("dp", "x", "core"))
    placed = (
        P("dp", ("x", "core"), None, None, None),
        P("dp", ("x", "core"), None, None, None),
        P("dp"),
        P("dp", None),
        P("dp", None),
        P("dp", None),
    )
    return jax.shard_map(
        body,
        mesh=fine,
        in_specs=placed,
        out_specs=(
            P("dp", ("x", "core"), None, None, None),
            P("dp", ("x", "core"), None, None, None),
            P("dp", None),
            P("dp", None),
            P("dp", None),
        ),
        check_vma=False,
    )
```

time: 293 us -> 256 us (0.87)
  waiting for transfers between devices: 119 us -> 61.5 us
  starting transfers between devices: 31 us -> 51.6 us
  Pallas kernels: 97.8 us -> 94.1 us
  other arithmetic: 23.2 us -> 26.3 us
    ppermute x13 -> x29, starting transfers between devices: 20 us -> 48.8 us  [flip(): return lax.ppermute(x, axis, [(i, i ^ mask) for i in range(count)])]
    ppermute x13 -> x29, waiting for transfers between devices: 85.8 us -> 61.5 us  [flip(): return lax.ppermute(x, axis, [(i, i ^ mask) for i in range(count)])]
    all_gather x1 -> x0, waiting for transfers between devices: 23.3 us -> none  [body(): wide_full = lax.all_gather(wide_mine, ('dp', 'core'), axis=0, tiled=True)]
    all_to_all x2 -> x0, waiting for transfers between devices: 8.79 us -> none  [reduce_all(): x = lax.all_to_all(x.astype(bf16), 'dp', 0, 0)]
    all_to_all x2 -> x0, starting transfers between devices: 8.2 us -> none  [reduce_all(): x = lax.all_to_all(x.astype(bf16), 'dp', 0, 0)]
    unnamed x8, other arithmetic: 5.55 us -> 0.13 us
    convert_element_type x4, other arithmetic: 3.57 us -> 7.85 us  [launch(): other = pick(1 - bit).astype(bf16)]
    pallas_call x1, Pallas kernels: 11.4 us -> 7.71 us  [normalize(): pl.pallas_call(lambda *refs: norm_kernel(pixels * (channels // GROUPS), b...]
  transfers between devices with their start and end apart: 19 -> 32, of which waited for: 11 -> 16; matrix products, arithmetic and copies ran while one was open for 8% -> 11% of each run, Pallas kernels for 34% -> 33%
where the time goes in v3:
time: 256 us; the launch traced here: 255 us
  Pallas kernels  94.1 us (37%)
  waiting for transfers between devices  61.5 us (24%)
  starting transfers between devices  51.6 us (20%)
  other arithmetic  26.3 us (10%)
  between operations  15.1 us (6%)
  local copies, waits for them, and re-layouts  4.47 us (2%)
    ppermute x29, waiting for transfers between devices, flip(): return lax.ppermute(x, axis, [(i, i ^ mask) for i in range(count)])  61.5 us
    ppermute x29, starting transfers between devices, flip(): return lax.ppermute(x, axis, [(i, i ^ mask) for i in range(count)])  48.8 us
    pallas_call x2, Pallas kernels, weight_grad(): pl.pallas_call(weight_grad_kernel, grid=(4,), in_specs=[pl.BlockSpec(memo...  16.9 us
    pallas_call x1, Pallas kernels, conv_forward(): pl.pallas_call(conv_forward_kernel, grid=(3,), in_specs=[whole(views.shap...  15.1 us
    pallas_call x1, Pallas kernels, conv_back_end(): pl.pallas_call(lambda *refs: conv_back_end_kernel(pixels * (channels // G...  12.1 us
    pallas_call x1, Pallas kernels, conv_back_start(): pl.pallas_call(conv_back_kernel, grid=(2,), in_specs=[whole(views.shape),...  11.7 us
    pallas_call x1, Pallas kernels, last_grad(): pl.pallas_call(last_grad_kernel, grid=(1,), in_specs=[pl.BlockSpec(memory...  10.4 us
    add x8, other arithmetic, pick(): return kept + lax.dynamic_index_in_dim(self.got, which, spot).astype(f32)  9.69 us
  transfers between devices with their start and end apart: 32, of which 16 were waited for; matrix products, arithmetic and copies ran while one was open for 11% of the time, Pallas kernels for 33%

profile of v3, /device:TPU:0, one launch (start us, length us, event | category | flops | bytes accessed | tf_op | source)
XLA Modules:
  0.0 255.3 jit_solution(8192895236018254932)
XLA Ops:
  7.2 1.9 fusion.1
  9.2 4.1 %collective-permute-start = (bf16[1,1,1,40,1280]{4,3,2,1,0:T(8,128)(2,1)S(1)}, bf16[1,1,1,40,1280]{4,3,2,1,0:T(8,128)(2,1)S(1)}, u32[]{:S(2)}, u32[]{:S(2)}) collective-permute-start(bf16[1,1,1,40,1280]{4,3,2,1,0:T(8,128)(2,1)S(1)} %dynamic-slice_bitcast_fusion), channel_id=1, source_target_pairs={{0,16},{4,20},{8,24},{12,28},{16,0},{20,4},{24,8},{28,12},{1,17},{... | collective-permute-start | bytes 307208 | tf_op jit(solution)/shard_map/ppermute | solution.py:30
  13.3 5.1 %collective-permute-done = bf16[1,1,1,40,1280]{4,3,2,1,0:T(8,128)(2,1)S(1)} collective-permute-done((bf16[1,1,1,40,1280]{4,3,2,1,0:T(8,128)(2,1)S(1)}, bf16[1,1,1,40,1280]{4,3,2,1,0:T(8,128)(2,1)S(1)}, u32[]{:S(2)}, u32[]{:S(2)}) %collective-permute-start) | collective-permute-done | bytes 102432 | tf_op jit(solution)/shard_map/ppermute | solution.py:30
  19.2 6.7 %collective-permute-done.1 = bf16[2,1,1,40,1280]{4,3,2,1,0:T(8,128)(2,1)S(1)} collective-permute-done((bf16[2,1,1,40,1280]{4,3,2,1,0:T(8,128)(2,1)S(1)}, bf16[2,1,1,40,1280]{4,3,2,1,0:T(8,128)(2,1)S(1)}, u32[]{:S(2)}, u32[]{:S(2)}) %collective-permute-start.1) | collective-permute-done | bytes 204832 | tf_op jit(solution)/shard_map/ppermute | solution.py:30
  27.4 1.5 fusion.refs_1_.refs_6_
  28.9 7.7 %norm.1 = (bf16[4,18,16,1920]{3,2,1,0:T(8,128)(2,1)}, f32[4,1,640]{2,1,0:T(1,128)}, f32[4,1,640]{2,1,0:T(1,128)}) custom-call(bf16[4,256,640]{2,1,0:T(8,128)(2,1)} %bitcast.81, f32[640,640]{1,0:T(8,128)} %fusion.refs_1_.refs_6_), custom_call_target="tpu_custom_call" | custom-call | tf_op jit(solution)/shard_map/norm/pallas_call | solution.py:194
  36.6 1.6 collective-permute-done.2
  38.4 1.5 collective-permute-start.4
  39.9 8.9 %collective-permute-done.4 = bf16[2,2,2,40,640]{4,3,2,1,0:T(8,128)(2,1)S(1)} collective-permute-done((bf16[2,2,2,40,640]{4,3,2,1,0:T(8,128)(2,1)S(1)}, bf16[2,2,2,40,640]{4,3,2,1,0:T(8,128)(2,1)S(1)}, u32[]{:S(2)}, u32[]{:S(2)}) %collective-permute-start.4) | collective-permute-done | bytes 409632 | tf_op jit(solution)/shard_map/ppermute | solution.py:30
  50.3 1.5 collective-permute-start.3
  51.8 8.4 %turn.1 = bf16[3,1920,1024]{2,1,0:T(8,128)(2,1)} custom-call(bf16[4,18,16,1920]{3,2,1,0:T(8,128)(2,1)} %get-tuple-element.56.views_ref), custom_call_target="tpu_custom_call" | custom-call | tf_op jit(solution)/shard_map/turn/pallas_call | solution.py:213
  60.6 1.6 pad_maximum_fusion
  62.9 6.6 %hidden_grad.1 = (bf16[4,256,640]{2,1,0:T(8,128)(2,1)}, bf16[4,18,16,1920]{3,2,1,0:T(8,128)(2,1)}, f32[1,640]{1,0:T(1,128)}) custom-call(bf16[2,256,640]{2,1,0:T(8,128)(2,1)} %bitcast.83, bf16[256,640]{1,0:T(8,128)(2,1)} %copy-done.4, bf16[640,1920]{1,0:T(8,128)(2,1)} %bitcast.76), custom_call_target="tpu_custom_call" | custom-call | tf_op jit(solution)/shard_map/hidden_grad/pallas_call | solution.py:243
  69.5 8.4 %weight_grad.2 = (f32[8,4,40,640]{3,2,1,0:T(8,128)}, bf16[8,4,40,640]{3,2,1,0:T(8,128)(2,1)}) custom-call(s32[1]{0:T(128)} %bitcast.4.core_ref, bf16[9,640,1024]{2,1,0:T(8,128)(2,1)} %bitcast.73, bf16[1024,640]{1,0:T(8,128)(2,1)} %bitcast.78), custom_call_target="tpu_custom_call" | custom-call | tf_op jit(solution)/shard_map/weight_grad/pallas_call | solution.py:279
  78.0 1.5 collective-permute-start.6
  79.4 3.4 %collective-permute-done.6 = bf16[8,4,40,640]{3,2,1,0:T(8,128)(2,1)S(1)} collective-permute-done((bf16[8,4,40,640]{3,2,1,0:T(8,128)(2,1)}, bf16[8,4,40,640]{3,2,1,0:T(8,128)(2,1)S(1)}, u32[]{:S(2)}, u32[]{:S(2)}) %collective-permute-start.6) | collective-permute-done | bytes 1638432 | tf_op jit(solution)/shard_map/ppermute | solution.py:30
  82.8 3.3 %add_convert_fusion.2 = (bf16[2,2,2,1,2,40,640]{6,5,4,3,2,1,0:T(8,128)(2,1)}, f32[2,2,2,1,2,40,640]{6,5,4,3,2,1,0:T(8,128)S(1)}) fusion(f32[2,2,2,2,2,40,640]{6,5,4,3,2,1,0:T(8,128)} %bitcast.85, s32[]{:T(128)S(6)} %select_n.232, bf16[2,2,2,2,2,40,640]{6,5,4,3,2,1,0:T(8,128)(2,1)S(1)} %bitcast.89, s32[]{:T(128)S(6)} %select_n.231), kind=kLoop, calls=%fused_computation.19 | loop fusion | flops 2048000 | bytes 7372808 | tf_op jit(solution)/shard_map/convert_element_type | solution.py:106
  86.2 8.4 %weight_grad.3 = (f32[8,4,40,640]{3,2,1,0:T(8,128)}, bf16[8,4,40,640]{3,2,1,0:T(8,128)(2,1)}) custom-call(s32[1]{0:T(128)} %bitcast.4.core_ref, bf16[9,640,1024]{2,1,0:T(8,128)(2,1)} %bitcast.74, bf16[1024,640]{1,0:T(8,128)(2,1)} %bitcast.79), custom_call_target="tpu_custom_call" | custom-call | tf_op jit(solution)/shard_map/weight_grad/pallas_call | solution.py:279
  95.0 1.5 collective-permute-start.7
  96.5 1.9 collective-permute-done.8
  98.3 3.2 %convert_add_fusion.1 = (f32[2,2,2,1,2,40,640]{6,5,4,3,2,1,0:T(8,128)S(1)}, bf16[2,2,2,1,2,40,640]{6,5,4,3,2,1,0:T(8,128)(2,1)}) fusion(f32[2,2,2,2,2,40,640]{6,5,4,3,2,1,0:T(8,128)} %bitcast.87, s32[]{:T(128)S(6)} %select_n.231, bf16[2,2,2,2,2,40,640]{6,5,4,3,2,1,0:T(8,128)(2,1)S(1)} %bitcast.91, s32[]{:T(128)S(6)} %select_n.232), kind=kLoop, calls=%fused_computation.17 | loop fusion | flops 2048000 | bytes 7372808 | tf_op jit(solution)/shard_map/add | solution.py:104
  101.5 1.7 collective-permute-start.10
  103.9 12.5 %collective-permute-done.7 = bf16[2,2,2,1,2,40,640]{6,5,4,3,2,1,0:T(8,128)(2,1)} collective-permute-done((bf16[2,2,2,1,2,40,640]{6,5,4,3,2,1,0:T(8,128)(2,1)}, bf16[2,2,2,1,2,40,640]{6,5,4,3,2,1,0:T(8,128)(2,1)}, u32[]{:S(2)}, u32[]{:S(2)}) %collective-permute-start.7) | collective-permute-done | bytes 819232 | tf_op jit(solution)/shard_map/ppermute | solution.py:30
  116.4 2.4 convert_add_fusion.5
  121.2 15.1 %conv_forward.1.hidden_ref = bf16[4,256,640]{2,1,0:T(8,128)(2,1)} custom-call(bf16[4,18,16,1920]{3,2,1,0:T(8,128)(2,1)} %get-tuple-element.56.views_ref, bf16[640,6016]{1,0:T(8,128)(2,1)} %all-gather.2.cloned.1.call-done.w_ref.refs_1_, f32[1,640]{1,0:T(1,128)} %broadcast_in_dim.10.shift_ref), custom_call_target="tpu_custom_call" | custom-call | tf_op jit(solution)/shard_map/conv_forward/pallas_call | solution.py:377
  139.5 1.8 convert_add_fusion.8
  141.3 2.0 convert_add_fusion.4
  144.0 10.4 %last_grad.1 = (f32[8,4,40,640]{3,2,1,0:T(8,128)}, bf16[8,4,40,640]{3,2,1,0:T(8,128)(2,1)}) custom-call(s32[1]{0:T(128)} %bitcast.4.core_ref, bf16[9,640,1024]{2,1,0:T(8,128)(2,1)} %bitcast.75, bf16[1024,640]{1,0:T(8,128)(2,1)} %bitcast.80, bf16[4,256,640]{2,1,0:T(8,128)(2,1)} %conv_forward.1.hidden_ref, bf16[256,640]{1,0:T(8,128)(2,1)} %copy-done.2, ...), custom_call_target="tpu_custom_call" | custom-call | tf_op jit(solution)/shard_map/last_grad/pallas_call | solution.py:314
  154.5 2.4 collective-permute-start.12
  158.2 1.6 collective-permute-start.14
  160.3 3.2 %add_convert_fusion = (bf16[2,2,2,1,2,40,640]{6,5,4,3,2,1,0:T(8,128)(2,1)}, f32[2,2,2,1,2,40,640]{6,5,4,3,2,1,0:T(8,128)S(1)}) fusion(f32[2,2,2,2,2,40,640]{6,5,4,3,2,1,0:T(8,128)} %bitcast.86, s32[]{:T(128)S(6)} %select_n.232, bf16[2,2,2,2,2,40,640]{6,5,4,3,2,1,0:T(8,128)(2,1)S(1)} %bitcast.90, s32[]{:T(128)S(6)} %select_n.231), kind=kLoop, calls=%fused_computation.15 | loop fusion | flops 2048000 | bytes 7372808 | tf_op jit(solution)/shard_map/convert_element_type | solution.py:106
  163.5 2.1 collective-permute-start.13
  165.5 3.0 %collective-permute-done.15 = bf16[2,2,1,1,2,40,640]{6,5,4,3,2,1,0:T(8,128)(2,1)S(1)} collective-permute-done((bf16[2,2,1,1,2,40,640]{6,5,4,3,2,1,0:T(8,128)(2,1)}, bf16[2,2,1,1,2,40,640]{6,5,4,3,2,1,0:T(8,128)(2,1)S(1)}, u32[]{:S(2)}, u32[]{:S(2)}) %collective-permute-start.15) | collective-permute-done | bytes 409632 | tf_op jit(solution)/shard_map/ppermute | solution.py:30
  169.8 6.6 %collective-permute-start.18 = (bf16[1,1,1,1,2,40,640]{6,5,4,3,2,1,0:T(8,128)(2,1)S(1)}, bf16[1,1,1,1,2,40,640]{6,5,4,3,2,1,0:T(8,128)(2,1)S(1)}, u32[]{:S(2)}, u32[]{:S(2)}) collective-permute-start(bf16[1,1,1,1,2,40,640]{6,5,4,3,2,1,0:T(8,128)(2,1)S(1)} %get-tuple-element.134), channel_id=1, source_target_pairs={{0,16},{4,20},{8,24},{12,28},{16,0},{20,4},{24,8},{28,12},{1,17},{... | collective-permute-start | bytes 307208 | tf_op jit(solution)/shard_map/ppermute | solution.py:30
  177.6 2.2 collective-permute-start.27
  179.8 4.7 %collective-permute-done.27 = f32[1,640]{1,0:T(1,128)S(1)} collective-permute-done((f32[1,640]{1,0:T(1,128)S(1)}, f32[1,640]{1,0:T(1,128)S(1)}, u32[]{:S(2)}, u32[]{:S(2)}) %collective-permute-start.27) | collective-permute-done | bytes 2592 | tf_op jit(solution)/shard_map/ppermute | solution.py:30
  184.4 11.7 %conv_back_start.1.refs_2_ = f32[1024,640]{1,0:T(8,128)} custom-call(bf16[4,18,16,1920]{3,2,1,0:T(8,128)(2,1)} %get-tuple-element.83.views_ref.refs_0_, bf16[640,6016]{1,0:T(8,128)(2,1)} %all-gather.2.cloned.1.call-done.w_ref.refs_1_), custom_call_target="tpu_custom_call" | custom-call | tf_op jit(solution)/shard_map/conv_back_start/pallas_call | solution.py:422
  196.1 5.2 %collective-permute-start.19 = (bf16[1,1,1,1,2,40,640]{6,5,4,3,2,1,0:T(8,128)(2,1)S(1)}, bf16[1,1,1,1,2,40,640]{6,5,4,3,2,1,0:T(8,128)(2,1)S(1)}, u32[]{:S(2)}, u32[]{:S(2)}) collective-permute-start(bf16[1,1,1,1,2,40,640]{6,5,4,3,2,1,0:T(8,128)(2,1)S(1)} %get-tuple-element.136), channel_id=1, source_target_pairs={{0,16},{4,20},{8,24},{12,28},{16,0},{20,4},{24,8},{28,12},{1,17},{... | collective-permute-start | bytes 307208 | tf_op jit(solution)/shard_map/ppermute | solution.py:30
  203.4 12.1 %conv_back_end.1 = f32[4,256,640]{2,1,0:T(8,128)} custom-call(bf16[4,18,16,1920]{3,2,1,0:T(8,128)(2,1)} %get-tuple-element.83.views_ref.refs_0_, bf16[640,6016]{1,0:T(8,128)(2,1)} %all-gather.2.cloned.1.call-done.w_ref.refs_1_, f32[1024,640]{1,0:T(8,128)} %conv_back_start.1.refs_2_, bf16[4,256,640]{2,1,0:T(8,128)(2,1)} %bitcast.82, ...), custom_call_target="tpu_custom_call" | custom-call | tf_op jit(solution)/shard_map/conv_back_end/pallas_call | solution.py:462
  215.5 1.8 collective-permute-start.20
  218.8 2.1 collective-permute-done.28
  221.0 3.4 %collective-permute-start.29 = (f32[2,896]{1,0:T(2,128)S(1)}, f32[2,896]{1,0:T(2,128)S(1)}, u32[]{:S(2)}, u32[]{:S(2)}) collective-permute-start(f32[2,896]{1,0:T(2,128)S(1)} %pad_maximum_fusion.13), channel_id=1, source_target_pairs={{0,8},{4,12},{8,0},{12,4},{16,24},{20,28},{24,16},{28,20},{1,9},{5... | collective-permute-start | bytes 21512 | tf_op jit(solution)/shard_map/ppermute | solution.py:30
  224.3 1.7 collective-permute-done.29
  226.3 2.0 collective-permute-start.22
  228.3 5.2 %temporal.1 = f32[2,256,640]{2,1,0:T(8,128)} custom-call(bf16[4,256,640]{2,1,0:T(8,128)(2,1)} %conv_forward.1.hidden_ref, bf16[256,640]{1,0:T(8,128)(2,1)} %copy-done.2, bf16[640,1920]{1,0:T(8,128)(2,1)} %bitcast.77), custom_call_target="tpu_custom_call" | custom-call | tf_op jit(solution)/shard_map/temporal/pallas_call | solution.py:345
  233.5 3.0 %collective-permute-start.23 = (bf16[1,1,1,1,2,40,640]{6,5,4,3,2,1,0:T(8,128)(2,1)S(1)}, bf16[1,1,1,1,2,40,640]{6,5,4,3,2,1,0:T(8,128)(2,1)S(1)}, u32[]{:S(2)}, u32[]{:S(2)}) collective-permute-start(bf16[1,1,1,1,2,40,640]{6,5,4,3,2,1,0:T(8,128)(2,1)S(1)} %add_convert_fusion.9), channel_id=1, source_target_pairs={{0,16},{4,20},{8,24},{12,28},{16,0},{20,4},{24,8},{28,12},{1,17},{... | collective-permute-start | bytes 307208 | tf_op jit(solution)/shard_map/ppermute | solution.py:30
  236.6 2.5 collective-permute-done.23
  240.7 4.4 %collective-permute-done.24 = f32[1,2,40,640]{3,2,1,0:T(8,128)S(1)} collective-permute-done((f32[1,2,40,640]{3,2,1,0:T(8,128)S(1)}, f32[1,2,40,640]{3,2,1,0:T(8,128)S(1)}, u32[]{:S(2)}, u32[]{:S(2)}) %collective-permute-start.24) | collective-permute-done | bytes 204832 | tf_op jit(solution)/shard_map/ppermute | solution.py:30
  (105 shorter events, 24.9 us)
Async XLA Ops:
  7.2 2.0 copy-start.5
  7.2 112.1 %all-gather.2.cloned.1.call-start = ((), (), s32[]{:S(2)}) async-start(), calls=%async_computation | async-start | bytes 8181760 | tf_op jit(solution)/shard_map/all_gather | solution.py:505
  9.2 9.2 %collective-permute-start = (bf16[1,1,1,40,1280]{4,3,2,1,0:T(8,128)(2,1)S(1)}, bf16[1,1,1,40,1280]{4,3,2,1,0:T(8,128)(2,1)S(1)}, u32[]{:S(2)}, u32[]{:S(2)}) collective-permute-start(bf16[1,1,1,40,1280]{4,3,2,1,0:T(8,128)(2,1)S(1)} %dynamic-slice_bitcast_fusion), channel_id=1, source_target_pairs={{0,16},{4,20},{8,24},{12,28},{16,0},{20,4},{24,8},{28,12},{1,17},{... | collective-permute-start | bytes 307208 | tf_op jit(solution)/shard_map/ppermute | solution.py:30
  18.4 7.5 %collective-permute-start.1 = (bf16[2,1,1,40,1280]{4,3,2,1,0:T(8,128)(2,1)S(1)}, bf16[2,1,1,40,1280]{4,3,2,1,0:T(8,128)(2,1)S(1)}, u32[]{:S(2)}, u32[]{:S(2)}) collective-permute-start(bf16[2,1,1,40,1280]{4,3,2,1,0:T(8,128)(2,1)S(1)} %pad_maximum_fusion.10), channel_id=1, source_target_pairs={{0,8},{4,12},{8,0},{12,4},{16,24},{20,28},{24,16},{28,20},{1,9},{5... | collective-permute-start | bytes 614408 | tf_op jit(solution)/shard_map/ppermute | solution.py:30
  26.0 12.2 %collective-permute-start.2 = (bf16[2,2,1,40,1280]{4,3,2,1,0:T(8,128)(2,1)S(1)}, bf16[2,2,1,40,1280]{4,3,2,1,0:T(8,128)(2,1)S(1)}, u32[]{:S(2)}, u32[]{:S(2)}) collective-permute-start(bf16[2,2,1,40,1280]{4,3,2,1,0:T(8,128)(2,1)S(1)} %pad_maximum_fusion.5), channel_id=1, source_target_pairs={{0,4},{4,0},{8,12},{12,8},{16,20},{20,16},{24,28},{28,24},{1,5},{5... | collective-permute-start | bytes 1228808 | tf_op jit(solution)/shard_map/ppermute | solution.py:30
  38.4 10.4 %collective-permute-start.4 = (bf16[2,2,2,40,640]{4,3,2,1,0:T(8,128)(2,1)S(1)}, bf16[2,2,2,40,640]{4,3,2,1,0:T(8,128)(2,1)S(1)}, u32[]{:S(2)}, u32[]{:S(2)}) collective-permute-start(bf16[2,2,2,40,640]{4,3,2,1,0:T(8,128)(2,1)S(1)} %broadcast_select_fusion.9), channel_id=1, source_target_pairs={{0,2},{2,0},{1,3},{3,1},{4,6},{6,4},{5,7},{7,5},{8,10},{10,8},{9,1... | collective-permute-start | bytes 1228808 | tf_op jit(solution)/shard_map/ppermute | solution.py:30
  49.0 1.3 copy-start
  50.1 10.1 %collective-permute-start.5 = (bf16[2,2,2,40,1920]{4,3,2,1,0:T(8,128)(2,1)}, bf16[2,2,2,40,1920]{4,3,2,1,0:T(8,128)(2,1)S(1)}, u32[]{:S(2)}, u32[]{:S(2)}) collective-permute-start(bf16[2,2,2,40,1920]{4,3,2,1,0:T(8,128)(2,1)} %pad_maximum_fusion.1), channel_id=1, source_target_pairs={{0,1},{1,0},{2,3},{3,2},{4,5},{5,4},{6,7},{7,6},{8,9},{9,8},{10,11... | collective-permute-start | bytes 3686408 | tf_op jit(solution)/shard_map/ppermute | solution.py:30
  50.3 11.9 %collective-permute-start.3 = (bf16[256,640]{1,0:T(8,128)(2,1)S(1)}, bf16[256,640]{1,0:T(8,128)(2,1)S(1)}, u32[]{:S(2)}, u32[]{:S(2)}) collective-permute-start(bf16[256,640]{1,0:T(8,128)(2,1)S(1)} %bitcast.93), channel_id=1, source_target_pairs={{1,0},{2,1},{3,2},{5,4},{6,5},{7,6},{9,8},{10,9},{11,10},{13,12},{... | collective-permute-start | bytes 983048 | tf_op jit(solution)/shard_map/ppermute | solution.py:501
  62.2 0.7 copy-start.4
  78.0 4.9 %collective-permute-start.6 = (bf16[8,4,40,640]{3,2,1,0:T(8,128)(2,1)}, bf16[8,4,40,640]{3,2,1,0:T(8,128)(2,1)S(1)}, u32[]{:S(2)}, u32[]{:S(2)}) collective-permute-start(bf16[8,4,40,640]{3,2,1,0:T(8,128)(2,1)} %get-tuple-element.59), channel_id=1, source_target_pairs={{0,1},{1,0},{2,3},{3,2},{4,5},{5,4},{6,7},{7,6},{8,9},{9,8},{10,11... | collective-permute-start | bytes 4915208 | tf_op jit(solution)/shard_map/ppermute | solution.py:30
  94.6 3.7 %collective-permute-start.8 = (bf16[8,4,40,640]{3,2,1,0:T(8,128)(2,1)}, bf16[8,4,40,640]{3,2,1,0:T(8,128)(2,1)S(1)}, u32[]{:S(2)}, u32[]{:S(2)}) collective-permute-start(bf16[8,4,40,640]{3,2,1,0:T(8,128)(2,1)} %get-tuple-element.61), channel_id=1, source_target_pairs={{0,1},{1,0},{2,3},{3,2},{4,5},{5,4},{6,7},{7,6},{8,9},{9,8},{10,11... | collective-permute-start | bytes 4915208 | tf_op jit(solution)/shard_map/ppermute | solution.py:30
  95.0 21.4 %collective-permute-start.7 = (bf16[2,2,2,1,2,40,640]{6,5,4,3,2,1,0:T(8,128)(2,1)}, bf16[2,2,2,1,2,40,640]{6,5,4,3,2,1,0:T(8,128)(2,1)}, u32[]{:S(2)}, u32[]{:S(2)}) collective-permute-start(bf16[2,2,2,1,2,40,640]{6,5,4,3,2,1,0:T(8,128)(2,1)} %get-tuple-element.103), channel_id=1, source_target_pairs={{0,2},{2,0},{1,3},{3,1},{4,6},{6,4},{5,7},{7,5},{8,10},{10,8},{9,1... | collective-permute-start | bytes 2457608 | tf_op jit(solution)/shard_map/ppermute | solution.py:30
  101.5 37.2 %collective-permute-start.10 = (bf16[2,2,2,1,2,40,640]{6,5,4,3,2,1,0:T(8,128)(2,1)}, bf16[2,2,2,1,2,40,640]{6,5,4,3,2,1,0:T(8,128)(2,1)}, u32[]{:S(2)}, u32[]{:S(2)}) collective-permute-start(bf16[2,2,2,1,2,40,640]{6,5,4,3,2,1,0:T(8,128)(2,1)} %get-tuple-element.102), channel_id=1, source_target_pairs={{0,2},{2,0},{1,3},{3,1},{4,6},{6,4},{5,7},{7,5},{8,10},{10,8},{9,1... | collective-permute-start | bytes 2457608 | tf_op jit(solution)/shard_map/ppermute | solution.py:30
  118.7 20.0 %collective-permute-start.9 = (bf16[2,2,1,1,2,40,640]{6,5,4,3,2,1,0:T(8,128)(2,1)}, bf16[2,2,1,1,2,40,640]{6,5,4,3,2,1,0:T(8,128)(2,1)S(1)}, u32[]{:S(2)}, u32[]{:S(2)}) collective-permute-start(bf16[2,2,1,1,2,40,640]{6,5,4,3,2,1,0:T(8,128)(2,1)} %get-tuple-element.110), channel_id=1, source_target_pairs={{0,4},{4,0},{8,12},{12,8},{16,20},{20,16},{24,28},{28,24},{1,5},{5... | collective-permute-start | bytes 1228808 | tf_op jit(solution)/shard_map/ppermute | solution.py:30
  121.2 18.2 %copy-start.1 = (f32[2,2,1,1,2,40,640]{6,5,4,3,2,1,0:T(8,128)S(1)}, f32[2,2,1,1,2,40,640]{6,5,4,3,2,1,0:T(8,128)}, u32[]{:S(2)}) copy-start(f32[2,2,1,1,2,40,640]{6,5,4,3,2,1,0:T(8,128)} %get-tuple-element.66) | copy-start | bytes 2457604
  137.4 5.9 %collective-permute-start.11 = (bf16[256,640]{1,0:T(8,128)(2,1)S(1)}, bf16[256,640]{1,0:T(8,128)(2,1)S(1)}, u32[]{:S(2)}, u32[]{:S(2)}) collective-permute-start(bf16[256,640]{1,0:T(8,128)(2,1)S(1)} %slice_bitcast_fusion), channel_id=1, source_target_pairs={{0,1},{1,2},{2,3},{4,5},{5,6},{6,7},{8,9},{9,10},{10,11},{12,13},{... | collective-permute-start | bytes 983048 | tf_op jit(solution)/shard_map/ppermute | solution.py:549
  138.7 0.8 copy-start.3
  143.3 0.7 copy-start.2
  154.5 5.8 %collective-permute-start.12 = (bf16[8,4,40,640]{3,2,1,0:T(8,128)(2,1)}, bf16[8,4,40,640]{3,2,1,0:T(8,128)(2,1)S(1)}, u32[]{:S(2)}, u32[]{:S(2)}) collective-permute-start(bf16[8,4,40,640]{3,2,1,0:T(8,128)(2,1)} %get-tuple-element.72), channel_id=1, source_target_pairs={{0,1},{1,0},{2,3},{3,2},{4,5},{5,4},{6,7},{7,6},{8,9},{9,8},{10,11... | collective-permute-start | bytes 4915208 | tf_op jit(solution)/shard_map/ppermute | solution.py:30
  156.9 11.6 %collective-permute-start.15 = (bf16[2,2,1,1,2,40,640]{6,5,4,3,2,1,0:T(8,128)(2,1)}, bf16[2,2,1,1,2,40,640]{6,5,4,3,2,1,0:T(8,128)(2,1)S(1)}, u32[]{:S(2)}, u32[]{:S(2)}) collective-permute-start(bf16[2,2,1,1,2,40,640]{6,5,4,3,2,1,0:T(8,128)(2,1)} %get-tuple-element.108), channel_id=1, source_target_pairs={{0,4},{4,0},{8,12},{12,8},{16,20},{20,16},{24,28},{28,24},{1,5},{5... | collective-permute-start | bytes 1228808 | tf_op jit(solution)/shard_map/ppermute | solution.py:30
  158.2 7.4 %collective-permute-start.14 = (bf16[2,1,1,1,2,40,640]{6,5,4,3,2,1,0:T(8,128)(2,1)}, bf16[2,1,1,1,2,40,640]{6,5,4,3,2,1,0:T(8,128)(2,1)S(1)}, u32[]{:S(2)}, u32[]{:S(2)}) collective-permute-start(bf16[2,1,1,1,2,40,640]{6,5,4,3,2,1,0:T(8,128)(2,1)} %get-tuple-element.120), channel_id=1, source_target_pairs={{0,8},{4,12},{8,0},{12,4},{16,24},{20,28},{24,16},{28,20},{1,9},{5... | collective-permute-start | bytes 614408 | tf_op jit(solution)/shard_map/ppermute | solution.py:30
  163.5 12.9 %copy-start.7 = (f32[1,640]{1,0:T(1,128)S(1)}, f32[1,640]{1,0:T(1,128)}, u32[]{:S(2)}) copy-start(f32[1,640]{1,0:T(1,128)} %get-tuple-element.96) | copy-start | bytes 7684
  163.5 37.9 %collective-permute-start.13 = (bf16[2,2,2,1,2,40,640]{6,5,4,3,2,1,0:T(8,128)(2,1)}, bf16[2,2,2,1,2,40,640]{6,5,4,3,2,1,0:T(8,128)(2,1)}, u32[]{:S(2)}, u32[]{:S(2)}) collective-permute-start(bf16[2,2,2,1,2,40,640]{6,5,4,3,2,1,0:T(8,128)(2,1)} %get-tuple-element.99), channel_id=1, source_target_pairs={{0,2},{2,0},{1,3},{3,1},{4,6},{6,4},{5,7},{7,5},{8,10},{10,8},{9,1... | collective-permute-start | bytes 2457608 | tf_op jit(solution)/shard_map/ppermute | solution.py:30
  168.6 27.5 %collective-permute-start.17 = (bf16[2,1,1,1,2,40,640]{6,5,4,3,2,1,0:T(8,128)(2,1)S(1)}, bf16[2,1,1,1,2,40,640]{6,5,4,3,2,1,0:T(8,128)(2,1)S(1)}, u32[]{:S(2)}, u32[]{:S(2)}) collective-permute-start(bf16[2,1,1,1,2,40,640]{6,5,4,3,2,1,0:T(8,128)(2,1)S(1)} %get-tuple-element.118), channel_id=1, source_target_pairs={{0,8},{4,12},{8,0},{12,4},{16,24},{20,28},{24,16},{28,20},{1,9},{5... | collective-permute-start | bytes 614408 | tf_op jit(solution)/shard_map/ppermute | solution.py:30
  169.8 26.3 %collective-permute-start.18 = (bf16[1,1,1,1,2,40,640]{6,5,4,3,2,1,0:T(8,128)(2,1)S(1)}, bf16[1,1,1,1,2,40,640]{6,5,4,3,2,1,0:T(8,128)(2,1)S(1)}, u32[]{:S(2)}, u32[]{:S(2)}) collective-permute-start(bf16[1,1,1,1,2,40,640]{6,5,4,3,2,1,0:T(8,128)(2,1)S(1)} %get-tuple-element.134), channel_id=1, source_target_pairs={{0,16},{4,20},{8,24},{12,28},{16,0},{20,4},{24,8},{28,12},{1,17},{... | collective-permute-start | bytes 307208 | tf_op jit(solution)/shard_map/ppermute | solution.py:30
  176.4 1.2 collective-permute-start.26
  177.6 6.8 %collective-permute-start.27 = (f32[1,640]{1,0:T(1,128)S(1)}, f32[1,640]{1,0:T(1,128)S(1)}, u32[]{:S(2)}, u32[]{:S(2)}) collective-permute-start(f32[1,640]{1,0:T(1,128)S(1)} %add.212), channel_id=1, source_target_pairs={{0,2},{2,0},{1,3},{3,1},{4,6},{6,4},{5,7},{7,5},{8,10},{10,8},{9,1... | collective-permute-start | bytes 7688 | tf_op jit(solution)/shard_map/ppermute | solution.py:30
  196.1 19.3 %collective-permute-start.19 = (bf16[1,1,1,1,2,40,640]{6,5,4,3,2,1,0:T(8,128)(2,1)S(1)}, bf16[1,1,1,1,2,40,640]{6,5,4,3,2,1,0:T(8,128)(2,1)S(1)}, u32[]{:S(2)}, u32[]{:S(2)}) collective-permute-start(bf16[1,1,1,1,2,40,640]{6,5,4,3,2,1,0:T(8,128)(2,1)S(1)} %get-tuple-element.136), channel_id=1, source_target_pairs={{0,16},{4,20},{8,24},{12,28},{16,0},{20,4},{24,8},{28,12},{1,17},{... | collective-permute-start | bytes 307208 | tf_op jit(solution)/shard_map/ppermute | solution.py:30
  202.7 23.4 %collective-permute-start.16 = (bf16[2,2,1,1,2,40,640]{6,5,4,3,2,1,0:T(8,128)(2,1)S(1)}, bf16[2,2,1,1,2,40,640]{6,5,4,3,2,1,0:T(8,128)(2,1)S(1)}, u32[]{:S(2)}, u32[]{:S(2)}) collective-permute-start(bf16[2,2,1,1,2,40,640]{6,5,4,3,2,1,0:T(8,128)(2,1)S(1)} %get-tuple-element.105), channel_id=1, source_target_pairs={{0,4},{4,0},{8,12},{12,8},{16,20},{20,16},{24,28},{28,24},{1,5},{5... | collective-permute-start | bytes 1228808 | tf_op jit(solution)/shard_map/ppermute | solution.py:30
  215.5 17.9 %collective-permute-start.20 = (f32[2,2,40,640]{3,2,1,0:T(8,128)S(1)}, f32[2,2,40,640]{3,2,1,0:T(8,128)S(1)}, u32[]{:S(2)}, u32[]{:S(2)}) collective-permute-start(f32[2,2,40,640]{3,2,1,0:T(8,128)S(1)} %pad_maximum_fusion.6), channel_id=1, source_target_pairs={{0,2},{2,0},{1,3},{3,1},{4,6},{6,4},{5,7},{7,5},{8,10},{10,8},{9,1... | collective-permute-start | bytes 1228808 | tf_op jit(solution)/shard_map/ppermute | solution.py:30
  217.3 3.6 %collective-permute-start.28 = (f32[1,896]{1,0:T(1,128)S(1)}, f32[1,896]{1,0:T(1,128)S(1)}, u32[]{:S(2)}, u32[]{:S(2)}) collective-permute-start(f32[1,896]{1,0:T(1,128)S(1)} %pad_maximum_fusion.14), channel_id=1, source_target_pairs={{0,4},{4,0},{8,12},{12,8},{16,20},{20,16},{24,28},{28,24},{1,5},{5... | collective-permute-start | bytes 10760 | tf_op jit(solution)/shard_map/ppermute | solution.py:30
  221.0 5.1 %collective-permute-start.29 = (f32[2,896]{1,0:T(2,128)S(1)}, f32[2,896]{1,0:T(2,128)S(1)}, u32[]{:S(2)}, u32[]{:S(2)}) collective-permute-start(f32[2,896]{1,0:T(2,128)S(1)} %pad_maximum_fusion.13), channel_id=1, source_target_pairs={{0,8},{4,12},{8,0},{12,4},{16,24},{20,28},{24,16},{28,20},{1,9},{5... | collective-permute-start | bytes 21512 | tf_op jit(solution)/shard_map/ppermute | solution.py:30
  226.1 13.6 %collective-permute-start.30 = (f32[4,896]{1,0:T(4,128)S(1)}, f32[4,896]{1,0:T(4,128)S(1)}, u32[]{:S(2)}, u32[]{:S(2)}) collective-permute-start(f32[4,896]{1,0:T(4,128)S(1)} %pad_maximum_fusion.12), channel_id=1, source_target_pairs={{0,16},{4,20},{8,24},{12,28},{16,0},{20,4},{24,8},{28,12},{1,17},{... | collective-permute-start | bytes 43016 | tf_op jit(solution)/shard_map/ppermute | solution.py:30
  226.3 7.2 %collective-permute-start.22 = (bf16[2,1,1,1,2,40,640]{6,5,4,3,2,1,0:T(8,128)(2,1)S(1)}, bf16[2,1,1,1,2,40,640]{6,5,4,3,2,1,0:T(8,128)(2,1)S(1)}, u32[]{:S(2)}, u32[]{:S(2)}) collective-permute-start(bf16[2,1,1,1,2,40,640]{6,5,4,3,2,1,0:T(8,128)(2,1)S(1)} %get-tuple-element.116), channel_id=1, source_target_pairs={{0,8},{4,12},{8,0},{12,4},{16,24},{20,28},{24,16},{28,20},{1,9},{5... | collective-permute-start | bytes 614408 | tf_op jit(solution)/shard_map/ppermute | solution.py:30
  233.5 5.6 %collective-permute-start.23 = (bf16[1,1,1,1,2,40,640]{6,5,4,3,2,1,0:T(8,128)(2,1)S(1)}, bf16[1,1,1,1,2,40,640]{6,5,4,3,2,1,0:T(8,128)(2,1)S(1)}, u32[]{:S(2)}, u32[]{:S(2)}) collective-permute-start(bf16[1,1,1,1,2,40,640]{6,5,4,3,2,1,0:T(8,128)(2,1)S(1)} %add_convert_fusion.9), channel_id=1, source_target_pairs={{0,16},{4,20},{8,24},{12,28},{16,0},{20,4},{24,8},{28,12},{1,17},{... | collective-permute-start | bytes 307208 | tf_op jit(solution)/shard_map/ppermute | solution.py:30
  236.6 8.6 %collective-permute-start.21 = (f32[2,4,40,640]{3,2,1,0:T(8,128)S(1)}, f32[2,4,40,640]{3,2,1,0:T(8,128)S(1)}, u32[]{:S(2)}, u32[]{:S(2)}) collective-permute-start(f32[2,4,40,640]{3,2,1,0:T(8,128)S(1)} %pad_maximum_fusion.2), channel_id=1, source_target_pairs={{0,1},{1,0},{2,3},{3,2},{4,5},{5,4},{6,7},{7,6},{8,9},{9,8},{10,11... | collective-permute-start | bytes 2457608 | tf_op jit(solution)/shard_map/ppermute | solution.py:30
  239.2 5.8 %collective-permute-start.24 = (f32[1,2,40,640]{3,2,1,0:T(8,128)S(1)}, f32[1,2,40,640]{3,2,1,0:T(8,128)S(1)}, u32[]{:S(2)}, u32[]{:S(2)}) collective-permute-start(f32[1,2,40,640]{3,2,1,0:T(8,128)S(1)} %add_bitcast_fusion), channel_id=1, source_target_pairs={{0,2},{2,0},{1,3},{3,1},{4,6},{6,4},{5,7},{7,5},{8,10},{10,8},{9,1... | collective-permute-start | bytes 614408 | tf_op jit(solution)/shard_map/ppermute | solution.py:30
  245.1 1.8 collective-permute-start.25
  247.1 1.4 copy-start.6
Sparse Core Ops, SparseCore 0:
  10.8 75.4 all-gather.1

commit v4 on v3

--- a/solution.py
+++ b/solution.py
@@ -36,6 +36,12 @@
 
 def params():
     return pltpu.CompilerParams(vmem_limit_bytes=VMEM_BYTES)
+
+
+def cost(microseconds):
+    return pl.CostEstimate(
+        flops=int(microseconds * 1.15e9), transcendentals=0, bytes_accessed=int(microseconds * 1e5)
+    )
 
 
 def whole(shape):
@@ -95,7 +101,9 @@
         self.stages = [("x", m, nd + i) for i, m in list(enumerate(x_masks))[::-1]]
         self.stages += [("dp", m, i) for i, m in list(enumerate(dp_masks))[::-1]]
 
-    def launch(self):
+    def launch(self, *tokens):
+        if tokens:
+            self.got = after(self.got, *tokens)
         axis, mask, spot = self.stages.pop(0)
         bit = is_upper(axis, mask).astype(jnp.int32)
 
@@ -199,6 +207,7 @@
             jax.ShapeDtypeStruct((count, 1, channels), f32),
         ),
         compiler_params=params(),
+        cost_estimate=cost(7.6),
         name="norm",
     )(frames, same)
 
@@ -217,6 +226,7 @@
         out_specs=pl.BlockSpec((1, wide, rows), lambda i: (i, 0, 0)),
         out_shape=jax.ShapeDtypeStruct((3, wide, rows), bf16),
         compiler_params=params(),
+        cost_estimate=cost(8.5),
         name="turn",
     )(views)
 
@@ -248,6 +258,7 @@
             jax.ShapeDtypeStruct((1, channels), f32),
         ),
         compiler_params=params(),
+        cost_estimate=cost(6.5),
         name="hidden_grad",
     )(cot, following, temporal)
 
@@ -290,6 +301,7 @@
             jax.ShapeDtypeStruct((shards, 4, half, channels), bf16),
         ),
         compiler_params=params(),
+        cost_estimate=cost(8.5),
         name="weight_grad",
     )(core, turned, hidden_back)
 
@@ -325,6 +337,7 @@
         out_specs=(whole(shape), whole(shape)),
         out_shape=(jax.ShapeDtypeStruct(shape, f32), jax.ShapeDtypeStruct(shape, bf16)),
         compiler_params=params(),
+        cost_estimate=cost(10.3),
         name="last_grad",
     )(core, turned, hidden_back, hidden, before, cot)
 
@@ -346,6 +359,7 @@
         temporal_kernel,
         out_shape=jax.ShapeDtypeStruct((frames // 2, pixels, channels), f32),
         compiler_params=params(),
+        cost_estimate=cost(5.2),
         name="temporal",
     )(hidden, before, temporal)
 
@@ -389,6 +403,7 @@
             pltpu.VMEM((wide, channels), bf16),
         ],
         compiler_params=params(),
+        cost_estimate=cost(15),
         name="conv_forward",
     )(views, spatial, shift)
 
@@ -403,16 +418,7 @@
 
 
 def conv_back_kernel(views_ref, w_ref, acc_ref):
-    r = pl.program_id(0)
-    part = back_part(views_ref, w_ref, r)
-
-    @pl.when(r == 0)
-    def _():
-        acc_ref[...] = part
-
-    @pl.when(r != 0)
-    def _():
-        acc_ref[...] += part
+    acc_ref[...] = back_part(views_ref, w_ref, 0)
 
 
 def conv_back_start(views, spatial):
@@ -421,11 +427,12 @@
     rows = frames * (high - 2) * breadth
     return pl.pallas_call(
         conv_back_kernel,
-        grid=(2,),
-        in_specs=[whole(views.shape), pl.BlockSpec((channels, wide), lambda i: (0, i))],
+        grid=(1,),
+        in_specs=[whole(views.shape), pl.BlockSpec((channels, wide), lambda i: (0, 0))],
         out_specs=whole((rows, channels)),
         out_shape=jax.ShapeDtypeStruct((rows, channels), f32),
         compiler_params=params(),
+        cost_estimate=cost(6.5),
         name="conv_back_start",
     )(views, spatial)
 
@@ -433,7 +440,20 @@
 def conv_back_end_kernel(
     count, views_ref, w_ref, part_ref, x_ref, mean_ref, scale_ref, same_ref, out_ref, acc_ref
 ):
-    acc_ref[...] = part_ref[...] + back_part(views_ref, w_ref, 2)
+    step = pl.program_id(0)
+    part = back_part(views_ref, w_ref, 1 + step)
+
+    @pl.when(step == 0)
+    def _():
+        acc_ref[...] = part_ref[...] + part
+
+    @pl.when(step == 1)
+    def _():
+        acc_ref[...] += part
+        back_through_norm(count, x_ref, mean_ref, scale_ref, same_ref, out_ref, acc_ref)
+
+
+def back_through_norm(count, x_ref, mean_ref, scale_ref, same_ref, out_ref, acc_ref):
     frames, pixels, _ = x_ref.shape
 
     def parts(f):
@@ -461,10 +481,10 @@
     count, pixels, channels = frames.shape
     return pl.pallas_call(
         lambda *refs: conv_back_end_kernel(pixels * (channels // GROUPS), *refs),
-        grid=(1,),
+        grid=(2,),
         in_specs=[
             whole(views.shape),
-            pl.BlockSpec((channels, 3 * channels), lambda i: (0, 2)),
+            pl.BlockSpec((channels, 3 * channels), lambda i: (0, 1 + i)),
             whole(part.shape),
             whole(frames.shape),
             whole(mean.shape),
@@ -475,6 +495,7 @@
         out_shape=jax.ShapeDtypeStruct(frames.shape, f32),
         scratch_shapes=[pltpu.VMEM((count * pixels, channels), f32)],
         compiler_params=params(),
+        cost_estimate=cost(18),
         name="conv_back_end",
     )(views, spatial, part, frames, mean, scale, same)
 
@@ -515,7 +536,7 @@
 
     def turn(token):
         held["turned"] = turned_columns(after(held["views"], token))
-        return held["turned"][0, :8, :128]
+        return held["turned"]
 
     temporal_full = gather_temporal(temporal_weight, (activate, turn))
     views, mean, scale = held["views"], held["mean"], held["scale"]
@@ -530,55 +551,64 @@
     one = weight_grad(turned, flat_back, 0, dp, core_scalar)
     chain_a = Chain(*one)
     sums = sums + after(arriving, one[1])
-    out_a = chain_a.launch()
-    for mask in bits_of(x_size):
-        arriving = flip(sums, "x", mask)
-        sums = sums + after(arriving, out_a)
+    arriving = flip(sums, "x", 1)
+    two = weight_grad(turned, after(flat_back, sums), 4, dp, core_scalar)
+    sums = sums + after(arriving, two[1])
+    for mask in bits_of(x_size)[1:]:
+        sums = sums + flip(sums, "x", mask)
     pairs = jnp.concatenate([sums, embedded[None]], axis=1)
-    two = weight_grad(turned, after(flat_back, out_a), 4, dp, core_scalar)
+    steps = bits_of(dp)
+    arriving = flip(pairs, "dp", steps.pop(0))
     chain_a.land(two[1])
     chain_b = Chain(*two)
-    out_b = chain_b.launch()
     out_a = chain_a.launch()
 
     time_full = spatial_full[:, 9 * channels :]
     time_shift = jnp.dot(time_full.astype(f32), embedded, precision=lax.Precision.HIGHEST)
-    hidden = conv_forward(views, spatial_full, after(time_shift, out_a, out_b)[None])
+    hidden = conv_forward(views, spatial_full, after(time_shift, out_a, pairs)[None])
+    pairs = jnp.concatenate([pairs, after(arriving, hidden)], axis=0)
+    arriving = flip(pairs, "dp", steps.pop(0))
     chain_a.land(hidden)
     chain_b.land(hidden)
     before = lax.ppermute(hidden[-1], ("x", "core"), neighbours(x_size, 1))
     out_a = chain_a.launch()
-    out_b = chain_b.launch()
-    for mask in bits_of(dp):
-        pairs = jnp.concatenate([pairs, flip(pairs, "dp", mask)], axis=0)
+    out_b = chain_b.launch(before)
     last = last_grad(
-        turned, flat_back, after(hidden, out_a, out_b), before, cot, dp, core_scalar
-    )
+        turned, flat_back, after(hidden, out_a, out_b, pairs), before, cot, dp, core_scalar
+    )
+    pairs = jnp.concatenate([pairs, after(arriving, last[1])], axis=0)
+    arriving = flip(pairs, "dp", steps.pop(0))
     chain_a.land(last[1])
     chain_b.land(last[1])
     chain_c = Chain(*last)
-    out_c = chain_c.launch()
     out_a = chain_a.launch()
     out_b = chain_b.launch()
 
-    part = conv_back_start(after(back_views, out_a, out_b, out_c), spatial_full)
+    part = conv_back_start(after(back_views, out_a, out_b, pairs), spatial_full)
+    pairs = jnp.concatenate([pairs, after(arriving, part)], axis=0)
+    for mask in steps:
+        pairs = jnp.concatenate([pairs, flip(pairs, "dp", mask)], axis=0)
     chain_a.land(part)
     chain_b.land(part)
     chain_c.land(part)
     out_c = chain_c.launch()
-    first = chain_a.finish()
-    out_b = chain_b.launch() if chain_b.stages else out_c
+    out_a = chain_a.launch()
+    out_b = chain_b.launch()
     input_grad = conv_back_end(
-        after(back_views, out_c, out_b), spatial_full, part, frames, mean, scale, same
-    )
+        after(back_views, out_a, out_b, out_c), spatial_full, part, frames, mean, scale, same
+    )
+    chain_a.land(input_grad)
     chain_b.land(input_grad)
     chain_c.land(input_grad)
     out_c = chain_c.launch()
-    rows = jnp.stack([first, chain_b.finish()])
-
-    downsampled = temporal_forward(after(hidden, out_c, rows), before, temporal_full)
+    first = chain_a.finish()
+    out_b = chain_b.launch()
+
+    downsampled = temporal_forward(after(hidden, first, out_b, out_c), before, temporal_full)
+    chain_b.land(downsampled)
     chain_c.land(downsampled)
-    rows = join_x(rows, downsampled)
+    out_c = chain_c.launch()
+    rows = join_x(jnp.stack([first, chain_b.finish()]))
     last_rows = join_core(join_x(chain_c.finish()[None]))[0]
     rows = join_core(rows)
     downsampled = downsampled.reshape(1, out_count, height, breadth, channels)

time: 256 us -> 230 us (0.90)
  starting transfers between devices: 51.6 us -> 40.6 us
  waiting for transfers between devices: 61.5 us -> 51.6 us
  other arithmetic: 26.3 us -> 20.1 us
    ppermute x29, starting transfers between devices: 48.8 us -> 36.3 us  [flip(): return lax.ppermute(x, axis, [(i, i ^ mask) for i in range(count)])]
    ppermute x29, waiting for transfers between devices: 61.5 us -> 51.6 us  [flip(): return lax.ppermute(x, axis, [(i, i ^ mask) for i in range(count)])]
    convert_element_type x4 -> x5, other arithmetic: 7.85 us -> 3.22 us  [launch(): other = pick(1 - bit).astype(bf16)]
    pallas_call x1, Pallas kernels: 12.1 us -> 16.3 us  [conv_back_end(): pl.pallas_call(lambda *refs: conv_back_end_kernel(pixels * (channels // G...]
    pallas_call x1, Pallas kernels: 11.7 us -> 8.01 us  [conv_back_start(): pl.pallas_call(conv_back_kernel, grid=(1,), in_specs=[whole(views.shape),...]
    add x8 -> x7, other arithmetic: 9.69 us -> 8.1 us  [pick(): return kept + lax.dynamic_index_in_dim(self.got, which, spot).astype(f32)]
  transfers between devices with their start and end apart: 32 -> 32, of which waited for: 16 -> 15; matrix products, arithmetic and copies ran while one was open for 11% -> 8% of each run, Pallas kernels for 33% -> 41%
where the time goes in v4:
time: 230 us; the launch traced here: 229 us
  Pallas kernels  94.7 us (41%)
  waiting for transfers between devices  51.6 us (22%)
  starting transfers between devices  40.6 us (18%)
  other arithmetic  20.1 us (9%)
  between operations  15.1 us (7%)
  local copies, waits for them, and re-layouts  4.95 us (2%)
  matrix products  2.35 us (1%)
    ppermute x29, waiting for transfers between devices, flip(): return lax.ppermute(x, axis, [(i, i ^ mask) for i in range(count)])  51.6 us
    ppermute x29, starting transfers between devices, flip(): return lax.ppermute(x, axis, [(i, i ^ mask) for i in range(count)])  36.3 us
    pallas_call x2, Pallas kernels, weight_grad(): pl.pallas_call(weight_grad_kernel, grid=(4,), in_specs=[pl.BlockSpec(memo...  17.1 us
    pallas_call x1, Pallas kernels, conv_back_end(): pl.pallas_call(lambda *refs: conv_back_end_kernel(pixels * (channels // G...  16.3 us
    pallas_call x1, Pallas kernels, conv_forward(): pl.pallas_call(conv_forward_kernel, grid=(3,), in_specs=[whole(views.shap...  15.1 us
    pallas_call x1, Pallas kernels, last_grad(): pl.pallas_call(last_grad_kernel, grid=(1,), in_specs=[pl.BlockSpec(memory...  10.4 us
    pallas_call x1, Pallas kernels, turned_columns(): pl.pallas_call(turn_kernel, grid=(3,), in_specs=[whole(views.shape)], out...  8.35 us
    add x7, other arithmetic, pick(): return kept + lax.dynamic_index_in_dim(self.got, which, spot).astype(f32)  8.1 us
  transfers between devices with their start and end apart: 32, of which 15 were waited for; matrix products, arithmetic and copies ran while one was open for 8% of the time, Pallas kernels for 41%

profile of v4, /device:TPU:0, one launch (start us, length us, event | category | flops | bytes accessed | tf_op | source)
XLA Modules:
  0.0 229.5 jit_solution(3991929753665783941)
XLA Ops:
  7.2 1.9 fusion.1
  9.2 4.1 %collective-permute-start = (bf16[1,1,1,40,1280]{4,3,2,1,0:T(8,128)(2,1)S(1)}, bf16[1,1,1,40,1280]{4,3,2,1,0:T(8,128)(2,1)S(1)}, u32[]{:S(2)}, u32[]{:S(2)}) collective-permute-start(bf16[1,1,1,40,1280]{4,3,2,1,0:T(8,128)(2,1)S(1)} %dynamic-slice_bitcast_fusion), channel_id=1, source_target_pairs={{0,16},{4,20},{8,24},{12,28},{16,0},{20,4},{24,8},{28,12},{1,17},{... | collective-permute-start | bytes 307208 | tf_op jit(solution)/shard_map/ppermute | solution.py:30
  13.3 5.1 %collective-permute-done = bf16[1,1,1,40,1280]{4,3,2,1,0:T(8,128)(2,1)S(1)} collective-permute-done((bf16[1,1,1,40,1280]{4,3,2,1,0:T(8,128)(2,1)S(1)}, bf16[1,1,1,40,1280]{4,3,2,1,0:T(8,128)(2,1)S(1)}, u32[]{:S(2)}, u32[]{:S(2)}) %collective-permute-start) | collective-permute-done | bytes 102432 | tf_op jit(solution)/shard_map/ppermute | solution.py:30
  19.2 1.5 fusion.refs_1_.refs_6_
  20.7 5.2 %collective-permute-done.1 = bf16[2,1,1,40,1280]{4,3,2,1,0:T(8,128)(2,1)S(1)} collective-permute-done((bf16[2,1,1,40,1280]{4,3,2,1,0:T(8,128)(2,1)S(1)}, bf16[2,1,1,40,1280]{4,3,2,1,0:T(8,128)(2,1)S(1)}, u32[]{:S(2)}, u32[]{:S(2)}) %collective-permute-start.1) | collective-permute-done | bytes 204832 | tf_op jit(solution)/shard_map/ppermute | solution.py:30
  26.0 1.4 collective-permute-start.2
  27.4 7.7 %norm.1 = (bf16[4,18,16,1920]{3,2,1,0:T(8,128)(2,1)}, f32[4,1,640]{2,1,0:T(1,128)}, f32[4,1,640]{2,1,0:T(1,128)}) custom-call(bf16[4,256,640]{2,1,0:T(8,128)(2,1)} %bitcast.88, f32[640,640]{1,0:T(8,128)} %fusion.refs_1_.refs_6_), custom_call_target="tpu_custom_call" | custom-call | flops 8739999744 | bytes 760000 | tf_op jit(solution)/shard_map/norm/pallas_call | solution.py:202
  35.1 3.1 %collective-permute-done.2 = bf16[2,2,1,40,1280]{4,3,2,1,0:T(8,128)(2,1)S(1)} collective-permute-done((bf16[2,2,1,40,1280]{4,3,2,1,0:T(8,128)(2,1)S(1)}, bf16[2,2,1,40,1280]{4,3,2,1,0:T(8,128)(2,1)S(1)}, u32[]{:S(2)}, u32[]{:S(2)}) %collective-permute-start.2) | collective-permute-done | bytes 409632 | tf_op jit(solution)/shard_map/ppermute | solution.py:30
  38.4 1.5 collective-permute-start.4
  39.9 8.4 %turn.1 = bf16[3,1920,1024]{2,1,0:T(8,128)(2,1)} custom-call(bf16[4,18,16,1920]{3,2,1,0:T(8,128)(2,1)} %get-tuple-element.63.views_ref), custom_call_target="tpu_custom_call" | custom-call | flops 9774999552 | bytes 850000 | tf_op jit(solution)/shard_map/turn/pallas_call | solution.py:222
  50.3 1.5 collective-permute-start.3
  51.8 1.5 collective-permute-done.5
  53.7 1.7 pad_maximum_fusion
  56.1 6.7 %hidden_grad.1 = (bf16[4,256,640]{2,1,0:T(8,128)(2,1)}, bf16[4,18,16,1920]{3,2,1,0:T(8,128)(2,1)}, f32[1,640]{1,0:T(1,128)}) custom-call(bf16[2,256,640]{2,1,0:T(8,128)(2,1)} %bitcast.80, bf16[256,640]{1,0:T(8,128)(2,1)} %copy-done.8, bf16[640,1920]{1,0:T(8,128)(2,1)} %bitcast.76), custom_call_target="tpu_custom_call" | custom-call | flops 7474999808 | bytes 650000 | tf_op jit(solution)/shard_map/hidden_grad/pallas_call | solution.py:253
  62.7 8.5 %weight_grad.2 = (f32[8,4,40,640]{3,2,1,0:T(8,128)}, bf16[8,4,40,640]{3,2,1,0:T(8,128)(2,1)}) custom-call(s32[1]{0:T(128)} %bitcast.4.core_ref, bf16[9,640,1024]{2,1,0:T(8,128)(2,1)} %bitcast.90, bf16[1024,640]{1,0:T(8,128)(2,1)} %bitcast.95), custom_call_target="tpu_custom_call" | custom-call | flops 9774999552 | bytes 850000 | tf_op jit(solution)/shard_map/weight_grad/pallas_call | solution.py:290
  71.2 4.2 %collective-permute-start.6 = (bf16[8,4,40,640]{3,2,1,0:T(8,128)(2,1)}, bf16[8,4,40,640]{3,2,1,0:T(8,128)(2,1)}, u32[]{:S(2)}, u32[]{:S(2)}) collective-permute-start(bf16[8,4,40,640]{3,2,1,0:T(8,128)(2,1)} %get-tuple-element.67), channel_id=1, source_target_pairs={{0,1},{1,0},{2,3},{3,2},{4,5},{5,4},{6,7},{7,6},{8,9},{9,8},{10,11... | collective-permute-start | bytes 4915208 | tf_op jit(solution)/shard_map/ppermute | solution.py:30
  76.2 2.4 %collective-permute-done.7 = f32[1,640]{1,0:T(1,128)S(1)} collective-permute-done((f32[1,640]{1,0:T(1,128)S(1)}, f32[1,640]{1,0:T(1,128)S(1)}, u32[]{:S(2)}, u32[]{:S(2)}) %collective-permute-start.7) | collective-permute-done | bytes 2592 | tf_op jit(solution)/shard_map/ppermute | solution.py:30
  78.6 8.6 %weight_grad.3 = (f32[8,4,40,640]{3,2,1,0:T(8,128)}, bf16[8,4,40,640]{3,2,1,0:T(8,128)(2,1)}) custom-call(s32[1]{0:T(128)} %bitcast.4.core_ref, bf16[9,640,1024]{2,1,0:T(8,128)(2,1)} %bitcast.91, bf16[1024,640]{1,0:T(8,128)(2,1)} %bitcast.96), custom_call_target="tpu_custom_call" | custom-call | flops 9774999552 | bytes 850000 | tf_op jit(solution)/shard_map/weight_grad/pallas_call | solution.py:290
  87.7 2.7 %convert_add_fusion.1 = (f32[2,2,2,1,2,40,640]{6,5,4,3,2,1,0:T(8,128)S(1)}, bf16[2,2,2,1,2,40,640]{6,5,4,3,2,1,0:T(8,128)(2,1)}) fusion(f32[2,2,2,2,2,40,640]{6,5,4,3,2,1,0:T(8,128)S(1)} %bitcast.75, s32[]{:T(128)S(6)} %select_n.232, bf16[2,2,2,2,2,40,640]{6,5,4,3,2,1,0:T(8,128)(2,1)} %bitcast.11, s32[]{:T(128)S(6)} %select_n.231), kind=kLoop, calls=%fused_computation.17 | loop fusion | flops 2048000 | bytes 7372808 | tf_op jit(solution)/shard_map/add | solution.py:112
  90.3 1.7 collective-permute-start.12
  92.1 1.4 convolution_reduce_fusion
  94.0 15.1 %conv_forward.1.hidden_ref = bf16[4,256,640]{2,1,0:T(8,128)(2,1)} custom-call(bf16[4,18,16,1920]{3,2,1,0:T(8,128)(2,1)} %get-tuple-element.63.views_ref, bf16[640,6016]{1,0:T(8,128)(2,1)} %all-gather.2.cloned.1.call-done.w_ref.refs_1_, f32[1,640]{1,0:T(1,128)} %broadcast_in_dim.11.shift_ref), custom_call_target="tpu_custom_call" | custom-call | flops 17250000896 | bytes 1500000 | tf_op jit(solution)/shard_map/conv_forward/pallas_call | solution.py:391
  109.1 1.8 slice_bitcast_fusion
  110.8 2.8 %collective-permute-start.10 = (bf16[256,640]{1,0:T(8,128)(2,1)}, bf16[256,640]{1,0:T(8,128)(2,1)}, u32[]{:S(2)}, u32[]{:S(2)}) collective-permute-start(bf16[256,640]{1,0:T(8,128)(2,1)} %slice_bitcast_fusion), channel_id=1, source_target_pairs={{0,1},{1,2},{2,3},{4,5},{5,6},{6,7},{8,9},{9,10},{10,11},{12,13},{... | collective-permute-start | bytes 983048 | tf_op jit(solution)/shard_map/ppermute | solution.py:573
  114.2 3.0 %collective-permute-done.13 = f32[1,896]{1,0:T(1,128)S(1)} collective-permute-done((f32[1,896]{1,0:T(1,128)S(1)}, f32[1,896]{1,0:T(1,128)S(1)}, u32[]{:S(2)}, u32[]{:S(2)}) %collective-permute-start.13) | collective-permute-done | bytes 3616 | tf_op jit(solution)/shard_map/ppermute | solution.py:30
  117.3 1.2 copy-done.3
  118.5 2.2 convert_add_fusion.4
  120.7 2.8 %add_convert_fusion.1 = (bf16[2,2,2,1,2,40,640]{6,5,4,3,2,1,0:T(8,128)(2,1)}, f32[2,2,2,1,2,40,640]{6,5,4,3,2,1,0:T(8,128)S(1)}) fusion(f32[2,2,2,2,2,40,640]{6,5,4,3,2,1,0:T(8,128)S(1)} %bitcast.74, s32[]{:T(128)S(6)} %select_n.231, bf16[2,2,2,2,2,40,640]{6,5,4,3,2,1,0:T(8,128)(2,1)} %bitcast.78, s32[]{:T(128)S(6)} %select_n.232), kind=kLoop, calls=%fused_computation.18 | loop fusion | flops 2048000 | bytes 7372808 | tf_op jit(solution)/shard_map/convert_element_type | solution.py:114
  123.5 10.4 %last_grad.1 = (f32[8,4,40,640]{3,2,1,0:T(8,128)}, bf16[8,4,40,640]{3,2,1,0:T(8,128)(2,1)}) custom-call(s32[1]{0:T(128)} %bitcast.4.core_ref, bf16[9,640,1024]{2,1,0:T(8,128)(2,1)} %bitcast.92, bf16[1024,640]{1,0:T(8,128)(2,1)} %bitcast.97, bf16[4,256,640]{2,1,0:T(8,128)(2,1)} %conv_forward.1.hidden_ref, ...), custom_call_target="tpu_custom_call" | custom-call | flops 11845000192 | bytes 1030000 | tf_op jit(solution)/shard_map/last_grad/pallas_call | solution.py:326
  135.5 2.5 %collective-permute-done.16 = f32[2,896]{1,0:T(2,128)S(1)} collective-permute-done((f32[2,896]{1,0:T(2,128)S(1)}, f32[2,896]{1,0:T(2,128)S(1)}, u32[]{:S(2)}, u32[]{:S(2)}) %collective-permute-start.16) | collective-permute-done | bytes 7200 | tf_op jit(solution)/shard_map/ppermute | solution.py:30
  138.1 8.0 %collective-permute-done.15 = bf16[2,2,1,1,2,40,640]{6,5,4,3,2,1,0:T(8,128)(2,1)} collective-permute-done((bf16[2,2,1,1,2,40,640]{6,5,4,3,2,1,0:T(8,128)(2,1)}, bf16[2,2,1,1,2,40,640]{6,5,4,3,2,1,0:T(8,128)(2,1)}, u32[]{:S(2)}, u32[]{:S(2)}) %collective-permute-start.15) | collective-permute-done | bytes 409632 | tf_op jit(solution)/shard_map/ppermute | solution.py:30
  147.2 1.7 collective-permute-start.18
  149.4 8.0 %conv_back_start.1.refs_2_ = f32[1024,640]{1,0:T(8,128)} custom-call(bf16[4,18,16,1920]{3,2,1,0:T(8,128)(2,1)} %get-tuple-element.99.views_ref.refs_0_, bf16[640,6016]{1,0:T(8,128)(2,1)} %all-gather.2.cloned.1.call-done.w_ref.refs_1_), custom_call_target="tpu_custom_call" | custom-call | flops 7474999808 | bytes 650000 | tf_op jit(solution)/shard_map/conv_back_start/pallas_call | solution.py:428
  157.5 7.2 %collective-permute-start.21 = (bf16[1,1,1,1,2,40,640]{6,5,4,3,2,1,0:T(8,128)(2,1)S(1)}, bf16[1,1,1,1,2,40,640]{6,5,4,3,2,1,0:T(8,128)(2,1)S(1)}, u32[]{:S(2)}, u32[]{:S(2)}) collective-permute-start(bf16[1,1,1,1,2,40,640]{6,5,4,3,2,1,0:T(8,128)(2,1)S(1)} %get-tuple-element.148), channel_id=1, source_target_pairs={{0,16},{4,20},{8,24},{12,28},{16,0},{20,4},{24,8},{28,12},{1,17},{... | collective-permute-start | bytes 307208 | tf_op jit(solution)/shard_map/ppermute | solution.py:30
  164.9 1.8 convert_add_fusion
  166.7 2.1 collective-permute-start.20
  168.8 16.3 %conv_back_end.1 = f32[4,256,640]{2,1,0:T(8,128)} custom-call(bf16[4,18,16,1920]{3,2,1,0:T(8,128)(2,1)} %get-tuple-element.99.views_ref.refs_0_, bf16[640,6016]{1,0:T(8,128)(2,1)} %all-gather.2.cloned.1.call-done.w_ref.refs_1_, f32[1024,640]{1,0:T(8,128)} %conv_back_start.1.refs_2_, bf16[4,256,640]{2,1,0:T(8,128)(2,1)} %bitcast.89, ...), custom_call_target="tpu_custom_call" | custom-call | flops 20700000256 | bytes 1800000 | tf_op jit(solution)/shard_map/conv_back_end/pallas_call | solution.py:482
  185.1 2.4 %collective-permute-start.22 = (bf16[1,1,1,1,2,40,640]{6,5,4,3,2,1,0:T(8,128)(2,1)S(1)}, bf16[1,1,1,1,2,40,640]{6,5,4,3,2,1,0:T(8,128)(2,1)S(1)}, u32[]{:S(2)}, u32[]{:S(2)}) collective-permute-start(bf16[1,1,1,1,2,40,640]{6,5,4,3,2,1,0:T(8,128)(2,1)S(1)} %get-tuple-element.150), channel_id=1, source_target_pairs={{0,16},{4,20},{8,24},{12,28},{16,0},{20,4},{24,8},{28,12},{1,17},{... | collective-permute-start | bytes 307208 | tf_op jit(solution)/shard_map/ppermute | solution.py:30
  188.4 5.2 %temporal.1 = f32[2,256,640]{2,1,0:T(8,128)} custom-call(bf16[4,256,640]{2,1,0:T(8,128)(2,1)} %conv_forward.1.hidden_ref, bf16[256,640]{1,0:T(8,128)(2,1)} %collective-permute-done.10.before_ref, bf16[640,1920]{1,0:T(8,128)(2,1)} %bitcast.77), custom_call_target="tpu_custom_call" | custom-call | flops 5980000256 | bytes 520000 | tf_op jit(solution)/shard_map/temporal/pallas_call | solution.py:358
  193.6 1.2 collective-permute-start.23
  194.8 1.2 collective-permute-start.30
  196.0 3.6 %collective-permute-done.30 = f32[4,896]{1,0:T(4,128)S(1)} collective-permute-done((f32[4,896]{1,0:T(4,128)S(1)}, f32[4,896]{1,0:T(4,128)S(1)}, u32[]{:S(2)}, u32[]{:S(2)}) %collective-permute-start.30) | collective-permute-done | bytes 14368 | tf_op jit(solution)/shard_map/ppermute | solution.py:30
  199.6 1.9 collective-permute-start.26
  201.5 1.3 collective-permute-done.23
  202.9 3.7 %collective-permute-done.26 = bf16[2,1,1,1,2,40,640]{6,5,4,3,2,1,0:T(8,128)(2,1)S(1)} collective-permute-done((bf16[2,1,1,1,2,40,640]{6,5,4,3,2,1,0:T(8,128)(2,1)S(1)}, bf16[2,1,1,1,2,40,640]{6,5,4,3,2,1,0:T(8,128)(2,1)S(1)}, u32[]{:S(2)}, u32[]{:S(2)}) %collective-permute-start.26) | collective-permute-done | bytes 204832 | tf_op jit(solution)/shard_map/ppermute | solution.py:30
  207.6 5.7 %collective-permute-done.27 = bf16[1,1,1,1,2,40,640]{6,5,4,3,2,1,0:T(8,128)(2,1)S(1)} collective-permute-done((bf16[1,1,1,1,2,40,640]{6,5,4,3,2,1,0:T(8,128)(2,1)S(1)}, bf16[1,1,1,1,2,40,640]{6,5,4,3,2,1,0:T(8,128)(2,1)S(1)}, u32[]{:S(2)}, u32[]{:S(2)}) %collective-permute-start.27) | collective-permute-done | bytes 102432 | tf_op jit(solution)/shard_map/ppermute | solution.py:30
  214.5 4.7 %collective-permute-done.28 = f32[1,2,40,640]{3,2,1,0:T(8,128)S(1)} collective-permute-done((f32[1,2,40,640]{3,2,1,0:T(8,128)S(1)}, f32[1,2,40,640]{3,2,1,0:T(8,128)S(1)}, u32[]{:S(2)}, u32[]{:S(2)}) %collective-permute-start.28) | collective-permute-done | bytes 204832 | tf_op jit(solution)/shard_map/ppermute | solution.py:30
  219.6 1.4 collective-permute-done.29
  (107 shorter events, 14.9 us)
Async XLA Ops:
  7.2 2.0 copy-start.5
  7.2 84.9 %all-gather.2.cloned.1.call-start = ((), (), s32[]{:S(2)}) async-start(), calls=%async_computation | async-start | bytes 8181760 | tf_op jit(solution)/shard_map/all_gather | solution.py:526
  9.2 9.2 %collective-permute-start = (bf16[1,1,1,40,1280]{4,3,2,1,0:T(8,128)(2,1)S(1)}, bf16[1,1,1,40,1280]{4,3,2,1,0:T(8,128)(2,1)S(1)}, u32[]{:S(2)}, u32[]{:S(2)}) collective-permute-start(bf16[1,1,1,40,1280]{4,3,2,1,0:T(8,128)(2,1)S(1)} %dynamic-slice_bitcast_fusion), channel_id=1, source_target_pairs={{0,16},{4,20},{8,24},{12,28},{16,0},{20,4},{24,8},{28,12},{1,17},{... | collective-permute-start | bytes 307208 | tf_op jit(solution)/shard_map/ppermute | solution.py:30
  18.4 7.5 %collective-permute-start.1 = (bf16[2,1,1,40,1280]{4,3,2,1,0:T(8,128)(2,1)S(1)}, bf16[2,1,1,40,1280]{4,3,2,1,0:T(8,128)(2,1)S(1)}, u32[]{:S(2)}, u32[]{:S(2)}) collective-permute-start(bf16[2,1,1,40,1280]{4,3,2,1,0:T(8,128)(2,1)S(1)} %pad_maximum_fusion.10), channel_id=1, source_target_pairs={{0,8},{4,12},{8,0},{12,4},{16,24},{20,28},{24,16},{28,20},{1,9},{5... | collective-permute-start | bytes 614408 | tf_op jit(solution)/shard_map/ppermute | solution.py:30
  26.0 12.2 %collective-permute-start.2 = (bf16[2,2,1,40,1280]{4,3,2,1,0:T(8,128)(2,1)S(1)}, bf16[2,2,1,40,1280]{4,3,2,1,0:T(8,128)(2,1)S(1)}, u32[]{:S(2)}, u32[]{:S(2)}) collective-permute-start(bf16[2,2,1,40,1280]{4,3,2,1,0:T(8,128)(2,1)S(1)} %pad_maximum_fusion.5), channel_id=1, source_target_pairs={{0,4},{4,0},{8,12},{12,8},{16,20},{20,16},{24,28},{28,24},{1,5},{5... | collective-permute-start | bytes 1228808 | tf_op jit(solution)/shard_map/ppermute | solution.py:30
  38.4 10.4 %collective-permute-start.4 = (bf16[2,2,2,40,640]{4,3,2,1,0:T(8,128)(2,1)S(1)}, bf16[2,2,2,40,640]{4,3,2,1,0:T(8,128)(2,1)S(1)}, u32[]{:S(2)}, u32[]{:S(2)}) collective-permute-start(bf16[2,2,2,40,640]{4,3,2,1,0:T(8,128)(2,1)S(1)} %broadcast_select_fusion.9), channel_id=1, source_target_pairs={{0,2},{2,0},{1,3},{3,1},{4,6},{6,4},{5,7},{7,5},{8,10},{10,8},{9,1... | collective-permute-start | bytes 1228808 | tf_op jit(solution)/shard_map/ppermute | solution.py:30
  49.0 1.3 copy-start.4
  50.1 3.1 %collective-permute-start.5 = (bf16[2,2,2,40,1920]{4,3,2,1,0:T(8,128)(2,1)}, bf16[2,2,2,40,1920]{4,3,2,1,0:T(8,128)(2,1)S(1)}, u32[]{:S(2)}, u32[]{:S(2)}) collective-permute-start(bf16[2,2,2,40,1920]{4,3,2,1,0:T(8,128)(2,1)} %pad_maximum_fusion.1), channel_id=1, source_target_pairs={{0,1},{1,0},{2,3},{3,2},{4,5},{5,4},{6,7},{7,6},{8,9},{9,8},{10,11... | collective-permute-start | bytes 3686408 | tf_op jit(solution)/shard_map/ppermute | solution.py:30
  50.3 5.0 %collective-permute-start.3 = (bf16[256,640]{1,0:T(8,128)(2,1)S(1)}, bf16[256,640]{1,0:T(8,128)(2,1)S(1)}, u32[]{:S(2)}, u32[]{:S(2)}) collective-permute-start(bf16[256,640]{1,0:T(8,128)(2,1)S(1)} %bitcast.79), channel_id=1, source_target_pairs={{1,0},{2,1},{3,2},{5,4},{6,5},{7,6},{9,8},{10,9},{11,10},{13,12},{... | collective-permute-start | bytes 983048 | tf_op jit(solution)/shard_map/ppermute | solution.py:522
  55.3 0.7 copy-start.8
  62.7 13.4 %copy-start.7 = (f32[1,640]{1,0:T(1,128)S(1)}, f32[1,640]{1,0:T(1,128)}, u32[]{:S(2)}) copy-start(f32[1,640]{1,0:T(1,128)} %get-tuple-element.68) | copy-start | bytes 7684
  71.2 16.4 %collective-permute-start.6 = (bf16[8,4,40,640]{3,2,1,0:T(8,128)(2,1)}, bf16[8,4,40,640]{3,2,1,0:T(8,128)(2,1)}, u32[]{:S(2)}, u32[]{:S(2)}) collective-permute-start(bf16[8,4,40,640]{3,2,1,0:T(8,128)(2,1)} %get-tuple-element.67), channel_id=1, source_target_pairs={{0,1},{1,0},{2,3},{3,2},{4,5},{5,4},{6,7},{7,6},{8,9},{9,8},{10,11... | collective-permute-start | bytes 4915208 | tf_op jit(solution)/shard_map/ppermute | solution.py:30
  76.1 2.5 %collective-permute-start.7 = (f32[1,640]{1,0:T(1,128)S(1)}, f32[1,640]{1,0:T(1,128)S(1)}, u32[]{:S(2)}, u32[]{:S(2)}) collective-permute-start(f32[1,640]{1,0:T(1,128)S(1)} %copy-done.7), channel_id=1, source_target_pairs={{0,1},{1,0},{2,3},{3,2},{4,5},{5,4},{6,7},{7,6},{8,9},{9,8},{10,11... | collective-permute-start | bytes 7688 | tf_op jit(solution)/shard_map/ppermute | solution.py:30
  78.6 9.0 %collective-permute-start.8 = (f32[1,640]{1,0:T(1,128)S(1)}, f32[1,640]{1,0:T(1,128)S(1)}, u32[]{:S(2)}, u32[]{:S(2)}) collective-permute-start(f32[1,640]{1,0:T(1,128)S(1)} %add.177), channel_id=1, source_target_pairs={{0,2},{2,0},{1,3},{3,1},{4,6},{6,4},{5,7},{7,5},{8,10},{10,8},{9,1... | collective-permute-start | bytes 7688 | tf_op jit(solution)/shard_map/ppermute | solution.py:30
  78.6 9.0 %copy-start.2 = (f32[8,4,40,640]{3,2,1,0:T(8,128)S(1)}, f32[8,4,40,640]{3,2,1,0:T(8,128)}, u32[]{:S(2)}) copy-start(f32[8,4,40,640]{3,2,1,0:T(8,128)} %get-tuple-element.66) | copy-start | bytes 9830404
  87.3 30.0 %collective-permute-start.9 = (bf16[8,4,40,640]{3,2,1,0:T(8,128)(2,1)}, bf16[8,4,40,640]{3,2,1,0:T(8,128)(2,1)S(1)}, u32[]{:S(2)}, u32[]{:S(2)}) collective-permute-start(bf16[8,4,40,640]{3,2,1,0:T(8,128)(2,1)} %get-tuple-element.71), channel_id=1, source_target_pairs={{0,1},{1,0},{2,3},{3,2},{4,5},{5,4},{6,7},{7,6},{8,9},{9,8},{10,11... | collective-permute-start | bytes 4915208 | tf_op jit(solution)/shard_map/ppermute | solution.py:30
  90.3 26.9 %collective-permute-start.12 = (bf16[2,2,2,1,2,40,640]{6,5,4,3,2,1,0:T(8,128)(2,1)}, bf16[2,2,2,1,2,40,640]{6,5,4,3,2,1,0:T(8,128)(2,1)}, u32[]{:S(2)}, u32[]{:S(2)}) collective-permute-start(bf16[2,2,2,1,2,40,640]{6,5,4,3,2,1,0:T(8,128)(2,1)} %get-tuple-element.116), channel_id=1, source_target_pairs={{0,2},{2,0},{1,3},{3,1},{4,6},{6,4},{5,7},{7,5},{8,10},{10,8},{9,1... | collective-permute-start | bytes 2457608 | tf_op jit(solution)/shard_map/ppermute | solution.py:30
  110.8 9.8 %collective-permute-start.10 = (bf16[256,640]{1,0:T(8,128)(2,1)}, bf16[256,640]{1,0:T(8,128)(2,1)}, u32[]{:S(2)}, u32[]{:S(2)}) collective-permute-start(bf16[256,640]{1,0:T(8,128)(2,1)} %slice_bitcast_fusion), channel_id=1, source_target_pairs={{0,1},{1,2},{2,3},{4,5},{5,6},{6,7},{8,9},{9,10},{10,11},{12,13},{... | collective-permute-start | bytes 983048 | tf_op jit(solution)/shard_map/ppermute | solution.py:573
  113.7 3.6 %collective-permute-start.13 = (f32[1,896]{1,0:T(1,128)S(1)}, f32[1,896]{1,0:T(1,128)S(1)}, u32[]{:S(2)}, u32[]{:S(2)}) collective-permute-start(f32[1,896]{1,0:T(1,128)S(1)} %pad_maximum_fusion.14), channel_id=1, source_target_pairs={{0,4},{4,0},{8,12},{12,8},{16,20},{20,16},{24,28},{28,24},{1,5},{5... | collective-permute-start | bytes 10760 | tf_op jit(solution)/shard_map/ppermute | solution.py:30
  117.3 1.2 copy-start.3
  118.4 2.2 copy-start.1
  123.5 25.4 %collective-permute-start.11 = (bf16[2,2,2,1,2,40,640]{6,5,4,3,2,1,0:T(8,128)(2,1)}, bf16[2,2,2,1,2,40,640]{6,5,4,3,2,1,0:T(8,128)(2,1)S(1)}, u32[]{:S(2)}, u32[]{:S(2)}) collective-permute-start(bf16[2,2,2,1,2,40,640]{6,5,4,3,2,1,0:T(8,128)(2,1)} %get-tuple-element.117), channel_id=1, source_target_pairs={{0,2},{2,0},{1,3},{3,1},{4,6},{6,4},{5,7},{7,5},{8,10},{10,8},{9,1... | collective-permute-start | bytes 2457608 | tf_op jit(solution)/shard_map/ppermute | solution.py:30
  133.8 31.0 %collective-permute-start.19 = (bf16[8,4,40,640]{3,2,1,0:T(8,128)(2,1)}, bf16[8,4,40,640]{3,2,1,0:T(8,128)(2,1)}, u32[]{:S(2)}, u32[]{:S(2)}) collective-permute-start(bf16[8,4,40,640]{3,2,1,0:T(8,128)(2,1)} %get-tuple-element.84), channel_id=1, source_target_pairs={{0,1},{1,0},{2,3},{3,2},{4,5},{5,4},{6,7},{7,6},{8,9},{9,8},{10,11... | collective-permute-start | bytes 4915208 | tf_op jit(solution)/shard_map/ppermute | solution.py:30
  133.8 12.2 %collective-permute-start.15 = (bf16[2,2,1,1,2,40,640]{6,5,4,3,2,1,0:T(8,128)(2,1)}, bf16[2,2,1,1,2,40,640]{6,5,4,3,2,1,0:T(8,128)(2,1)}, u32[]{:S(2)}, u32[]{:S(2)}) collective-permute-start(bf16[2,2,1,1,2,40,640]{6,5,4,3,2,1,0:T(8,128)(2,1)} %get-tuple-element.122), channel_id=1, source_target_pairs={{0,4},{4,0},{8,12},{12,8},{16,20},{20,16},{24,28},{28,24},{1,5},{5... | collective-permute-start | bytes 1228808 | tf_op jit(solution)/shard_map/ppermute | solution.py:30
  134.4 3.6 %collective-permute-start.16 = (f32[2,896]{1,0:T(2,128)S(1)}, f32[2,896]{1,0:T(2,128)S(1)}, u32[]{:S(2)}, u32[]{:S(2)}) collective-permute-start(f32[2,896]{1,0:T(2,128)S(1)} %pad_maximum_fusion.13), channel_id=1, source_target_pairs={{0,8},{4,12},{8,0},{12,4},{16,24},{20,28},{24,16},{28,20},{1,9},{5... | collective-permute-start | bytes 21512 | tf_op jit(solution)/shard_map/ppermute | solution.py:30
  147.2 10.3 %collective-permute-start.18 = (bf16[2,1,1,1,2,40,640]{6,5,4,3,2,1,0:T(8,128)(2,1)S(1)}, bf16[2,1,1,1,2,40,640]{6,5,4,3,2,1,0:T(8,128)(2,1)S(1)}, u32[]{:S(2)}, u32[]{:S(2)}) collective-permute-start(bf16[2,1,1,1,2,40,640]{6,5,4,3,2,1,0:T(8,128)(2,1)S(1)} %get-tuple-element.132), channel_id=1, source_target_pairs={{0,8},{4,12},{8,0},{12,4},{16,24},{20,28},{24,16},{28,20},{1,9},{5... | collective-permute-start | bytes 614408 | tf_op jit(solution)/shard_map/ppermute | solution.py:30
  149.1 15.6 %collective-permute-start.14 = (bf16[2,2,1,1,2,40,640]{6,5,4,3,2,1,0:T(8,128)(2,1)S(1)}, bf16[2,2,1,1,2,40,640]{6,5,4,3,2,1,0:T(8,128)(2,1)S(1)}, u32[]{:S(2)}, u32[]{:S(2)}) collective-permute-start(bf16[2,2,1,1,2,40,640]{6,5,4,3,2,1,0:T(8,128)(2,1)S(1)} %get-tuple-element.123), channel_id=1, source_target_pairs={{0,4},{4,0},{8,12},{12,8},{16,20},{20,16},{24,28},{28,24},{1,5},{5... | collective-permute-start | bytes 1228808 | tf_op jit(solution)/shard_map/ppermute | solution.py:30
  149.4 15.5 %copy-start = (f32[8,4,40,640]{3,2,1,0:T(8,128)S(1)}, f32[8,4,40,640]{3,2,1,0:T(8,128)}, u32[]{:S(2)}) copy-start(f32[8,4,40,640]{3,2,1,0:T(8,128)} %get-tuple-element.96) | copy-start | bytes 9830404
  157.5 27.6 %collective-permute-start.21 = (bf16[1,1,1,1,2,40,640]{6,5,4,3,2,1,0:T(8,128)(2,1)S(1)}, bf16[1,1,1,1,2,40,640]{6,5,4,3,2,1,0:T(8,128)(2,1)S(1)}, u32[]{:S(2)}, u32[]{:S(2)}) collective-permute-start(bf16[1,1,1,1,2,40,640]{6,5,4,3,2,1,0:T(8,128)(2,1)S(1)} %get-tuple-element.148), channel_id=1, source_target_pairs={{0,16},{4,20},{8,24},{12,28},{16,0},{20,4},{24,8},{28,12},{1,17},{... | collective-permute-start | bytes 307208 | tf_op jit(solution)/shard_map/ppermute | solution.py:30
  164.8 20.2 %collective-permute-start.17 = (bf16[2,1,1,1,2,40,640]{6,5,4,3,2,1,0:T(8,128)(2,1)S(1)}, bf16[2,1,1,1,2,40,640]{6,5,4,3,2,1,0:T(8,128)(2,1)S(1)}, u32[]{:S(2)}, u32[]{:S(2)}) collective-permute-start(bf16[2,1,1,1,2,40,640]{6,5,4,3,2,1,0:T(8,128)(2,1)S(1)} %get-tuple-element.133), channel_id=1, source_target_pairs={{0,8},{4,12},{8,0},{12,4},{16,24},{20,28},{24,16},{28,20},{1,9},{5... | collective-permute-start | bytes 614408 | tf_op jit(solution)/shard_map/ppermute | solution.py:30
  166.7 20.9 %collective-permute-start.20 = (bf16[2,2,2,1,2,40,640]{6,5,4,3,2,1,0:T(8,128)(2,1)S(1)}, bf16[2,2,2,1,2,40,640]{6,5,4,3,2,1,0:T(8,128)(2,1)S(1)}, u32[]{:S(2)}, u32[]{:S(2)}) collective-permute-start(bf16[2,2,2,1,2,40,640]{6,5,4,3,2,1,0:T(8,128)(2,1)S(1)} %get-tuple-element.114), channel_id=1, source_target_pairs={{0,2},{2,0},{1,3},{3,1},{4,6},{6,4},{5,7},{7,5},{8,10},{10,8},{9,1... | collective-permute-start | bytes 2457608 | tf_op jit(solution)/shard_map/ppermute | solution.py:30
  185.1 8.5 %collective-permute-start.22 = (bf16[1,1,1,1,2,40,640]{6,5,4,3,2,1,0:T(8,128)(2,1)S(1)}, bf16[1,1,1,1,2,40,640]{6,5,4,3,2,1,0:T(8,128)(2,1)S(1)}, u32[]{:S(2)}, u32[]{:S(2)}) collective-permute-start(bf16[1,1,1,1,2,40,640]{6,5,4,3,2,1,0:T(8,128)(2,1)S(1)} %get-tuple-element.150), channel_id=1, source_target_pairs={{0,16},{4,20},{8,24},{12,28},{16,0},{20,4},{24,8},{28,12},{1,17},{... | collective-permute-start | bytes 307208 | tf_op jit(solution)/shard_map/ppermute | solution.py:30
  187.8 11.8 %collective-permute-start.25 = (bf16[2,2,1,1,2,40,640]{6,5,4,3,2,1,0:T(8,128)(2,1)S(1)}, bf16[2,2,1,1,2,40,640]{6,5,4,3,2,1,0:T(8,128)(2,1)S(1)}, u32[]{:S(2)}, u32[]{:S(2)}) collective-permute-start(bf16[2,2,1,1,2,40,640]{6,5,4,3,2,1,0:T(8,128)(2,1)S(1)} %get-tuple-element.120), channel_id=1, source_target_pairs={{0,4},{4,0},{8,12},{12,8},{16,20},{20,16},{24,28},{28,24},{1,5},{5... | collective-permute-start | bytes 1228808 | tf_op jit(solution)/shard_map/ppermute | solution.py:30
  193.6 9.2 %collective-permute-start.23 = (f32[2,2,40,640]{3,2,1,0:T(8,128)S(1)}, f32[2,2,40,640]{3,2,1,0:T(8,128)S(1)}, u32[]{:S(2)}, u32[]{:S(2)}) collective-permute-start(f32[2,2,40,640]{3,2,1,0:T(8,128)S(1)} %pad_maximum_fusion.6), channel_id=1, source_target_pairs={{0,2},{2,0},{1,3},{3,1},{4,6},{6,4},{5,7},{7,5},{8,10},{10,8},{9,1... | collective-permute-start | bytes 1228808 | tf_op jit(solution)/shard_map/ppermute | solution.py:30
  194.8 4.7 %collective-permute-start.30 = (f32[4,896]{1,0:T(4,128)S(1)}, f32[4,896]{1,0:T(4,128)S(1)}, u32[]{:S(2)}, u32[]{:S(2)}) collective-permute-start(f32[4,896]{1,0:T(4,128)S(1)} %pad_maximum_fusion.12), channel_id=1, source_target_pairs={{0,16},{4,20},{8,24},{12,28},{16,0},{20,4},{24,8},{28,12},{1,17},{... | collective-permute-start | bytes 43016 | tf_op jit(solution)/shard_map/ppermute | solution.py:30
  199.6 6.9 %collective-permute-start.26 = (bf16[2,1,1,1,2,40,640]{6,5,4,3,2,1,0:T(8,128)(2,1)S(1)}, bf16[2,1,1,1,2,40,640]{6,5,4,3,2,1,0:T(8,128)(2,1)S(1)}, u32[]{:S(2)}, u32[]{:S(2)}) collective-permute-start(bf16[2,1,1,1,2,40,640]{6,5,4,3,2,1,0:T(8,128)(2,1)S(1)} %get-tuple-element.129), channel_id=1, source_target_pairs={{0,8},{4,12},{8,0},{12,4},{16,24},{20,28},{24,16},{28,20},{1,9},{5... | collective-permute-start | bytes 614408 | tf_op jit(solution)/shard_map/ppermute | solution.py:30
  206.6 6.7 %collective-permute-start.27 = (bf16[1,1,1,1,2,40,640]{6,5,4,3,2,1,0:T(8,128)(2,1)S(1)}, bf16[1,1,1,1,2,40,640]{6,5,4,3,2,1,0:T(8,128)(2,1)S(1)}, u32[]{:S(2)}, u32[]{:S(2)}) collective-permute-start(bf16[1,1,1,1,2,40,640]{6,5,4,3,2,1,0:T(8,128)(2,1)S(1)} %add_convert_fusion.9), channel_id=1, source_target_pairs={{0,16},{4,20},{8,24},{12,28},{16,0},{20,4},{24,8},{28,12},{1,17},{... | collective-permute-start | bytes 307208 | tf_op jit(solution)/shard_map/ppermute | solution.py:30
  207.5 11.8 %collective-permute-start.24 = (f32[2,4,40,640]{3,2,1,0:T(8,128)S(1)}, f32[2,4,40,640]{3,2,1,0:T(8,128)S(1)}, u32[]{:S(2)}, u32[]{:S(2)}) collective-permute-start(f32[2,4,40,640]{3,2,1,0:T(8,128)S(1)} %pad_maximum_fusion.2), channel_id=1, source_target_pairs={{0,1},{1,0},{2,3},{3,2},{4,5},{5,4},{6,7},{7,6},{8,9},{9,8},{10,11... | collective-permute-start | bytes 2457608 | tf_op jit(solution)/shard_map/ppermute | solution.py:30
  213.3 5.8 %collective-permute-start.28 = (f32[1,2,40,640]{3,2,1,0:T(8,128)S(1)}, f32[1,2,40,640]{3,2,1,0:T(8,128)S(1)}, u32[]{:S(2)}, u32[]{:S(2)}) collective-permute-start(f32[1,2,40,640]{3,2,1,0:T(8,128)S(1)} %add_bitcast_fusion), channel_id=1, source_target_pairs={{0,2},{2,0},{1,3},{3,1},{4,6},{6,4},{5,7},{7,5},{8,10},{10,8},{9,1... | collective-permute-start | bytes 614408 | tf_op jit(solution)/shard_map/ppermute | solution.py:30
  219.2 1.8 collective-permute-start.29
  221.2 1.4 copy-start.6
Sparse Core Ops, SparseCore 0:
  10.8 75.4 all-gather.1

commit v5 on v3

--- a/solution.py
+++ b/solution.py
@@ -16,6 +16,7 @@
 bf16 = jnp.bfloat16
 f32 = jnp.float32
 VMEM_BYTES = 56 * 1024 * 1024
+PAIR_WIDTH = 8960
 
 
 def embedding(diffusion_step, embed_width):
@@ -36,6 +37,12 @@
 
 def params():
     return pltpu.CompilerParams(vmem_limit_bytes=VMEM_BYTES)
+
+
+def cost(microseconds):
+    return pl.CostEstimate(
+        flops=int(microseconds * 1.15e9), transcendentals=0, bytes_accessed=int(microseconds * 1e5)
+    )
 
 
 def whole(shape):
@@ -84,27 +91,36 @@
 
 
 class Chain:
-    def __init__(self, keep, send):
+    def __init__(self, keep, *sends):
         shards, taps, half, cols = keep.shape
         dp_masks = bits_of(shards)[::-1]
         x_masks = bits_of(lax.axis_size("x"))[::-1]
         nd, nx = len(dp_masks), len(x_masks)
         shape = (2,) * (nd + nx) + (taps >> nx, half, cols)
-        self.got = flip(send, "core").reshape(shape)
+        gots = [flip(send, "core") for send in sends]
+        if len(gots) == 1:
+            self.got, self.pair = gots[0].reshape(shape), None
+        else:
+            shape_of_one = shape[:nd] + (1,) + shape[nd + 1 :]
+            self.got, self.pair = (got.reshape(shape_of_one) for got in gots)
         self.keep = keep.reshape(shape)
-        self.stages = [("x", m, nd + i) for i, m in list(enumerate(x_masks))[::-1]]
+        self.stages = [("x", m, nd + i) for i, m in enumerate(x_masks)]
         self.stages += [("dp", m, i) for i, m in list(enumerate(dp_masks))[::-1]]
 
-    def launch(self):
+    def launch(self, *tokens):
+        if tokens:
+            self.got = after(self.got, *tokens)
         axis, mask, spot = self.stages.pop(0)
         bit = is_upper(axis, mask).astype(jnp.int32)
 
         def pick(which):
             kept = lax.dynamic_index_in_dim(self.keep, which, spot)
+            if self.pair is not None:
+                return kept + jnp.where(which != 0, self.pair, self.got).astype(f32)
             return kept + lax.dynamic_index_in_dim(self.got, which, spot).astype(f32)
 
         other = pick(1 - bit).astype(bf16)
-        self.keep, self.got = pick(bit), flip(other, axis, mask)
+        self.keep, self.got, self.pair = pick(bit), flip(other, axis, mask), None
         return other
 
     def land(self, token):
@@ -199,6 +215,7 @@
             jax.ShapeDtypeStruct((count, 1, channels), f32),
         ),
         compiler_params=params(),
+        cost_estimate=cost(7.6),
         name="norm",
     )(frames, same)
 
@@ -217,6 +234,7 @@
         out_specs=pl.BlockSpec((1, wide, rows), lambda i: (i, 0, 0)),
         out_shape=jax.ShapeDtypeStruct((3, wide, rows), bf16),
         compiler_params=params(),
+        cost_estimate=cost(8.5),
         name="turn",
     )(views)
 
@@ -248,11 +266,12 @@
             jax.ShapeDtypeStruct((1, channels), f32),
         ),
         compiler_params=params(),
+        cost_estimate=cost(6.5),
         name="hidden_grad",
     )(cot, following, temporal)
 
 
-def store_halves(core_ref, grad, keep_ref, send_ref, slot):
+def store_halves(core_ref, grad, keep_ref, send_ref, slot, send_slot):
     shards, _, half, channels = keep_ref.shape
     grad = grad.reshape(shards, 2 * half, channels)
     low, high = grad[:, :half], grad[:, half:]
@@ -260,16 +279,16 @@
     @pl.when(core_ref[0] == 0)
     def _():
         keep_ref[:, slot] = low
-        send_ref[:, slot] = high.astype(bf16)
+        send_ref[:, send_slot] = high.astype(bf16)
 
     @pl.when(core_ref[0] != 0)
     def _():
         keep_ref[:, slot] = high
-        send_ref[:, slot] = low.astype(bf16)
+        send_ref[:, send_slot] = low.astype(bf16)
 
 
 def weight_grad_kernel(core_ref, x_ref, back_ref, keep_ref, send_ref):
-    store_halves(core_ref, matmul(x_ref[0], back_ref[...]), keep_ref, send_ref, 0)
+    store_halves(core_ref, matmul(x_ref[0], back_ref[...]), keep_ref, send_ref, 0, 0)
 
 
 def weight_grad(turned, hidden_back, first, shards, core):
@@ -290,27 +309,31 @@
             jax.ShapeDtypeStruct((shards, 4, half, channels), bf16),
         ),
         compiler_params=params(),
+        cost_estimate=cost(8.5),
         name="weight_grad",
     )(core, turned, hidden_back)
 
 
 def last_grad_kernel(
-    core_ref, x_ref, back_ref, hidden_ref, before_ref, cot_ref, keep_ref, send_ref
+    core_ref, x_ref, back_ref, hidden_ref, before_ref, cot_ref, keep_ref, one_ref, two_ref
 ):
-    store_halves(core_ref, matmul(x_ref[0], back_ref[...]), keep_ref, send_ref, 0)
+    sends = ((one_ref, 0), (one_ref, 1), (two_ref, 0), (two_ref, 1))
+    grad = matmul(x_ref[0], back_ref[...])
+    store_halves(core_ref, grad, keep_ref, sends[0][0], 0, sends[0][1])
     for k in range(3):
         grad = 0.0
         for o in range(cot_ref.shape[0]):
             frame = 2 * o + k - 1
             x = before_ref[...] if frame < 0 else hidden_ref[frame]
             grad += matmul_tn(x, cot_ref[o])
-        store_halves(core_ref, grad, keep_ref, send_ref, 1 + k)
+        store_halves(core_ref, grad, keep_ref, sends[1 + k][0], 1 + k, sends[1 + k][1])
 
 
 def last_grad(turned, hidden_back, hidden, before, cot, shards, core):
     rows, channels = hidden_back.shape
     half = channels // shards // 2
     shape = (shards, 4, half, channels)
+    two = (shards, 2, half, channels)
     return pl.pallas_call(
         last_grad_kernel,
         grid=(1,),
@@ -322,9 +345,14 @@
             whole(before.shape),
             whole(cot.shape),
         ],
-        out_specs=(whole(shape), whole(shape)),
-        out_shape=(jax.ShapeDtypeStruct(shape, f32), jax.ShapeDtypeStruct(shape, bf16)),
-        compiler_params=params(),
+        out_specs=(whole(shape), whole(two), whole(two)),
+        out_shape=(
+            jax.ShapeDtypeStruct(shape, f32),
+            jax.ShapeDtypeStruct(two, bf16),
+            jax.ShapeDtypeStruct(two, bf16),
+        ),
+        compiler_params=params(),
+        cost_estimate=cost(10.3),
         name="last_grad",
     )(core, turned, hidden_back, hidden, before, cot)
 
@@ -346,11 +374,12 @@
         temporal_kernel,
         out_shape=jax.ShapeDtypeStruct((frames // 2, pixels, channels), f32),
         compiler_params=params(),
+        cost_estimate=cost(5.2),
         name="temporal",
     )(hidden, before, temporal)
 
 
-def conv_forward_kernel(views_ref, w_ref, shift_ref, out_ref, acc_ref, tall_ref):
+def conv_forward_kernel(views_ref, w_ref, shift_ref, out_ref, last_ref, acc_ref, tall_ref):
     r = pl.program_id(0)
     rows, channels = acc_ref.shape
     for s in range(3):
@@ -367,7 +396,9 @@
 
     @pl.when(r == 2)
     def _():
-        out_ref[...] = (acc_ref[...] + part).astype(bf16).reshape(out_ref.shape)
+        hidden = (acc_ref[...] + part).astype(bf16).reshape(out_ref.shape)
+        out_ref[...] = hidden
+        last_ref[...] = hidden[-1]
 
 
 def conv_forward(views, spatial, shift):
@@ -382,13 +413,17 @@
             pl.BlockSpec((channels, wide), lambda i: (0, i)),
             whole((1, channels)),
         ],
-        out_specs=whole((frames, pixels, channels)),
-        out_shape=jax.ShapeDtypeStruct((frames, pixels, channels), bf16),
+        out_specs=(whole((frames, pixels, channels)), whole((pixels, channels))),
+        out_shape=(
+            jax.ShapeDtypeStruct((frames, pixels, channels), bf16),
+            jax.ShapeDtypeStruct((pixels, channels), bf16),
+        ),
         scratch_shapes=[
             pltpu.VMEM((frames * pixels, channels), f32),
             pltpu.VMEM((wide, channels), bf16),
         ],
         compiler_params=params(),
+        cost_estimate=cost(15),
         name="conv_forward",
     )(views, spatial, shift)
 
@@ -426,6 +461,7 @@
         out_specs=whole((rows, channels)),
         out_shape=jax.ShapeDtypeStruct((rows, channels), f32),
         compiler_params=params(),
+        cost_estimate=cost(12),
         name="conv_back_start",
     )(views, spatial)
 
@@ -434,6 +470,10 @@
     count, views_ref, w_ref, part_ref, x_ref, mean_ref, scale_ref, same_ref, out_ref, acc_ref
 ):
     acc_ref[...] = part_ref[...] + back_part(views_ref, w_ref, 2)
+    back_through_norm(count, x_ref, mean_ref, scale_ref, same_ref, out_ref, acc_ref)
+
+
+def back_through_norm(count, x_ref, mean_ref, scale_ref, same_ref, out_ref, acc_ref):
     frames, pixels, _ = x_ref.shape
 
     def parts(f):
@@ -475,6 +515,7 @@
         out_shape=jax.ShapeDtypeStruct(frames.shape, f32),
         scratch_shapes=[pltpu.VMEM((count * pixels, channels), f32)],
         compiler_params=params(),
+        cost_estimate=cost(12),
         name="conv_back_end",
     )(views, spatial, part, frames, mean, scale, same)
 
@@ -515,7 +556,7 @@
 
     def turn(token):
         held["turned"] = turned_columns(after(held["views"], token))
-        return held["turned"][0, :8, :128]
+        return held["turned"]
 
     temporal_full = gather_temporal(temporal_weight, (activate, turn))
     views, mean, scale = held["views"], held["mean"], held["scale"]
@@ -524,61 +565,55 @@
     embedded = embedding(timesteps[0], time_weight.shape[1])
     hidden_back, back_views, shift_sum = hidden_gradient(cot, following, temporal_full, breadth)
     flat_back = hidden_back.reshape(frame_count * pixels, channels)
-    sums = shift_sum
-    arriving = flip(sums, "core")
+    pairs = jnp.concatenate([shift_sum, embedded[None]], axis=1)
+    pairs = jnp.pad(pairs, ((0, 0), (0, PAIR_WIDTH - pairs.shape[1])))
+    pairs = lax.all_gather(pairs, ("dp", "x", "core"), axis=0, tiled=True)
 
     one = weight_grad(turned, flat_back, 0, dp, core_scalar)
     chain_a = Chain(*one)
-    sums = sums + after(arriving, one[1])
-    out_a = chain_a.launch()
-    for mask in bits_of(x_size):
-        arriving = flip(sums, "x", mask)
-        sums = sums + after(arriving, out_a)
-    pairs = jnp.concatenate([sums, embedded[None]], axis=1)
-    two = weight_grad(turned, after(flat_back, out_a), 4, dp, core_scalar)
+    two = weight_grad(turned, flat_back, 4, dp, core_scalar)
     chain_a.land(two[1])
     chain_b = Chain(*two)
-    out_b = chain_b.launch()
     out_a = chain_a.launch()
 
     time_full = spatial_full[:, 9 * channels :]
     time_shift = jnp.dot(time_full.astype(f32), embedded, precision=lax.Precision.HIGHEST)
-    hidden = conv_forward(views, spatial_full, after(time_shift, out_a, out_b)[None])
+    hidden, end = conv_forward(views, spatial_full, after(time_shift, out_a)[None])
     chain_a.land(hidden)
     chain_b.land(hidden)
-    before = lax.ppermute(hidden[-1], ("x", "core"), neighbours(x_size, 1))
+    before = lax.ppermute(end, ("x", "core"), neighbours(x_size, 1))
     out_a = chain_a.launch()
-    out_b = chain_b.launch()
-    for mask in bits_of(dp):
-        pairs = jnp.concatenate([pairs, flip(pairs, "dp", mask)], axis=0)
-    last = last_grad(
-        turned, flat_back, after(hidden, out_a, out_b), before, cot, dp, core_scalar
-    )
+    out_b = chain_b.launch(before)
+    last = last_grad(turned, flat_back, after(hidden, out_a, out_b), before, cot, dp, core_scalar)
     chain_a.land(last[1])
     chain_b.land(last[1])
     chain_c = Chain(*last)
-    out_c = chain_c.launch()
     out_a = chain_a.launch()
-    out_b = chain_b.launch()
-
-    part = conv_back_start(after(back_views, out_a, out_b, out_c), spatial_full)
+    out_b = chain_b.launch(out_a)
+    out_c = chain_c.launch(out_b)
+
+    part = conv_back_start(after(back_views, out_c), spatial_full)
     chain_a.land(part)
     chain_b.land(part)
     chain_c.land(part)
-    out_c = chain_c.launch()
-    first = chain_a.finish()
-    out_b = chain_b.launch() if chain_b.stages else out_c
+    out_a = chain_a.launch()
+    out_b = chain_b.launch(out_a)
+    out_c = chain_c.launch(out_b)
     input_grad = conv_back_end(
-        after(back_views, out_c, out_b), spatial_full, part, frames, mean, scale, same
-    )
+        after(back_views, out_c), spatial_full, part, frames, mean, scale, same
+    )
+    chain_a.land(input_grad)
     chain_b.land(input_grad)
     chain_c.land(input_grad)
     out_c = chain_c.launch()
-    rows = jnp.stack([first, chain_b.finish()])
-
-    downsampled = temporal_forward(after(hidden, out_c, rows), before, temporal_full)
+    first = chain_a.finish()
+    out_b = chain_b.launch(out_c)
+
+    downsampled = temporal_forward(after(hidden, first, out_b), before, temporal_full)
+    chain_b.land(downsampled)
     chain_c.land(downsampled)
-    rows = join_x(rows, downsampled)
+    out_c = chain_c.launch()
+    rows = join_x(jnp.stack([first, after(chain_b.finish(), out_c)]))
     last_rows = join_core(join_x(chain_c.finish()[None]))[0]
     rows = join_core(rows)
     downsampled = downsampled.reshape(1, out_count, height, breadth, channels)
@@ -589,7 +624,7 @@
     )
     time_grad = lax.dot_general(
         mine,
-        pairs[:, channels:],
+        pairs[:, channels : channels + time_weight.shape[1]],
         (((0,), (0,)), ((), ())),
         precision=lax.Precision.HIGHEST,
         preferred_element_type=f32,

time: 256 us -> 220 us (0.86)
  waiting for transfers between devices: 61.5 us -> 34.1 us
  starting transfers between devices: 51.6 us -> 45 us
  other arithmetic: 26.3 us -> 20.8 us
    ppermute x29 -> x25, waiting for transfers between devices: 61.5 us -> 34.1 us  [flip(): return lax.ppermute(x, axis, [(i, i ^ mask) for i in range(count)])]
    ppermute x29 -> x25, starting transfers between devices: 48.8 us -> 40.4 us  [flip(): return lax.ppermute(x, axis, [(i, i ^ mask) for i in range(count)])]
    convert_element_type x4, other arithmetic: 7.85 us -> 3.1 us  [launch(): other = pick(1 - bit).astype(bf16)]
    add x8 -> x7, other arithmetic: 9.69 us -> 6.48 us  [pick(): return kept + lax.dynamic_index_in_dim(self.got, which, spot).astype(f32)]
    unnamed x16 -> x19, local copies, waits for them, and re-layouts: 2.84 us -> 5.42 us
  transfers between devices with their start and end apart: 32 -> 29, of which waited for: 16 -> 11; matrix products, arithmetic and copies ran while one was open for 11% -> 10% of each run, Pallas kernels for 33% -> 43%
where the time goes in v5:
time: 220 us; the launch traced here: 219 us
  Pallas kernels  94.4 us (43%)
  starting transfers between devices  45 us (20%)
  waiting for transfers between devices  34.1 us (16%)
  other arithmetic  20.8 us (9%)
  between operations  16.5 us (8%)
  local copies, waits for them, and re-layouts  6.05 us (3%)
  matrix products  2.34 us (1%)
    ppermute x25, starting transfers between devices, flip(): return lax.ppermute(x, axis, [(i, i ^ mask) for i in range(count)])  40.4 us
    ppermute x25, waiting for transfers between devices, flip(): return lax.ppermute(x, axis, [(i, i ^ mask) for i in range(count)])  34.1 us
    pallas_call x2, Pallas kernels, weight_grad(): pl.pallas_call(weight_grad_kernel, grid=(4,), in_specs=[pl.BlockSpec(memo...  17.1 us
    pallas_call x1, Pallas kernels, conv_forward(): pl.pallas_call(conv_forward_kernel, grid=(3,), in_specs=[whole(views.shap...  15.2 us
    pallas_call x1, Pallas kernels, conv_back_end(): pl.pallas_call(lambda *refs: conv_back_end_kernel(pixels * (channels // G...  12.1 us
    pallas_call x1, Pallas kernels, conv_back_start(): pl.pallas_call(conv_back_kernel, grid=(2,), in_specs=[whole(views.shape),...  11.7 us
    pallas_call x1, Pallas kernels, last_grad(): pl.pallas_call(last_grad_kernel, grid=(1,), in_specs=[pl.BlockSpec(memory...  10.4 us
    pallas_call x1, Pallas kernels, turned_columns(): pl.pallas_call(turn_kernel, grid=(3,), in_specs=[whole(views.shape)], out...  8.35 us
  transfers between devices with their start and end apart: 29, of which 11 were waited for; matrix products, arithmetic and copies ran while one was open for 10% of the time, Pallas kernels for 43%

profile of v5, /device:TPU:0, one launch (start us, length us, event | category | flops | bytes accessed | tf_op | source)
XLA Modules:
  0.0 219.2 jit_solution(10432019729954726026)
XLA Ops:
  8.1 1.9 fusion.1
  10.0 4.1 %collective-permute-start = (bf16[1,1,1,40,1280]{4,3,2,1,0:T(8,128)(2,1)S(1)}, bf16[1,1,1,40,1280]{4,3,2,1,0:T(8,128)(2,1)S(1)}, u32[]{:S(2)}, u32[]{:S(2)}) collective-permute-start(bf16[1,1,1,40,1280]{4,3,2,1,0:T(8,128)(2,1)S(1)} %dynamic-slice_bitcast_fusion), channel_id=1, source_target_pairs={{0,16},{4,20},{8,24},{12,28},{16,0},{20,4},{24,8},{28,12},{1,17},{... | collective-permute-start | bytes 307208 | tf_op jit(solution)/shard_map/ppermute | solution.py:31
  14.2 5.1 %collective-permute-done = bf16[1,1,1,40,1280]{4,3,2,1,0:T(8,128)(2,1)S(1)} collective-permute-done((bf16[1,1,1,40,1280]{4,3,2,1,0:T(8,128)(2,1)S(1)}, bf16[1,1,1,40,1280]{4,3,2,1,0:T(8,128)(2,1)S(1)}, u32[]{:S(2)}, u32[]{:S(2)}) %collective-permute-start) | collective-permute-done | bytes 102432 | tf_op jit(solution)/shard_map/ppermute | solution.py:31
  20.1 1.5 fusion.refs_1_.refs_6_
  21.6 5.3 %collective-permute-done.1 = bf16[2,1,1,40,1280]{4,3,2,1,0:T(8,128)(2,1)S(1)} collective-permute-done((bf16[2,1,1,40,1280]{4,3,2,1,0:T(8,128)(2,1)S(1)}, bf16[2,1,1,40,1280]{4,3,2,1,0:T(8,128)(2,1)S(1)}, u32[]{:S(2)}, u32[]{:S(2)}) %collective-permute-start.1) | collective-permute-done | bytes 204832 | tf_op jit(solution)/shard_map/ppermute | solution.py:31
  26.9 1.4 collective-permute-start.2
  28.3 7.7 %norm.1 = (bf16[4,18,16,1920]{3,2,1,0:T(8,128)(2,1)}, f32[4,1,640]{2,1,0:T(1,128)}, f32[4,1,640]{2,1,0:T(1,128)}) custom-call(bf16[4,256,640]{2,1,0:T(8,128)(2,1)} %bitcast.104, f32[640,640]{1,0:T(8,128)} %fusion.refs_1_.refs_6_), custom_call_target="tpu_custom_call" | custom-call | flops 8739999744 | bytes 760000 | tf_op jit(solution)/shard_map/norm/pallas_call | solution.py:210
  36.1 3.0 %collective-permute-done.2 = bf16[2,2,1,40,1280]{4,3,2,1,0:T(8,128)(2,1)S(1)} collective-permute-done((bf16[2,2,1,40,1280]{4,3,2,1,0:T(8,128)(2,1)S(1)}, bf16[2,2,1,40,1280]{4,3,2,1,0:T(8,128)(2,1)S(1)}, u32[]{:S(2)}, u32[]{:S(2)}) %collective-permute-start.2) | collective-permute-done | bytes 409632 | tf_op jit(solution)/shard_map/ppermute | solution.py:31
  39.2 1.5 collective-permute-start.4
  40.7 8.4 %turn.1 = bf16[3,1920,1024]{2,1,0:T(8,128)(2,1)} custom-call(bf16[4,18,16,1920]{3,2,1,0:T(8,128)(2,1)} %get-tuple-element.66.views_ref), custom_call_target="tpu_custom_call" | custom-call | flops 9774999552 | bytes 850000 | tf_op jit(solution)/shard_map/turn/pallas_call | solution.py:230
  49.8 1.1 pad_maximum_fusion.1
  51.1 1.5 collective-permute-start.3
  52.6 1.5 collective-permute-done.5
  54.5 1.7 pad_maximum_fusion
  56.9 6.7 %hidden_grad.1 = (bf16[4,256,640]{2,1,0:T(8,128)(2,1)}, bf16[4,18,16,1920]{3,2,1,0:T(8,128)(2,1)}, f32[1,640]{1,0:T(1,128)}) custom-call(bf16[2,256,640]{2,1,0:T(8,128)(2,1)} %bitcast.100, bf16[256,640]{1,0:T(8,128)(2,1)} %copy-done.8, bf16[640,1920]{1,0:T(8,128)(2,1)} %bitcast.92), custom_call_target="tpu_custom_call" | custom-call | flops 7474999808 | bytes 650000 | tf_op jit(solution)/shard_map/hidden_grad/pallas_call | solution.py:261
  63.6 8.5 %weight_grad.2 = (f32[8,4,40,640]{3,2,1,0:T(8,128)}, bf16[8,4,40,640]{3,2,1,0:T(8,128)(2,1)}) custom-call(s32[1]{0:T(128)} %bitcast.4.core_ref, bf16[9,640,1024]{2,1,0:T(8,128)(2,1)} %bitcast.106, bf16[1024,640]{1,0:T(8,128)(2,1)} %bitcast.110), custom_call_target="tpu_custom_call" | custom-call | flops 9774999552 | bytes 850000 | tf_op jit(solution)/shard_map/weight_grad/pallas_call | solution.py:298
  72.0 4.3 %collective-permute-start.6 = (bf16[8,4,40,640]{3,2,1,0:T(8,128)(2,1)}, bf16[8,4,40,640]{3,2,1,0:T(8,128)(2,1)}, u32[]{:S(2)}, u32[]{:S(2)}) collective-permute-start(bf16[8,4,40,640]{3,2,1,0:T(8,128)(2,1)} %get-tuple-element.70), channel_id=1, source_target_pairs={{0,1},{1,0},{2,3},{3,2},{4,5},{5,4},{6,7},{7,6},{8,9},{9,8},{10,11... | collective-permute-start | bytes 4915208 | tf_op jit(solution)/shard_map/ppermute | solution.py:31
  77.0 8.6 %weight_grad.3 = (f32[8,4,40,640]{3,2,1,0:T(8,128)}, bf16[8,4,40,640]{3,2,1,0:T(8,128)(2,1)}) custom-call(s32[1]{0:T(128)} %bitcast.4.core_ref, bf16[9,640,1024]{2,1,0:T(8,128)(2,1)} %bitcast.107, bf16[1024,640]{1,0:T(8,128)(2,1)} %bitcast.111), custom_call_target="tpu_custom_call" | custom-call | flops 9774999552 | bytes 850000 | tf_op jit(solution)/shard_map/weight_grad/pallas_call | solution.py:298
  85.7 2.8 %convert_add_fusion.1 = (f32[2,2,2,1,2,40,640]{6,5,4,3,2,1,0:T(8,128)S(1)}, bf16[2,2,2,1,2,40,640]{6,5,4,3,2,1,0:T(8,128)(2,1)}) fusion(f32[2,2,2,2,2,40,640]{6,5,4,3,2,1,0:T(8,128)S(1)} %bitcast.91, s32[]{:T(128)S(6)} %select_n.244, bf16[2,2,2,2,2,40,640]{6,5,4,3,2,1,0:T(8,128)(2,1)} %bitcast.11, s32[]{:T(128)S(6)} %select_n.243), kind=kLoop, calls=%fused_computation.17 | loop fusion | flops 2048000 | bytes 7372808 | tf_op jit(solution)/shard_map/add | solution.py:120
  88.5 1.4 convolution_reduce_fusion
  90.4 15.2 %conv_forward.1 = (bf16[4,256,640]{2,1,0:T(8,128)(2,1)}, bf16[256,640]{1,0:T(8,128)(2,1)}) custom-call(bf16[4,18,16,1920]{3,2,1,0:T(8,128)(2,1)} %get-tuple-element.66.views_ref, bf16[640,6016]{1,0:T(8,128)(2,1)} %all-gather.4.cloned.1.call-done.w_ref.refs_1_, f32[1,640]{1,0:T(1,128)} %broadcast_in_dim.10.shift_ref), custom_call_target="tpu_custom_call" | custom-call | flops 17250000896 | bytes 1500000 | tf_op jit(solution)/shard_map/conv_forward/pallas_call | solution.py:408
  105.6 3.0 %collective-permute-start.8 = (bf16[256,640]{1,0:T(8,128)(2,1)}, bf16[256,640]{1,0:T(8,128)(2,1)}, u32[]{:S(2)}, u32[]{:S(2)}) collective-permute-start(bf16[256,640]{1,0:T(8,128)(2,1)} %get-tuple-element.79), channel_id=1, source_target_pairs={{0,1},{1,2},{2,3},{4,5},{5,6},{6,7},{8,9},{9,10},{10,11},{12,13},{... | collective-permute-start | bytes 983048 | tf_op jit(solution)/shard_map/ppermute | solution.py:584
  109.3 1.2 copy-done.3
  110.5 2.2 convert_add_fusion.5
  113.1 2.8 %add_convert_fusion.1 = (bf16[2,2,2,1,2,40,640]{6,5,4,3,2,1,0:T(8,128)(2,1)}, f32[2,2,2,1,2,40,640]{6,5,4,3,2,1,0:T(8,128)S(1)}) fusion(f32[2,2,2,2,2,40,640]{6,5,4,3,2,1,0:T(8,128)S(1)} %bitcast.89, s32[]{:T(128)S(6)} %select_n.243, bf16[2,2,2,2,2,40,640]{6,5,4,3,2,1,0:T(8,128)(2,1)} %bitcast.96, s32[]{:T(128)S(6)} %select_n.244), kind=kLoop, calls=%fused_computation.18 | loop fusion | flops 2048000 | bytes 7372808 | tf_op jit(solution)/shard_map/convert_element_type | solution.py:122
  115.8 3.3 %collective-permute-start.9 = (bf16[2,2,2,1,2,40,640]{6,5,4,3,2,1,0:T(8,128)(2,1)}, bf16[2,2,2,1,2,40,640]{6,5,4,3,2,1,0:T(8,128)(2,1)S(1)}, u32[]{:S(2)}, u32[]{:S(2)}) collective-permute-start(bf16[2,2,2,1,2,40,640]{6,5,4,3,2,1,0:T(8,128)(2,1)} %get-tuple-element.123), channel_id=1, source_target_pairs={{0,2},{2,0},{1,3},{3,1},{4,6},{6,4},{5,7},{7,5},{8,10},{10,8},{9,1... | collective-permute-start | bytes 2457608 | tf_op jit(solution)/shard_map/ppermute | solution.py:31
  119.2 10.4 %last_grad.1 = (f32[8,4,40,640]{3,2,1,0:T(8,128)}, bf16[8,2,40,640]{3,2,1,0:T(8,128)(2,1)}, bf16[8,2,40,640]{3,2,1,0:T(8,128)(2,1)}) custom-call(s32[1]{0:T(128)} %bitcast.4.core_ref, bf16[9,640,1024]{2,1,0:T(8,128)(2,1)} %bitcast.108, bf16[1024,640]{1,0:T(8,128)(2,1)} %bitcast.112, bf16[4,256,640]{2,1,0:T(8,128)(2,1)} %get-tuple-element.110.hidden_ref, ...), custom_call_target="tpu_custom_call" | custom-call | flops 11845000192 | bytes 1030000 | tf_op jit(solution)/shard_map/last_grad/pallas_call | solution.py:337
  130.7 1.1 convert_add_fusion.8
  131.8 1.4 collective-permute-start.15
  133.2 3.9 %collective-permute-done.9 = bf16[2,2,2,1,2,40,640]{6,5,4,3,2,1,0:T(8,128)(2,1)S(1)} collective-permute-done((bf16[2,2,2,1,2,40,640]{6,5,4,3,2,1,0:T(8,128)(2,1)}, bf16[2,2,2,1,2,40,640]{6,5,4,3,2,1,0:T(8,128)(2,1)S(1)}, u32[]{:S(2)}, u32[]{:S(2)}) %collective-permute-start.9) | collective-permute-done | bytes 819232 | tf_op jit(solution)/shard_map/ppermute | solution.py:31
  137.3 0.9 collective-permute-start.12
  139.1 1.9 convert_add_fusion
  141.3 11.7 %conv_back_start.1.refs_2_ = f32[1024,640]{1,0:T(8,128)} custom-call(bf16[4,18,16,1920]{3,2,1,0:T(8,128)(2,1)} %get-tuple-element.103.views_ref.refs_0_, bf16[640,6016]{1,0:T(8,128)(2,1)} %all-gather.4.cloned.1.call-done.w_ref.refs_1_), custom_call_target="tpu_custom_call" | custom-call | flops 13799999488 | bytes 1200000 | tf_op jit(solution)/shard_map/conv_back_start/pallas_call | solution.py:457
  153.1 5.1 %collective-permute-start.19 = (bf16[1,1,1,1,2,40,640]{6,5,4,3,2,1,0:T(8,128)(2,1)S(1)}, bf16[1,1,1,1,2,40,640]{6,5,4,3,2,1,0:T(8,128)(2,1)S(1)}, u32[]{:S(2)}, u32[]{:S(2)}) collective-permute-start(bf16[1,1,1,1,2,40,640]{6,5,4,3,2,1,0:T(8,128)(2,1)S(1)} %get-tuple-element.154), channel_id=1, source_target_pairs={{0,16},{4,20},{8,24},{12,28},{16,0},{20,4},{24,8},{28,12},{1,17},{... | collective-permute-start | bytes 307208 | tf_op jit(solution)/shard_map/ppermute | solution.py:31
  158.3 3.6 %collective-permute-start.16 = (bf16[2,1,1,1,2,40,640]{6,5,4,3,2,1,0:T(8,128)(2,1)S(1)}, bf16[2,1,1,1,2,40,640]{6,5,4,3,2,1,0:T(8,128)(2,1)S(1)}, u32[]{:S(2)}, u32[]{:S(2)}) collective-permute-start(bf16[2,1,1,1,2,40,640]{6,5,4,3,2,1,0:T(8,128)(2,1)S(1)} %get-tuple-element.137), channel_id=1, source_target_pairs={{0,8},{4,12},{8,0},{12,4},{16,24},{20,28},{24,16},{28,20},{1,9},{5... | collective-permute-start | bytes 614408 | tf_op jit(solution)/shard_map/ppermute | solution.py:31
  162.1 0.9 collective-permute-start.18
  163.0 12.1 %conv_back_end.1 = f32[4,256,640]{2,1,0:T(8,128)} custom-call(bf16[4,18,16,1920]{3,2,1,0:T(8,128)(2,1)} %get-tuple-element.103.views_ref.refs_0_, bf16[640,6016]{1,0:T(8,128)(2,1)} %all-gather.4.cloned.1.call-done.w_ref.refs_1_, f32[1024,640]{1,0:T(8,128)} %conv_back_start.1.refs_2_, bf16[4,256,640]{2,1,0:T(8,128)(2,1)} %bitcast.105, ...), custom_call_target="tpu_custom_call" | custom-call | flops 13799999488 | bytes 1200000 | tf_op jit(solution)/shard_map/conv_back_end/pallas_call | solution.py:502
  175.4 7.7 %collective-permute-start.20 = (bf16[1,1,1,1,2,40,640]{6,5,4,3,2,1,0:T(8,128)(2,1)S(1)}, bf16[1,1,1,1,2,40,640]{6,5,4,3,2,1,0:T(8,128)(2,1)S(1)}, u32[]{:S(2)}, u32[]{:S(2)}) collective-permute-start(bf16[1,1,1,1,2,40,640]{6,5,4,3,2,1,0:T(8,128)(2,1)S(1)} %get-tuple-element.156), channel_id=1, source_target_pairs={{0,16},{4,20},{8,24},{12,28},{16,0},{20,4},{24,8},{28,12},{1,17},{... | collective-permute-start | bytes 307208 | tf_op jit(solution)/shard_map/ppermute | solution.py:31
  183.2 5.2 %temporal.1 = f32[2,256,640]{2,1,0:T(8,128)} custom-call(bf16[4,256,640]{2,1,0:T(8,128)(2,1)} %get-tuple-element.110.hidden_ref, bf16[256,640]{1,0:T(8,128)(2,1)} %collective-permute-done.8.before_ref, bf16[640,1920]{1,0:T(8,128)(2,1)} %bitcast.93), custom_call_target="tpu_custom_call" | custom-call | flops 5980000256 | bytes 520000 | tf_op jit(solution)/shard_map/temporal/pallas_call | solution.py:373
  188.4 1.7 collective-permute-start.24
  190.1 4.8 %collective-permute-done.24 = bf16[1,1,1,1,2,40,640]{6,5,4,3,2,1,0:T(8,128)(2,1)S(1)} collective-permute-done((bf16[1,1,1,1,2,40,640]{6,5,4,3,2,1,0:T(8,128)(2,1)S(1)}, bf16[1,1,1,1,2,40,640]{6,5,4,3,2,1,0:T(8,128)(2,1)S(1)}, u32[]{:S(2)}, u32[]{:S(2)}) %collective-permute-start.24) | collective-permute-done | bytes 102432 | tf_op jit(solution)/shard_map/ppermute | solution.py:31
  195.6 1.5 collective-permute-start.22
  197.1 1.3 copy.21
  198.5 4.5 %collective-permute-done.25 = f32[1,2,40,640]{3,2,1,0:T(8,128)S(1)} collective-permute-done((f32[1,2,40,640]{3,2,1,0:T(8,128)S(1)}, f32[1,2,40,640]{3,2,1,0:T(8,128)S(1)}, u32[]{:S(2)}, u32[]{:S(2)}) %collective-permute-start.25) | collective-permute-done | bytes 204832 | tf_op jit(solution)/shard_map/ppermute | solution.py:31
  203.2 4.5 %collective-permute-done.22 = f32[2,2,40,640]{3,2,1,0:T(8,128)S(1)} collective-permute-done((f32[2,2,40,640]{3,2,1,0:T(8,128)S(1)}, f32[2,2,40,640]{3,2,1,0:T(8,128)S(1)}, u32[]{:S(2)}, u32[]{:S(2)}) %collective-permute-start.22) | collective-permute-done | bytes 409632 | tf_op jit(solution)/shard_map/ppermute | solution.py:31
  207.9 1.0 fusion.37
  209.0 0.9 pad_maximum_fusion.3
  210.5 1.2 copy-done.6
  (97 shorter events, 10.1 us)
Async XLA Ops:
  8.0 2.0 copy-start.5
  8.0 80.4 %all-gather.4.cloned.1.call-start = ((), (), s32[]{:S(2)}) async-start(), calls=%async_computation | async-start | bytes 8181760 | tf_op jit(solution)/shard_map/all_gather | solution.py:546
  10.0 187.2 %all-gather.6.cloned.1.call-start = ((), (), s32[]{:S(2)}) async-start(), calls=%async_computation.1 | async-start | bytes 1182720 | tf_op jit(solution)/shard_map/all_gather | solution.py:570
  10.0 9.2 %collective-permute-start = (bf16[1,1,1,40,1280]{4,3,2,1,0:T(8,128)(2,1)S(1)}, bf16[1,1,1,40,1280]{4,3,2,1,0:T(8,128)(2,1)S(1)}, u32[]{:S(2)}, u32[]{:S(2)}) collective-permute-start(bf16[1,1,1,40,1280]{4,3,2,1,0:T(8,128)(2,1)S(1)} %dynamic-slice_bitcast_fusion), channel_id=1, source_target_pairs={{0,16},{4,20},{8,24},{12,28},{16,0},{20,4},{24,8},{28,12},{1,17},{... | collective-permute-start | bytes 307208 | tf_op jit(solution)/shard_map/ppermute | solution.py:31
  19.3 7.6 %collective-permute-start.1 = (bf16[2,1,1,40,1280]{4,3,2,1,0:T(8,128)(2,1)S(1)}, bf16[2,1,1,40,1280]{4,3,2,1,0:T(8,128)(2,1)S(1)}, u32[]{:S(2)}, u32[]{:S(2)}) collective-permute-start(bf16[2,1,1,40,1280]{4,3,2,1,0:T(8,128)(2,1)S(1)} %pad_maximum_fusion.10), channel_id=1, source_target_pairs={{0,8},{4,12},{8,0},{12,4},{16,24},{20,28},{24,16},{28,20},{1,9},{5... | collective-permute-start | bytes 614408 | tf_op jit(solution)/shard_map/ppermute | solution.py:31
  26.9 12.1 %collective-permute-start.2 = (bf16[2,2,1,40,1280]{4,3,2,1,0:T(8,128)(2,1)S(1)}, bf16[2,2,1,40,1280]{4,3,2,1,0:T(8,128)(2,1)S(1)}, u32[]{:S(2)}, u32[]{:S(2)}) collective-permute-start(bf16[2,2,1,40,1280]{4,3,2,1,0:T(8,128)(2,1)S(1)} %pad_maximum_fusion.5), channel_id=1, source_target_pairs={{0,4},{4,0},{8,12},{12,8},{16,20},{20,16},{24,28},{28,24},{1,5},{5... | collective-permute-start | bytes 1228808 | tf_op jit(solution)/shard_map/ppermute | solution.py:31
  39.2 10.4 %collective-permute-start.4 = (bf16[2,2,2,40,640]{4,3,2,1,0:T(8,128)(2,1)S(1)}, bf16[2,2,2,40,640]{4,3,2,1,0:T(8,128)(2,1)S(1)}, u32[]{:S(2)}, u32[]{:S(2)}) collective-permute-start(bf16[2,2,2,40,640]{4,3,2,1,0:T(8,128)(2,1)S(1)} %broadcast_select_fusion.9), channel_id=1, source_target_pairs={{0,2},{2,0},{1,3},{3,1},{4,6},{6,4},{5,7},{7,5},{8,10},{10,8},{9,1... | collective-permute-start | bytes 1228808 | tf_op jit(solution)/shard_map/ppermute | solution.py:31
  49.8 1.3 copy-start.4
  51.0 3.1 %collective-permute-start.5 = (bf16[2,2,2,40,1920]{4,3,2,1,0:T(8,128)(2,1)}, bf16[2,2,2,40,1920]{4,3,2,1,0:T(8,128)(2,1)S(1)}, u32[]{:S(2)}, u32[]{:S(2)}) collective-permute-start(bf16[2,2,2,40,1920]{4,3,2,1,0:T(8,128)(2,1)} %pad_maximum_fusion.1), channel_id=1, source_target_pairs={{0,1},{1,0},{2,3},{3,2},{4,5},{5,4},{6,7},{7,6},{8,9},{9,8},{10,11... | collective-permute-start | bytes 3686408 | tf_op jit(solution)/shard_map/ppermute | solution.py:31
  51.1 5.0 %collective-permute-start.3 = (bf16[256,640]{1,0:T(8,128)(2,1)S(1)}, bf16[256,640]{1,0:T(8,128)(2,1)S(1)}, u32[]{:S(2)}, u32[]{:S(2)}) collective-permute-start(bf16[256,640]{1,0:T(8,128)(2,1)S(1)} %bitcast.99), channel_id=1, source_target_pairs={{1,0},{2,1},{3,2},{5,4},{6,5},{7,6},{9,8},{10,9},{11,10},{13,12},{... | collective-permute-start | bytes 983048 | tf_op jit(solution)/shard_map/ppermute | solution.py:542
  56.2 0.7 copy-start.8
  72.0 13.7 %collective-permute-start.6 = (bf16[8,4,40,640]{3,2,1,0:T(8,128)(2,1)}, bf16[8,4,40,640]{3,2,1,0:T(8,128)(2,1)}, u32[]{:S(2)}, u32[]{:S(2)}) collective-permute-start(bf16[8,4,40,640]{3,2,1,0:T(8,128)(2,1)} %get-tuple-element.70), channel_id=1, source_target_pairs={{0,1},{1,0},{2,3},{3,2},{4,5},{5,4},{6,7},{7,6},{8,9},{9,8},{10,11... | collective-permute-start | bytes 4915208 | tf_op jit(solution)/shard_map/ppermute | solution.py:31
  77.0 8.7 %copy-start.2 = (f32[8,4,40,640]{3,2,1,0:T(8,128)S(1)}, f32[8,4,40,640]{3,2,1,0:T(8,128)}, u32[]{:S(2)}) copy-start(f32[8,4,40,640]{3,2,1,0:T(8,128)} %get-tuple-element.69) | copy-start | bytes 9830404
  85.6 23.7 %collective-permute-start.7 = (bf16[8,4,40,640]{3,2,1,0:T(8,128)(2,1)}, bf16[8,4,40,640]{3,2,1,0:T(8,128)(2,1)S(1)}, u32[]{:S(2)}, u32[]{:S(2)}) collective-permute-start(bf16[8,4,40,640]{3,2,1,0:T(8,128)(2,1)} %get-tuple-element.71), channel_id=1, source_target_pairs={{0,1},{1,0},{2,3},{3,2},{4,5},{5,4},{6,7},{7,6},{8,9},{9,8},{10,11... | collective-permute-start | bytes 4915208 | tf_op jit(solution)/shard_map/ppermute | solution.py:31
  88.4 20.9 %collective-permute-start.10 = (bf16[2,2,2,1,2,40,640]{6,5,4,3,2,1,0:T(8,128)(2,1)}, bf16[2,2,2,1,2,40,640]{6,5,4,3,2,1,0:T(8,128)(2,1)}, u32[]{:S(2)}, u32[]{:S(2)}) collective-permute-start(bf16[2,2,2,1,2,40,640]{6,5,4,3,2,1,0:T(8,128)(2,1)} %get-tuple-element.122), channel_id=1, source_target_pairs={{0,2},{2,0},{1,3},{3,1},{4,6},{6,4},{5,7},{7,5},{8,10},{10,8},{9,1... | collective-permute-start | bytes 2457608 | tf_op jit(solution)/shard_map/ppermute | solution.py:31
  105.6 7.4 %collective-permute-start.8 = (bf16[256,640]{1,0:T(8,128)(2,1)}, bf16[256,640]{1,0:T(8,128)(2,1)}, u32[]{:S(2)}, u32[]{:S(2)}) collective-permute-start(bf16[256,640]{1,0:T(8,128)(2,1)} %get-tuple-element.79), channel_id=1, source_target_pairs={{0,1},{1,2},{2,3},{4,5},{5,6},{6,7},{8,9},{9,10},{10,11},{12,13},{... | collective-permute-start | bytes 983048 | tf_op jit(solution)/shard_map/ppermute | solution.py:584
  109.3 1.2 copy-start.3
  110.5 2.6 %copy-start = (f32[8,4,40,640]{3,2,1,0:T(8,128)S(1)}, f32[8,4,40,640]{3,2,1,0:T(8,128)}, u32[]{:S(2)}) copy-start(f32[8,4,40,640]{3,2,1,0:T(8,128)} %get-tuple-element.76) | copy-start | bytes 9830404
  112.7 18.0 %collective-permute-start.11 = (bf16[2,2,1,1,2,40,640]{6,5,4,3,2,1,0:T(8,128)(2,1)}, bf16[2,2,1,1,2,40,640]{6,5,4,3,2,1,0:T(8,128)(2,1)}, u32[]{:S(2)}, u32[]{:S(2)}) collective-permute-start(bf16[2,2,1,1,2,40,640]{6,5,4,3,2,1,0:T(8,128)(2,1)} %get-tuple-element.130), channel_id=1, source_target_pairs={{0,4},{4,0},{8,12},{12,8},{16,20},{20,16},{24,28},{28,24},{1,5},{5... | collective-permute-start | bytes 1228808 | tf_op jit(solution)/shard_map/ppermute | solution.py:31
  115.8 14.2 %copy-start.7 = (f32[1,640]{1,0:T(1,128)S(1)}, f32[1,640]{1,0:T(1,128)}, u32[]{:S(2)}) copy-start(f32[1,640]{1,0:T(1,128)} %get-tuple-element.118) | copy-start | bytes 7684
  115.8 21.3 %collective-permute-start.9 = (bf16[2,2,2,1,2,40,640]{6,5,4,3,2,1,0:T(8,128)(2,1)}, bf16[2,2,2,1,2,40,640]{6,5,4,3,2,1,0:T(8,128)(2,1)S(1)}, u32[]{:S(2)}, u32[]{:S(2)}) collective-permute-start(bf16[2,2,2,1,2,40,640]{6,5,4,3,2,1,0:T(8,128)(2,1)} %get-tuple-element.123), channel_id=1, source_target_pairs={{0,2},{2,0},{1,3},{3,1},{4,6},{6,4},{5,7},{7,5},{8,10},{10,8},{9,1... | collective-permute-start | bytes 2457608 | tf_op jit(solution)/shard_map/ppermute | solution.py:31
  129.5 8.7 %collective-permute-start.14 = (bf16[8,2,40,640]{3,2,1,0:T(8,128)(2,1)}, bf16[8,2,40,640]{3,2,1,0:T(8,128)(2,1)}, u32[]{:S(2)}, u32[]{:S(2)}) collective-permute-start(bf16[8,2,40,640]{3,2,1,0:T(8,128)(2,1)} %get-tuple-element.84), channel_id=1, source_target_pairs={{0,1},{1,0},{2,3},{3,2},{4,5},{5,4},{6,7},{7,6},{8,9},{9,8},{10,11... | collective-permute-start | bytes 2457608 | tf_op jit(solution)/shard_map/ppermute | solution.py:31
  129.5 8.7 %collective-permute-start.13 = (bf16[8,2,40,640]{3,2,1,0:T(8,128)(2,1)}, bf16[8,2,40,640]{3,2,1,0:T(8,128)(2,1)}, u32[]{:S(2)}, u32[]{:S(2)}) collective-permute-start(bf16[8,2,40,640]{3,2,1,0:T(8,128)(2,1)} %get-tuple-element.92), channel_id=1, source_target_pairs={{0,1},{1,0},{2,3},{3,2},{4,5},{5,4},{6,7},{7,6},{8,9},{9,8},{10,11... | collective-permute-start | bytes 2457608 | tf_op jit(solution)/shard_map/ppermute | solution.py:31
  131.8 21.2 %collective-permute-start.15 = (bf16[2,1,1,1,2,40,640]{6,5,4,3,2,1,0:T(8,128)(2,1)S(1)}, bf16[2,1,1,1,2,40,640]{6,5,4,3,2,1,0:T(8,128)(2,1)S(1)}, u32[]{:S(2)}, u32[]{:S(2)}) collective-permute-start(bf16[2,1,1,1,2,40,640]{6,5,4,3,2,1,0:T(8,128)(2,1)S(1)} %get-tuple-element.140), channel_id=1, source_target_pairs={{0,8},{4,12},{8,0},{12,4},{16,24},{20,28},{24,16},{28,20},{1,9},{5... | collective-permute-start | bytes 614408 | tf_op jit(solution)/shard_map/ppermute | solution.py:31
  137.1 1.9 copy-start.1
  137.3 20.9 %collective-permute-start.12 = (bf16[2,2,1,1,2,40,640]{6,5,4,3,2,1,0:T(8,128)(2,1)S(1)}, bf16[2,2,1,1,2,40,640]{6,5,4,3,2,1,0:T(8,128)(2,1)S(1)}, u32[]{:S(2)}, u32[]{:S(2)}) collective-permute-start(bf16[2,2,1,1,2,40,640]{6,5,4,3,2,1,0:T(8,128)(2,1)S(1)} %get-tuple-element.127), channel_id=1, source_target_pairs={{0,4},{4,0},{8,12},{12,8},{16,20},{20,16},{24,28},{28,24},{1,5},{5... | collective-permute-start | bytes 1228808 | tf_op jit(solution)/shard_map/ppermute | solution.py:31
  141.0 20.9 %collective-permute-start.17 = (bf16[2,2,2,1,2,40,640]{6,5,4,3,2,1,0:T(8,128)(2,1)S(1)}, bf16[2,2,2,1,2,40,640]{6,5,4,3,2,1,0:T(8,128)(2,1)S(1)}, u32[]{:S(2)}, u32[]{:S(2)}) collective-permute-start(bf16[2,2,2,1,2,40,640]{6,5,4,3,2,1,0:T(8,128)(2,1)S(1)} %get-tuple-element.120), channel_id=1, source_target_pairs={{0,2},{2,0},{1,3},{3,1},{4,6},{6,4},{5,7},{7,5},{8,10},{10,8},{9,1... | collective-permute-start | bytes 2457608 | tf_op jit(solution)/shard_map/ppermute | solution.py:31
  153.1 22.0 %collective-permute-start.19 = (bf16[1,1,1,1,2,40,640]{6,5,4,3,2,1,0:T(8,128)(2,1)S(1)}, bf16[1,1,1,1,2,40,640]{6,5,4,3,2,1,0:T(8,128)(2,1)S(1)}, u32[]{:S(2)}, u32[]{:S(2)}) collective-permute-start(bf16[1,1,1,1,2,40,640]{6,5,4,3,2,1,0:T(8,128)(2,1)S(1)} %get-tuple-element.154), channel_id=1, source_target_pairs={{0,16},{4,20},{8,24},{12,28},{16,0},{20,4},{24,8},{28,12},{1,17},{... | collective-permute-start | bytes 307208 | tf_op jit(solution)/shard_map/ppermute | solution.py:31
  158.3 16.8 %collective-permute-start.16 = (bf16[2,1,1,1,2,40,640]{6,5,4,3,2,1,0:T(8,128)(2,1)S(1)}, bf16[2,1,1,1,2,40,640]{6,5,4,3,2,1,0:T(8,128)(2,1)S(1)}, u32[]{:S(2)}, u32[]{:S(2)}) collective-permute-start(bf16[2,1,1,1,2,40,640]{6,5,4,3,2,1,0:T(8,128)(2,1)S(1)} %get-tuple-element.137), channel_id=1, source_target_pairs={{0,8},{4,12},{8,0},{12,4},{16,24},{20,28},{24,16},{28,20},{1,9},{5... | collective-permute-start | bytes 614408 | tf_op jit(solution)/shard_map/ppermute | solution.py:31
  162.1 13.0 %collective-permute-start.18 = (bf16[2,2,1,1,2,40,640]{6,5,4,3,2,1,0:T(8,128)(2,1)S(1)}, bf16[2,2,1,1,2,40,640]{6,5,4,3,2,1,0:T(8,128)(2,1)S(1)}, u32[]{:S(2)}, u32[]{:S(2)}) collective-permute-start(bf16[2,2,1,1,2,40,640]{6,5,4,3,2,1,0:T(8,128)(2,1)S(1)} %get-tuple-element.126), channel_id=1, source_target_pairs={{0,4},{4,0},{8,12},{12,8},{16,20},{20,16},{24,28},{28,24},{1,5},{5... | collective-permute-start | bytes 1228808 | tf_op jit(solution)/shard_map/ppermute | solution.py:31
  175.2 13.1 %collective-permute-start.21 = (bf16[2,1,1,1,2,40,640]{6,5,4,3,2,1,0:T(8,128)(2,1)S(1)}, bf16[2,1,1,1,2,40,640]{6,5,4,3,2,1,0:T(8,128)(2,1)S(1)}, u32[]{:S(2)}, u32[]{:S(2)}) collective-permute-start(bf16[2,1,1,1,2,40,640]{6,5,4,3,2,1,0:T(8,128)(2,1)S(1)} %get-tuple-element.136), channel_id=1, source_target_pairs={{0,8},{4,12},{8,0},{12,4},{16,24},{20,28},{24,16},{28,20},{1,9},{5... | collective-permute-start | bytes 614408 | tf_op jit(solution)/shard_map/ppermute | solution.py:31
  175.4 14.7 %collective-permute-start.20 = (bf16[1,1,1,1,2,40,640]{6,5,4,3,2,1,0:T(8,128)(2,1)S(1)}, bf16[1,1,1,1,2,40,640]{6,5,4,3,2,1,0:T(8,128)(2,1)S(1)}, u32[]{:S(2)}, u32[]{:S(2)}) collective-permute-start(bf16[1,1,1,1,2,40,640]{6,5,4,3,2,1,0:T(8,128)(2,1)S(1)} %get-tuple-element.156), channel_id=1, source_target_pairs={{0,16},{4,20},{8,24},{12,28},{16,0},{20,4},{24,8},{28,12},{1,17},{... | collective-permute-start | bytes 307208 | tf_op jit(solution)/shard_map/ppermute | solution.py:31
  188.4 6.5 %collective-permute-start.24 = (bf16[1,1,1,1,2,40,640]{6,5,4,3,2,1,0:T(8,128)(2,1)S(1)}, bf16[1,1,1,1,2,40,640]{6,5,4,3,2,1,0:T(8,128)(2,1)S(1)}, u32[]{:S(2)}, u32[]{:S(2)}) collective-permute-start(bf16[1,1,1,1,2,40,640]{6,5,4,3,2,1,0:T(8,128)(2,1)S(1)} %add_convert_fusion.9), channel_id=1, source_target_pairs={{0,16},{4,20},{8,24},{12,28},{16,0},{20,4},{24,8},{28,12},{1,17},{... | collective-permute-start | bytes 307208 | tf_op jit(solution)/shard_map/ppermute | solution.py:31
  194.9 8.1 %collective-permute-start.25 = (f32[1,2,40,640]{3,2,1,0:T(8,128)S(1)}, f32[1,2,40,640]{3,2,1,0:T(8,128)S(1)}, u32[]{:S(2)}, u32[]{:S(2)}) collective-permute-start(f32[1,2,40,640]{3,2,1,0:T(8,128)S(1)} %add_bitcast_fusion), channel_id=1, source_target_pairs={{0,2},{2,0},{1,3},{3,1},{4,6},{6,4},{5,7},{7,5},{8,10},{10,8},{9,1... | collective-permute-start | bytes 614408 | tf_op jit(solution)/shard_map/ppermute | solution.py:31
  195.6 12.0 %collective-permute-start.22 = (f32[2,2,40,640]{3,2,1,0:T(8,128)S(1)}, f32[2,2,40,640]{3,2,1,0:T(8,128)S(1)}, u32[]{:S(2)}, u32[]{:S(2)}) collective-permute-start(f32[2,2,40,640]{3,2,1,0:T(8,128)S(1)} %pad_maximum_fusion.6), channel_id=1, source_target_pairs={{0,2},{2,0},{1,3},{3,1},{4,6},{6,4},{5,7},{7,5},{8,10},{10,8},{9,1... | collective-permute-start | bytes 1228808 | tf_op jit(solution)/shard_map/ppermute | solution.py:31
  203.1 5.8 %collective-permute-start.26 = (f32[1,4,40,640]{3,2,1,0:T(8,128)S(1)}, f32[1,4,40,640]{3,2,1,0:T(8,128)S(1)}, u32[]{:S(2)}, u32[]{:S(2)}) collective-permute-start(f32[1,4,40,640]{3,2,1,0:T(8,128)S(1)} %pad_maximum_fusion.7), channel_id=1, source_target_pairs={{0,1},{1,0},{2,3},{3,2},{4,5},{5,4},{6,7},{7,6},{8,9},{9,8},{10,11... | collective-permute-start | bytes 1228808 | tf_op jit(solution)/shard_map/ppermute | solution.py:31
  207.8 2.4 %collective-permute-start.23 = (f32[2,4,40,640]{3,2,1,0:T(8,128)S(1)}, f32[2,4,40,640]{3,2,1,0:T(8,128)S(1)}, u32[]{:S(2)}, u32[]{:S(2)}) collective-permute-start(f32[2,4,40,640]{3,2,1,0:T(8,128)S(1)} %pad_maximum_fusion.2), channel_id=1, source_target_pairs={{0,1},{1,0},{2,3},{3,2},{4,5},{5,4},{6,7},{7,6},{8,9},{9,8},{10,11... | collective-permute-start | bytes 2457608 | tf_op jit(solution)/shard_map/ppermute | solution.py:31
  210.5 1.2 copy-start.6
Sparse Core Ops, SparseCore 0:
  11.6 75.8 all-gather.3
Sparse Core Ops, SparseCore 1:
  130.8 60.3 all-gather.5

commit v6 on v5

--- a/solution.py
+++ b/solution.py
@@ -35,8 +35,8 @@
     return [1 << i for i in range(count.bit_length() - 1)]
 
 
-def params():
-    return pltpu.CompilerParams(vmem_limit_bytes=VMEM_BYTES)
+def params(size=VMEM_BYTES):
+    return pltpu.CompilerParams(vmem_limit_bytes=size)
 
 
 def cost(microseconds):
@@ -265,7 +265,7 @@
             jax.ShapeDtypeStruct((2 * outs, pixels // breadth + 2, breadth, 3 * channels), bf16),
             jax.ShapeDtypeStruct((1, channels), f32),
         ),
-        compiler_params=params(),
+        compiler_params=params(VMEM_BYTES // 2),
         cost_estimate=cost(6.5),
         name="hidden_grad",
     )(cot, following, temporal)
@@ -288,19 +288,23 @@
 
 
 def weight_grad_kernel(core_ref, x_ref, back_ref, keep_ref, send_ref):
-    store_halves(core_ref, matmul(x_ref[0], back_ref[...]), keep_ref, send_ref, 0, 0)
+    both = x_ref[...]
+    grads = matmul(both.reshape(both.shape[0] * both.shape[1], both.shape[2]), back_ref[...])
+    for k in range(2):
+        grad = grads[k * both.shape[1] : (k + 1) * both.shape[1]]
+        store_halves(core_ref, grad, keep_ref, send_ref, k, k)
 
 
 def weight_grad(turned, hidden_back, first, shards, core):
     rows, channels = hidden_back.shape
     half = channels // shards // 2
-    out_spec = pl.BlockSpec((shards, 1, half, channels), lambda i: (0, i, 0, 0))
+    out_spec = pl.BlockSpec((shards, 2, half, channels), lambda i: (0, i, 0, 0))
     return pl.pallas_call(
         weight_grad_kernel,
-        grid=(4,),
+        grid=(2,),
         in_specs=[
             pl.BlockSpec(memory_space=pltpu.SMEM),
-            pl.BlockSpec((1, channels, rows), lambda i: (first + i, 0, 0)),
+            pl.BlockSpec((2, channels, rows), lambda i: (first // 2 + i, 0, 0)),
             whole((rows, channels)),
         ],
         out_specs=(out_spec, out_spec),
@@ -320,12 +324,16 @@
     sends = ((one_ref, 0), (one_ref, 1), (two_ref, 0), (two_ref, 1))
     grad = matmul(x_ref[0], back_ref[...])
     store_halves(core_ref, grad, keep_ref, sends[0][0], 0, sends[0][1])
+    outs, pixels, channels = cot_ref.shape
+    seen = []
+    for o in range(outs):
+        first = before_ref[...] if o == 0 else hidden_ref[2 * o - 1]
+        seen.append(jnp.concatenate([first, hidden_ref[2 * o], hidden_ref[2 * o + 1]], axis=1))
+    grads = matmul_tn(
+        jnp.concatenate(seen, axis=0), cot_ref[...].reshape(outs * pixels, channels)
+    )
     for k in range(3):
-        grad = 0.0
-        for o in range(cot_ref.shape[0]):
-            frame = 2 * o + k - 1
-            x = before_ref[...] if frame < 0 else hidden_ref[frame]
-            grad += matmul_tn(x, cot_ref[o])
+        grad = grads[k * channels : (k + 1) * channels]
         store_halves(core_ref, grad, keep_ref, sends[1 + k][0], 1 + k, sends[1 + k][1])
 
 
@@ -612,8 +620,9 @@
     downsampled = temporal_forward(after(hidden, first, out_b), before, temporal_full)
     chain_b.land(downsampled)
     chain_c.land(downsampled)
-    out_c = chain_c.launch()
-    rows = join_x(jnp.stack([first, after(chain_b.finish(), out_c)]))
+    rows = jnp.stack([first, chain_b.finish()])
+    out_c = chain_c.launch(rows)
+    rows = join_x(rows)
     last_rows = join_core(join_x(chain_c.finish()[None]))[0]
     rows = join_core(rows)
     downsampled = downsampled.reshape(1, out_count, height, breadth, channels)

time: 220 us -> 216 us (0.982)
  Pallas kernels: 94.4 us -> 88.5 us
  other arithmetic: 20.8 us -> 16.7 us
  waiting for transfers between devices: 34.1 us -> 37.5 us
  local copies, waits for them, and re-layouts: 6.05 us -> 9.24 us
    pallas_call x1, Pallas kernels: 6.66 us -> 2.19 us  [hidden_gradient(): pl.pallas_call(lambda *refs: hidden_grad_kernel(breadth, *refs), out_shap...]
    all_gather x1, waiting for transfers between devices: 0.01 us -> 2.87 us  [body(): lax.all_gather(spatial_mine, ('dp', 'core'), axis=0, tiled=True)]
    add x7, other arithmetic: 6.48 us -> 3.87 us  [pick(): return kept + lax.dynamic_index_in_dim(self.got, which, spot).astype(f32)]
    unnamed x19, local copies, waits for them, and re-layouts: 5.42 us -> 7.88 us
  transfers between devices with their start and end apart: 29 -> 29, of which waited for: 11 -> 12; matrix products, arithmetic and copies ran while one was open for 10% -> 9% of each run, Pallas kernels for 43% -> 41%
where the time goes in v6:
time: 216 us; the launch traced here: 215 us
  Pallas kernels  88.5 us (41%)
  starting transfers between devices  44.4 us (21%)
  waiting for transfers between devices  37.5 us (17%)
  other arithmetic  16.7 us (8%)
  between operations  16.5 us (8%)
  local copies, waits for them, and re-layouts  9.24 us (4%)
  matrix products  2.34 us (1%)
    ppermute x25, starting transfers between devices, flip(): return lax.ppermute(x, axis, [(i, i ^ mask) for i in range(count)])  40 us
    ppermute x25, waiting for transfers between devices, flip(): return lax.ppermute(x, axis, [(i, i ^ mask) for i in range(count)])  33.7 us
    pallas_call x2, Pallas kernels, weight_grad(): pl.pallas_call(weight_grad_kernel, grid=(2,), in_specs=[pl.BlockSpec(memo...  17 us
    pallas_call x1, Pallas kernels, conv_forward(): pl.pallas_call(conv_forward_kernel, grid=(3,), in_specs=[whole(views.shap...  15.2 us
    pallas_call x1, Pallas kernels, conv_back_end(): pl.pallas_call(lambda *refs: conv_back_end_kernel(pixels * (channels // G...  12.1 us
    pallas_call x1, Pallas kernels, conv_back_start(): pl.pallas_call(conv_back_kernel, grid=(2,), in_specs=[whole(views.shape),...  11.7 us
    pallas_call x1, Pallas kernels, last_grad(): pl.pallas_call(last_grad_kernel, grid=(1,), in_specs=[pl.BlockSpec(memory...  9.09 us
    pallas_call x1, Pallas kernels, turned_columns(): pl.pallas_call(turn_kernel, grid=(3,), in_specs=[whole(views.shape)], out...  8.35 us
  transfers between devices with their start and end apart: 29, of which 12 were waited for; matrix products, arithmetic and copies ran while one was open for 9% of the time, Pallas kernels for 41%

profile of v6, /device:TPU:0, one launch (start us, length us, event | category | flops | bytes accessed | tf_op | source)
XLA Modules:
  0.0 215.3 jit_solution(2885755065597781721)
XLA Ops:
  8.1 1.9 fusion.1
  10.0 4.1 %collective-permute-start = (bf16[1,1,1,40,1280]{4,3,2,1,0:T(8,128)(2,1)S(1)}, bf16[1,1,1,40,1280]{4,3,2,1,0:T(8,128)(2,1)S(1)}, u32[]{:S(2)}, u32[]{:S(2)}) collective-permute-start(bf16[1,1,1,40,1280]{4,3,2,1,0:T(8,128)(2,1)S(1)} %dynamic-slice_bitcast_fusion), channel_id=1, source_target_pairs={{0,16},{4,20},{8,24},{12,28},{16,0},{20,4},{24,8},{28,12},{1,17},{... | collective-permute-start | bytes 307208 | tf_op jit(solution)/shard_map/ppermute | solution.py:31
  14.2 5.1 %collective-permute-done = bf16[1,1,1,40,1280]{4,3,2,1,0:T(8,128)(2,1)S(1)} collective-permute-done((bf16[1,1,1,40,1280]{4,3,2,1,0:T(8,128)(2,1)S(1)}, bf16[1,1,1,40,1280]{4,3,2,1,0:T(8,128)(2,1)S(1)}, u32[]{:S(2)}, u32[]{:S(2)}) %collective-permute-start) | collective-permute-done | bytes 102432 | tf_op jit(solution)/shard_map/ppermute | solution.py:31
  20.1 1.5 fusion.refs_1_.refs_6_
  21.6 5.3 %collective-permute-done.1 = bf16[2,1,1,40,1280]{4,3,2,1,0:T(8,128)(2,1)S(1)} collective-permute-done((bf16[2,1,1,40,1280]{4,3,2,1,0:T(8,128)(2,1)S(1)}, bf16[2,1,1,40,1280]{4,3,2,1,0:T(8,128)(2,1)S(1)}, u32[]{:S(2)}, u32[]{:S(2)}) %collective-permute-start.1) | collective-permute-done | bytes 204832 | tf_op jit(solution)/shard_map/ppermute | solution.py:31
  26.9 1.4 collective-permute-start.2
  28.3 7.7 %norm.1 = (bf16[4,18,16,1920]{3,2,1,0:T(8,128)(2,1)}, f32[4,1,640]{2,1,0:T(1,128)}, f32[4,1,640]{2,1,0:T(1,128)}) custom-call(bf16[4,256,640]{2,1,0:T(8,128)(2,1)} %bitcast.103, f32[640,640]{1,0:T(8,128)} %fusion.refs_1_.refs_6_), custom_call_target="tpu_custom_call" | custom-call | flops 8739999744 | bytes 760000 | tf_op jit(solution)/shard_map/norm/pallas_call | solution.py:210
  36.1 3.0 %collective-permute-done.2 = bf16[2,2,1,40,1280]{4,3,2,1,0:T(8,128)(2,1)S(1)} collective-permute-done((bf16[2,2,1,40,1280]{4,3,2,1,0:T(8,128)(2,1)S(1)}, bf16[2,2,1,40,1280]{4,3,2,1,0:T(8,128)(2,1)S(1)}, u32[]{:S(2)}, u32[]{:S(2)}) %collective-permute-start.2) | collective-permute-done | bytes 409632 | tf_op jit(solution)/shard_map/ppermute | solution.py:31
  39.2 1.5 collective-permute-start.4
  40.7 8.4 %turn.1 = bf16[3,1920,1024]{2,1,0:T(8,128)(2,1)} custom-call(bf16[4,18,16,1920]{3,2,1,0:T(8,128)(2,1)} %get-tuple-element.66.views_ref), custom_call_target="tpu_custom_call" | custom-call | flops 9774999552 | bytes 850000 | tf_op jit(solution)/shard_map/turn/pallas_call | solution.py:230
  49.8 1.1 pad_maximum_fusion.1
  51.9 1.5 collective-permute-start.3
  54.7 0.8 collective-permute-done.3.refs_1_
  55.6 2.2 %hidden_grad.1 = (bf16[4,256,640]{2,1,0:T(8,128)(2,1)S(1)}, bf16[4,18,16,1920]{3,2,1,0:T(8,128)(2,1)S(1)}, f32[1,640]{1,0:T(1,128)S(1)}) custom-call(bf16[2,256,640]{2,1,0:T(8,128)(2,1)S(1)} %bitcast.91, bf16[256,640]{1,0:T(8,128)(2,1)S(1)} %collective-permute-done.3.refs_1_, bf16[640,1920]{1,0:T(8,128)(2,1)S(1)} %bitcast.88), custom_call_target="tpu_custom_call" | custom-call | flops 7474999808 | bytes 650000 | tf_op jit(solution)/shard_map/hidden_grad/pallas_call | solution.py:261
  57.8 1.0 copy-done.2
  58.9 2.0 copy-done.3
  60.9 8.5 %weight_grad.2 = (f32[8,4,40,640]{3,2,1,0:T(8,128)}, bf16[8,4,40,640]{3,2,1,0:T(8,128)(2,1)}) custom-call(s32[1]{0:T(128)} %bitcast.4.core_ref, bf16[9,640,1024]{2,1,0:T(8,128)(2,1)} %bitcast.105, bf16[1024,640]{1,0:T(8,128)(2,1)} %bitcast.92), custom_call_target="tpu_custom_call" | custom-call | flops 9774999552 | bytes 850000 | tf_op jit(solution)/shard_map/weight_grad/pallas_call | solution.py:302
  69.3 5.7 %collective-permute-start.6 = (bf16[8,4,40,640]{3,2,1,0:T(8,128)(2,1)}, bf16[8,4,40,640]{3,2,1,0:T(8,128)(2,1)S(1)}, u32[]{:S(2)}, u32[]{:S(2)}) collective-permute-start(bf16[8,4,40,640]{3,2,1,0:T(8,128)(2,1)} %get-tuple-element.70), channel_id=1, source_target_pairs={{0,1},{1,0},{2,3},{3,2},{4,5},{5,4},{6,7},{7,6},{8,9},{9,8},{10,11... | collective-permute-start | bytes 4915208 | tf_op jit(solution)/shard_map/ppermute | solution.py:31
  75.7 8.6 %weight_grad.3 = (f32[8,4,40,640]{3,2,1,0:T(8,128)}, bf16[8,4,40,640]{3,2,1,0:T(8,128)(2,1)}) custom-call(s32[1]{0:T(128)} %bitcast.4.core_ref, bf16[9,640,1024]{2,1,0:T(8,128)(2,1)} %bitcast.106, bf16[1024,640]{1,0:T(8,128)(2,1)} %bitcast.93), custom_call_target="tpu_custom_call" | custom-call | flops 9774999552 | bytes 850000 | tf_op jit(solution)/shard_map/weight_grad/pallas_call | solution.py:302
  84.4 1.4 convert_add_fusion.1
  85.8 2.9 %all-gather.4.cloned.1.call-done.w_ref.refs_1_ = bf16[640,6016]{1,0:T(8,128)(2,1)} async-done(((bf16[40,6016]{1,0:T(8,128)(2,1)}), bf16[640,6016]{1,0:T(8,128)(2,1)}) %all-gather.4.cloned.1.call-update) | async-done | bytes 7700496 | tf_op jit(solution)/shard_map/all_gather | solution.py:554
  88.7 1.4 convolution_reduce_fusion
  90.6 15.2 %conv_forward.1 = (bf16[4,256,640]{2,1,0:T(8,128)(2,1)}, bf16[256,640]{1,0:T(8,128)(2,1)}) custom-call(bf16[4,18,16,1920]{3,2,1,0:T(8,128)(2,1)} %get-tuple-element.66.views_ref, bf16[640,6016]{1,0:T(8,128)(2,1)} %all-gather.4.cloned.1.call-done.w_ref.refs_1_, f32[1,640]{1,0:T(1,128)} %broadcast_in_dim.10.shift_ref), custom_call_target="tpu_custom_call" | custom-call | flops 17250000896 | bytes 1500000 | tf_op jit(solution)/shard_map/conv_forward/pallas_call | solution.py:416
  105.8 2.9 %collective-permute-start.8 = (bf16[256,640]{1,0:T(8,128)(2,1)}, bf16[256,640]{1,0:T(8,128)(2,1)}, u32[]{:S(2)}, u32[]{:S(2)}) collective-permute-start(bf16[256,640]{1,0:T(8,128)(2,1)} %get-tuple-element.79), channel_id=1, source_target_pairs={{0,1},{1,2},{2,3},{4,5},{5,6},{6,7},{8,9},{9,10},{10,11},{12,13},{... | collective-permute-start | bytes 983048 | tf_op jit(solution)/shard_map/ppermute | solution.py:592
  108.7 1.0 convert_add_fusion.5
  110.7 2.8 %add_convert_fusion.1 = (bf16[2,2,2,1,2,40,640]{6,5,4,3,2,1,0:T(8,128)(2,1)}, f32[2,2,2,1,2,40,640]{6,5,4,3,2,1,0:T(8,128)S(1)}) fusion(f32[2,2,2,2,2,40,640]{6,5,4,3,2,1,0:T(8,128)S(1)} %bitcast.95, s32[]{:T(128)S(6)} %select_n.243, bf16[2,2,2,2,2,40,640]{6,5,4,3,2,1,0:T(8,128)(2,1)} %bitcast.13, s32[]{:T(128)S(6)} %select_n.244), kind=kLoop, calls=%fused_computation.18 | loop fusion | flops 2048000 | bytes 7372808 | tf_op jit(solution)/shard_map/convert_element_type | solution.py:122
  113.5 3.9 %collective-permute-start.9 = (bf16[2,2,2,1,2,40,640]{6,5,4,3,2,1,0:T(8,128)(2,1)}, bf16[2,2,2,1,2,40,640]{6,5,4,3,2,1,0:T(8,128)(2,1)S(1)}, u32[]{:S(2)}, u32[]{:S(2)}) collective-permute-start(bf16[2,2,2,1,2,40,640]{6,5,4,3,2,1,0:T(8,128)(2,1)} %get-tuple-element.123), channel_id=1, source_target_pairs={{0,2},{2,0},{1,3},{3,1},{4,6},{6,4},{5,7},{7,5},{8,10},{10,8},{9,1... | collective-permute-start | bytes 2457608 | tf_op jit(solution)/shard_map/ppermute | solution.py:31
  117.4 9.1 %last_grad.1 = (f32[8,4,40,640]{3,2,1,0:T(8,128)}, bf16[8,2,40,640]{3,2,1,0:T(8,128)(2,1)}, bf16[8,2,40,640]{3,2,1,0:T(8,128)(2,1)}) custom-call(s32[1]{0:T(128)} %bitcast.4.core_ref, bf16[9,640,1024]{2,1,0:T(8,128)(2,1)} %bitcast.107, bf16[1024,640]{1,0:T(8,128)(2,1)} %bitcast.94, bf16[4,256,640]{2,1,0:T(8,128)(2,1)} %get-tuple-element.110.hidden_ref, ...), custom_call_target="tpu_custom_call" | custom-call | flops 11845000192 | bytes 1030000 | tf_op jit(solution)/shard_map/last_grad/pallas_call | solution.py:345
  127.7 1.1 convert_add_fusion.8
  128.8 1.2 collective-permute-start.15
  130.0 5.4 %collective-permute-done.9 = bf16[2,2,2,1,2,40,640]{6,5,4,3,2,1,0:T(8,128)(2,1)S(1)} collective-permute-done((bf16[2,2,2,1,2,40,640]{6,5,4,3,2,1,0:T(8,128)(2,1)}, bf16[2,2,2,1,2,40,640]{6,5,4,3,2,1,0:T(8,128)(2,1)S(1)}, u32[]{:S(2)}, u32[]{:S(2)}) %collective-permute-start.9) | collective-permute-done | bytes 819232 | tf_op jit(solution)/shard_map/ppermute | solution.py:31
  136.0 1.3 copy-done.5
  137.3 1.9 convert_add_fusion
  139.6 11.7 %conv_back_start.1.refs_2_ = f32[1024,640]{1,0:T(8,128)} custom-call(bf16[4,18,16,1920]{3,2,1,0:T(8,128)(2,1)} %copy-done.3, bf16[640,6016]{1,0:T(8,128)(2,1)} %all-gather.4.cloned.1.call-done.w_ref.refs_1_), custom_call_target="tpu_custom_call" | custom-call | flops 13799999488 | bytes 1200000 | tf_op jit(solution)/shard_map/conv_back_start/pallas_call | solution.py:465
  151.3 4.2 %collective-permute-start.19 = (bf16[1,1,1,1,2,40,640]{6,5,4,3,2,1,0:T(8,128)(2,1)S(1)}, bf16[1,1,1,1,2,40,640]{6,5,4,3,2,1,0:T(8,128)(2,1)S(1)}, u32[]{:S(2)}, u32[]{:S(2)}) collective-permute-start(bf16[1,1,1,1,2,40,640]{6,5,4,3,2,1,0:T(8,128)(2,1)S(1)} %get-tuple-element.154), channel_id=1, source_target_pairs={{0,16},{4,20},{8,24},{12,28},{16,0},{20,4},{24,8},{28,12},{1,17},{... | collective-permute-start | bytes 307208 | tf_op jit(solution)/shard_map/ppermute | solution.py:31
  155.7 3.8 %collective-permute-start.16 = (bf16[2,1,1,1,2,40,640]{6,5,4,3,2,1,0:T(8,128)(2,1)S(1)}, bf16[2,1,1,1,2,40,640]{6,5,4,3,2,1,0:T(8,128)(2,1)S(1)}, u32[]{:S(2)}, u32[]{:S(2)}) collective-permute-start(bf16[2,1,1,1,2,40,640]{6,5,4,3,2,1,0:T(8,128)(2,1)S(1)} %get-tuple-element.137), channel_id=1, source_target_pairs={{0,8},{4,12},{8,0},{12,4},{16,24},{20,28},{24,16},{28,20},{1,9},{5... | collective-permute-start | bytes 614408 | tf_op jit(solution)/shard_map/ppermute | solution.py:31
  159.6 1.0 collective-permute-start.18
  160.6 12.1 %conv_back_end.1 = f32[4,256,640]{2,1,0:T(8,128)} custom-call(bf16[4,18,16,1920]{3,2,1,0:T(8,128)(2,1)} %copy-done.3, bf16[640,6016]{1,0:T(8,128)(2,1)} %all-gather.4.cloned.1.call-done.w_ref.refs_1_, f32[1024,640]{1,0:T(8,128)} %conv_back_start.1.refs_2_, bf16[4,256,640]{2,1,0:T(8,128)(2,1)} %bitcast.104, f32[4,1,640]{2,1,0:T(1,128)} %get-tuple-element.64.refs_4_, ...), custom_call_target="tpu_custom_call" | custom-call | flops 13799999488 | bytes 1200000 | tf_op jit(solution)/shard_map/conv_back_end/pallas_call | solution.py:510
  173.0 7.6 %collective-permute-start.20 = (bf16[1,1,1,1,2,40,640]{6,5,4,3,2,1,0:T(8,128)(2,1)S(1)}, bf16[1,1,1,1,2,40,640]{6,5,4,3,2,1,0:T(8,128)(2,1)S(1)}, u32[]{:S(2)}, u32[]{:S(2)}) collective-permute-start(bf16[1,1,1,1,2,40,640]{6,5,4,3,2,1,0:T(8,128)(2,1)S(1)} %get-tuple-element.156), channel_id=1, source_target_pairs={{0,16},{4,20},{8,24},{12,28},{16,0},{20,4},{24,8},{28,12},{1,17},{... | collective-permute-start | bytes 307208 | tf_op jit(solution)/shard_map/ppermute | solution.py:31
  180.7 5.2 %temporal.1 = f32[2,256,640]{2,1,0:T(8,128)} custom-call(bf16[4,256,640]{2,1,0:T(8,128)(2,1)} %get-tuple-element.110.hidden_ref, bf16[256,640]{1,0:T(8,128)(2,1)} %collective-permute-done.8.before_ref, bf16[640,1920]{1,0:T(8,128)(2,1)} %bitcast.89), custom_call_target="tpu_custom_call" | custom-call | flops 5980000256 | bytes 520000 | tf_op jit(solution)/shard_map/temporal/pallas_call | solution.py:381
  186.8 4.8 %collective-permute-done.24 = bf16[1,1,1,1,2,40,640]{6,5,4,3,2,1,0:T(8,128)(2,1)S(1)} collective-permute-done((bf16[1,1,1,1,2,40,640]{6,5,4,3,2,1,0:T(8,128)(2,1)S(1)}, bf16[1,1,1,1,2,40,640]{6,5,4,3,2,1,0:T(8,128)(2,1)S(1)}, u32[]{:S(2)}, u32[]{:S(2)}) %collective-permute-start.24) | collective-permute-done | bytes 102432 | tf_op jit(solution)/shard_map/ppermute | solution.py:31
  192.0 1.7 collective-permute-start.21
  193.7 1.3 copy.21
  195.1 4.3 %collective-permute-done.25 = f32[1,2,40,640]{3,2,1,0:T(8,128)S(1)} collective-permute-done((f32[1,2,40,640]{3,2,1,0:T(8,128)S(1)}, f32[1,2,40,640]{3,2,1,0:T(8,128)S(1)}, u32[]{:S(2)}, u32[]{:S(2)}) %collective-permute-start.25) | collective-permute-done | bytes 204832 | tf_op jit(solution)/shard_map/ppermute | solution.py:31
  199.5 4.2 %collective-permute-done.21 = f32[2,2,40,640]{3,2,1,0:T(8,128)S(1)} collective-permute-done((f32[2,2,40,640]{3,2,1,0:T(8,128)S(1)}, f32[2,2,40,640]{3,2,1,0:T(8,128)S(1)}, u32[]{:S(2)}, u32[]{:S(2)}) %collective-permute-start.21) | collective-permute-done | bytes 409632 | tf_op jit(solution)/shard_map/ppermute | solution.py:31
  204.0 1.0 fusion.37
  205.1 0.9 pad_maximum_fusion.3
  206.6 1.2 copy-done.8
  (97 shorter events, 11.3 us)
Async XLA Ops:
  8.0 2.0 copy-start.7
  8.0 80.7 %all-gather.4.cloned.1.call-start = ((), (), s32[]{:S(2)}) async-start(), calls=%async_computation | async-start | bytes 8181760 | tf_op jit(solution)/shard_map/all_gather | solution.py:554
  10.0 183.8 %all-gather.6.cloned.1.call-start = ((), (), s32[]{:S(2)}) async-start(), calls=%async_computation.1 | async-start | bytes 1182720 | tf_op jit(solution)/shard_map/all_gather | solution.py:578
  10.0 9.2 %collective-permute-start = (bf16[1,1,1,40,1280]{4,3,2,1,0:T(8,128)(2,1)S(1)}, bf16[1,1,1,40,1280]{4,3,2,1,0:T(8,128)(2,1)S(1)}, u32[]{:S(2)}, u32[]{:S(2)}) collective-permute-start(bf16[1,1,1,40,1280]{4,3,2,1,0:T(8,128)(2,1)S(1)} %dynamic-slice_bitcast_fusion), channel_id=1, source_target_pairs={{0,16},{4,20},{8,24},{12,28},{16,0},{20,4},{24,8},{28,12},{1,17},{... | collective-permute-start | bytes 307208 | tf_op jit(solution)/shard_map/ppermute | solution.py:31
  19.3 7.6 %collective-permute-start.1 = (bf16[2,1,1,40,1280]{4,3,2,1,0:T(8,128)(2,1)S(1)}, bf16[2,1,1,40,1280]{4,3,2,1,0:T(8,128)(2,1)S(1)}, u32[]{:S(2)}, u32[]{:S(2)}) collective-permute-start(bf16[2,1,1,40,1280]{4,3,2,1,0:T(8,128)(2,1)S(1)} %pad_maximum_fusion.10), channel_id=1, source_target_pairs={{0,8},{4,12},{8,0},{12,4},{16,24},{20,28},{24,16},{28,20},{1,9},{5... | collective-permute-start | bytes 614408 | tf_op jit(solution)/shard_map/ppermute | solution.py:31
  26.9 12.1 %collective-permute-start.2 = (bf16[2,2,1,40,1280]{4,3,2,1,0:T(8,128)(2,1)S(1)}, bf16[2,2,1,40,1280]{4,3,2,1,0:T(8,128)(2,1)S(1)}, u32[]{:S(2)}, u32[]{:S(2)}) collective-permute-start(bf16[2,2,1,40,1280]{4,3,2,1,0:T(8,128)(2,1)S(1)} %pad_maximum_fusion.5), channel_id=1, source_target_pairs={{0,4},{4,0},{8,12},{12,8},{16,20},{20,16},{24,28},{28,24},{1,5},{5... | collective-permute-start | bytes 1228808 | tf_op jit(solution)/shard_map/ppermute | solution.py:31
  39.2 10.4 %collective-permute-start.4 = (bf16[2,2,2,40,640]{4,3,2,1,0:T(8,128)(2,1)S(1)}, bf16[2,2,2,40,640]{4,3,2,1,0:T(8,128)(2,1)S(1)}, u32[]{:S(2)}, u32[]{:S(2)}) collective-permute-start(bf16[2,2,2,40,640]{4,3,2,1,0:T(8,128)(2,1)S(1)} %broadcast_select_fusion.9), channel_id=1, source_target_pairs={{0,2},{2,0},{1,3},{3,1},{4,6},{6,4},{5,7},{7,5},{8,10},{10,8},{9,1... | collective-permute-start | bytes 1228808 | tf_op jit(solution)/shard_map/ppermute | solution.py:31
  49.8 1.3 copy-start.1
  51.0 3.1 %collective-permute-start.5 = (bf16[2,2,2,40,1920]{4,3,2,1,0:T(8,128)(2,1)}, bf16[2,2,2,40,1920]{4,3,2,1,0:T(8,128)(2,1)S(1)}, u32[]{:S(2)}, u32[]{:S(2)}) collective-permute-start(bf16[2,2,2,40,1920]{4,3,2,1,0:T(8,128)(2,1)} %pad_maximum_fusion.1), channel_id=1, source_target_pairs={{0,1},{1,0},{2,3},{3,2},{4,5},{5,4},{6,7},{7,6},{8,9},{9,8},{10,11... | collective-permute-start | bytes 3686408 | tf_op jit(solution)/shard_map/ppermute | solution.py:31
  51.9 3.7 %collective-permute-start.3 = (bf16[256,640]{1,0:T(8,128)(2,1)}, bf16[256,640]{1,0:T(8,128)(2,1)S(1)}, u32[]{:S(2)}, u32[]{:S(2)}) collective-permute-start(bf16[256,640]{1,0:T(8,128)(2,1)} %bitcast.7), channel_id=1, source_target_pairs={{1,0},{2,1},{3,2},{5,4},{6,5},{7,6},{9,8},{10,9},{11,10},{13,12},{... | collective-permute-start | bytes 983048 | tf_op jit(solution)/shard_map/ppermute | solution.py:550
  54.7 3.1 %copy-start = (bf16[2,2,2,80,1920]{4,3,2,1,0:T(8,128)(2,1)}, bf16[2,2,2,80,1920]{4,3,2,1,0:T(8,128)(2,1)S(1)}, u32[]{:S(2)}) copy-start(bf16[2,2,2,80,1920]{4,3,2,1,0:T(8,128)(2,1)S(1)} %pad_maximum_fusion) | copy-start | bytes 7372804
  57.8 1.1 copy-start.2
  58.8 2.0 copy-start.3
  69.3 15.1 %collective-permute-start.6 = (bf16[8,4,40,640]{3,2,1,0:T(8,128)(2,1)}, bf16[8,4,40,640]{3,2,1,0:T(8,128)(2,1)S(1)}, u32[]{:S(2)}, u32[]{:S(2)}) collective-permute-start(bf16[8,4,40,640]{3,2,1,0:T(8,128)(2,1)} %get-tuple-element.70), channel_id=1, source_target_pairs={{0,1},{1,0},{2,3},{3,2},{4,5},{5,4},{6,7},{7,6},{8,9},{9,8},{10,11... | collective-permute-start | bytes 4915208 | tf_op jit(solution)/shard_map/ppermute | solution.py:31
  75.7 8.7 %copy-start.6 = (f32[8,4,40,640]{3,2,1,0:T(8,128)S(1)}, f32[8,4,40,640]{3,2,1,0:T(8,128)}, u32[]{:S(2)}) copy-start(f32[8,4,40,640]{3,2,1,0:T(8,128)} %get-tuple-element.69) | copy-start | bytes 9830404
  84.3 24.4 %collective-permute-start.7 = (bf16[8,4,40,640]{3,2,1,0:T(8,128)(2,1)}, bf16[8,4,40,640]{3,2,1,0:T(8,128)(2,1)}, u32[]{:S(2)}, u32[]{:S(2)}) collective-permute-start(bf16[8,4,40,640]{3,2,1,0:T(8,128)(2,1)} %get-tuple-element.71), channel_id=1, source_target_pairs={{0,1},{1,0},{2,3},{3,2},{4,5},{5,4},{6,7},{7,6},{8,9},{9,8},{10,11... | collective-permute-start | bytes 4915208 | tf_op jit(solution)/shard_map/ppermute | solution.py:31
  85.8 22.9 %collective-permute-start.10 = (bf16[2,2,2,1,2,40,640]{6,5,4,3,2,1,0:T(8,128)(2,1)}, bf16[2,2,2,1,2,40,640]{6,5,4,3,2,1,0:T(8,128)(2,1)S(1)}, u32[]{:S(2)}, u32[]{:S(2)}) collective-permute-start(bf16[2,2,2,1,2,40,640]{6,5,4,3,2,1,0:T(8,128)(2,1)} %get-tuple-element.122), channel_id=1, source_target_pairs={{0,2},{2,0},{1,3},{3,1},{4,6},{6,4},{5,7},{7,5},{8,10},{10,8},{9,1... | collective-permute-start | bytes 2457608 | tf_op jit(solution)/shard_map/ppermute | solution.py:31
  105.8 4.2 %collective-permute-start.8 = (bf16[256,640]{1,0:T(8,128)(2,1)}, bf16[256,640]{1,0:T(8,128)(2,1)}, u32[]{:S(2)}, u32[]{:S(2)}) collective-permute-start(bf16[256,640]{1,0:T(8,128)(2,1)} %get-tuple-element.79), channel_id=1, source_target_pairs={{0,1},{1,2},{2,3},{4,5},{5,6},{6,7},{8,9},{9,10},{10,11},{12,13},{... | collective-permute-start | bytes 983048 | tf_op jit(solution)/shard_map/ppermute | solution.py:592
  108.7 2.1 copy-start.4
  109.6 18.1 %collective-permute-start.11 = (bf16[2,2,1,1,2,40,640]{6,5,4,3,2,1,0:T(8,128)(2,1)}, bf16[2,2,1,1,2,40,640]{6,5,4,3,2,1,0:T(8,128)(2,1)}, u32[]{:S(2)}, u32[]{:S(2)}) collective-permute-start(bf16[2,2,1,1,2,40,640]{6,5,4,3,2,1,0:T(8,128)(2,1)} %get-tuple-element.130), channel_id=1, source_target_pairs={{0,4},{4,0},{8,12},{12,8},{16,20},{20,16},{24,28},{28,24},{1,5},{5... | collective-permute-start | bytes 1228808 | tf_op jit(solution)/shard_map/ppermute | solution.py:31
  113.5 21.9 %collective-permute-start.9 = (bf16[2,2,2,1,2,40,640]{6,5,4,3,2,1,0:T(8,128)(2,1)}, bf16[2,2,2,1,2,40,640]{6,5,4,3,2,1,0:T(8,128)(2,1)S(1)}, u32[]{:S(2)}, u32[]{:S(2)}) collective-permute-start(bf16[2,2,2,1,2,40,640]{6,5,4,3,2,1,0:T(8,128)(2,1)} %get-tuple-element.123), channel_id=1, source_target_pairs={{0,2},{2,0},{1,3},{3,1},{4,6},{6,4},{5,7},{7,5},{8,10},{10,8},{9,1... | collective-permute-start | bytes 2457608 | tf_op jit(solution)/shard_map/ppermute | solution.py:31
  126.5 9.5 %collective-permute-start.14 = (bf16[8,2,40,640]{3,2,1,0:T(8,128)(2,1)}, bf16[8,2,40,640]{3,2,1,0:T(8,128)(2,1)}, u32[]{:S(2)}, u32[]{:S(2)}) collective-permute-start(bf16[8,2,40,640]{3,2,1,0:T(8,128)(2,1)} %get-tuple-element.84), channel_id=1, source_target_pairs={{0,1},{1,0},{2,3},{3,2},{4,5},{5,4},{6,7},{7,6},{8,9},{9,8},{10,11... | collective-permute-start | bytes 2457608 | tf_op jit(solution)/shard_map/ppermute | solution.py:31
  126.5 9.5 %collective-permute-start.13 = (bf16[8,2,40,640]{3,2,1,0:T(8,128)(2,1)}, bf16[8,2,40,640]{3,2,1,0:T(8,128)(2,1)}, u32[]{:S(2)}, u32[]{:S(2)}) collective-permute-start(bf16[8,2,40,640]{3,2,1,0:T(8,128)(2,1)} %get-tuple-element.92), channel_id=1, source_target_pairs={{0,1},{1,0},{2,3},{3,2},{4,5},{5,4},{6,7},{7,6},{8,9},{9,8},{10,11... | collective-permute-start | bytes 2457608 | tf_op jit(solution)/shard_map/ppermute | solution.py:31
  128.8 22.5 %collective-permute-start.15 = (bf16[2,1,1,1,2,40,640]{6,5,4,3,2,1,0:T(8,128)(2,1)S(1)}, bf16[2,1,1,1,2,40,640]{6,5,4,3,2,1,0:T(8,128)(2,1)S(1)}, u32[]{:S(2)}, u32[]{:S(2)}) collective-permute-start(bf16[2,1,1,1,2,40,640]{6,5,4,3,2,1,0:T(8,128)(2,1)S(1)} %get-tuple-element.140), channel_id=1, source_target_pairs={{0,8},{4,12},{8,0},{12,4},{16,24},{20,28},{24,16},{28,20},{1,9},{5... | collective-permute-start | bytes 614408 | tf_op jit(solution)/shard_map/ppermute | solution.py:31
  135.4 1.9 copy-start.5
  135.6 20.0 %collective-permute-start.12 = (bf16[2,2,1,1,2,40,640]{6,5,4,3,2,1,0:T(8,128)(2,1)S(1)}, bf16[2,2,1,1,2,40,640]{6,5,4,3,2,1,0:T(8,128)(2,1)S(1)}, u32[]{:S(2)}, u32[]{:S(2)}) collective-permute-start(bf16[2,2,1,1,2,40,640]{6,5,4,3,2,1,0:T(8,128)(2,1)S(1)} %get-tuple-element.127), channel_id=1, source_target_pairs={{0,4},{4,0},{8,12},{12,8},{16,20},{20,16},{24,28},{28,24},{1,5},{5... | collective-permute-start | bytes 1228808 | tf_op jit(solution)/shard_map/ppermute | solution.py:31
  139.3 20.2 %collective-permute-start.17 = (bf16[2,2,2,1,2,40,640]{6,5,4,3,2,1,0:T(8,128)(2,1)S(1)}, bf16[2,2,2,1,2,40,640]{6,5,4,3,2,1,0:T(8,128)(2,1)S(1)}, u32[]{:S(2)}, u32[]{:S(2)}) collective-permute-start(bf16[2,2,2,1,2,40,640]{6,5,4,3,2,1,0:T(8,128)(2,1)S(1)} %get-tuple-element.120), channel_id=1, source_target_pairs={{0,2},{2,0},{1,3},{3,1},{4,6},{6,4},{5,7},{7,5},{8,10},{10,8},{9,1... | collective-permute-start | bytes 2457608 | tf_op jit(solution)/shard_map/ppermute | solution.py:31
  151.3 21.4 %collective-permute-start.19 = (bf16[1,1,1,1,2,40,640]{6,5,4,3,2,1,0:T(8,128)(2,1)S(1)}, bf16[1,1,1,1,2,40,640]{6,5,4,3,2,1,0:T(8,128)(2,1)S(1)}, u32[]{:S(2)}, u32[]{:S(2)}) collective-permute-start(bf16[1,1,1,1,2,40,640]{6,5,4,3,2,1,0:T(8,128)(2,1)S(1)} %get-tuple-element.154), channel_id=1, source_target_pairs={{0,16},{4,20},{8,24},{12,28},{16,0},{20,4},{24,8},{28,12},{1,17},{... | collective-permute-start | bytes 307208 | tf_op jit(solution)/shard_map/ppermute | solution.py:31
  155.7 17.1 %collective-permute-start.16 = (bf16[2,1,1,1,2,40,640]{6,5,4,3,2,1,0:T(8,128)(2,1)S(1)}, bf16[2,1,1,1,2,40,640]{6,5,4,3,2,1,0:T(8,128)(2,1)S(1)}, u32[]{:S(2)}, u32[]{:S(2)}) collective-permute-start(bf16[2,1,1,1,2,40,640]{6,5,4,3,2,1,0:T(8,128)(2,1)S(1)} %get-tuple-element.137), channel_id=1, source_target_pairs={{0,8},{4,12},{8,0},{12,4},{16,24},{20,28},{24,16},{28,20},{1,9},{5... | collective-permute-start | bytes 614408 | tf_op jit(solution)/shard_map/ppermute | solution.py:31
  159.6 13.1 %collective-permute-start.18 = (bf16[2,2,1,1,2,40,640]{6,5,4,3,2,1,0:T(8,128)(2,1)S(1)}, bf16[2,2,1,1,2,40,640]{6,5,4,3,2,1,0:T(8,128)(2,1)S(1)}, u32[]{:S(2)}, u32[]{:S(2)}) collective-permute-start(bf16[2,2,1,1,2,40,640]{6,5,4,3,2,1,0:T(8,128)(2,1)S(1)} %get-tuple-element.126), channel_id=1, source_target_pairs={{0,4},{4,0},{8,12},{12,8},{16,20},{20,16},{24,28},{28,24},{1,5},{5... | collective-permute-start | bytes 1228808 | tf_op jit(solution)/shard_map/ppermute | solution.py:31
  172.9 13.0 %collective-permute-start.23 = (bf16[2,1,1,1,2,40,640]{6,5,4,3,2,1,0:T(8,128)(2,1)S(1)}, bf16[2,1,1,1,2,40,640]{6,5,4,3,2,1,0:T(8,128)(2,1)S(1)}, u32[]{:S(2)}, u32[]{:S(2)}) collective-permute-start(bf16[2,1,1,1,2,40,640]{6,5,4,3,2,1,0:T(8,128)(2,1)S(1)} %get-tuple-element.136), channel_id=1, source_target_pairs={{0,8},{4,12},{8,0},{12,4},{16,24},{20,28},{24,16},{28,20},{1,9},{5... | collective-permute-start | bytes 614408 | tf_op jit(solution)/shard_map/ppermute | solution.py:31
  173.0 12.8 %collective-permute-start.20 = (bf16[1,1,1,1,2,40,640]{6,5,4,3,2,1,0:T(8,128)(2,1)S(1)}, bf16[1,1,1,1,2,40,640]{6,5,4,3,2,1,0:T(8,128)(2,1)S(1)}, u32[]{:S(2)}, u32[]{:S(2)}) collective-permute-start(bf16[1,1,1,1,2,40,640]{6,5,4,3,2,1,0:T(8,128)(2,1)S(1)} %get-tuple-element.156), channel_id=1, source_target_pairs={{0,16},{4,20},{8,24},{12,28},{16,0},{20,4},{24,8},{28,12},{1,17},{... | collective-permute-start | bytes 307208 | tf_op jit(solution)/shard_map/ppermute | solution.py:31
  186.0 5.6 %collective-permute-start.24 = (bf16[1,1,1,1,2,40,640]{6,5,4,3,2,1,0:T(8,128)(2,1)S(1)}, bf16[1,1,1,1,2,40,640]{6,5,4,3,2,1,0:T(8,128)(2,1)S(1)}, u32[]{:S(2)}, u32[]{:S(2)}) collective-permute-start(bf16[1,1,1,1,2,40,640]{6,5,4,3,2,1,0:T(8,128)(2,1)S(1)} %add_convert_fusion.9), channel_id=1, source_target_pairs={{0,16},{4,20},{8,24},{12,28},{16,0},{20,4},{24,8},{28,12},{1,17},{... | collective-permute-start | bytes 307208 | tf_op jit(solution)/shard_map/ppermute | solution.py:31
  191.6 7.7 %collective-permute-start.25 = (f32[1,2,40,640]{3,2,1,0:T(8,128)S(1)}, f32[1,2,40,640]{3,2,1,0:T(8,128)S(1)}, u32[]{:S(2)}, u32[]{:S(2)}) collective-permute-start(f32[1,2,40,640]{3,2,1,0:T(8,128)S(1)} %add_bitcast_fusion), channel_id=1, source_target_pairs={{0,2},{2,0},{1,3},{3,1},{4,6},{6,4},{5,7},{7,5},{8,10},{10,8},{9,1... | collective-permute-start | bytes 614408 | tf_op jit(solution)/shard_map/ppermute | solution.py:31
  192.0 11.8 %collective-permute-start.21 = (f32[2,2,40,640]{3,2,1,0:T(8,128)S(1)}, f32[2,2,40,640]{3,2,1,0:T(8,128)S(1)}, u32[]{:S(2)}, u32[]{:S(2)}) collective-permute-start(f32[2,2,40,640]{3,2,1,0:T(8,128)S(1)} %pad_maximum_fusion.6), channel_id=1, source_target_pairs={{0,2},{2,0},{1,3},{3,1},{4,6},{6,4},{5,7},{7,5},{8,10},{10,8},{9,1... | collective-permute-start | bytes 1228808 | tf_op jit(solution)/shard_map/ppermute | solution.py:31
  199.4 5.5 %collective-permute-start.26 = (f32[1,4,40,640]{3,2,1,0:T(8,128)S(1)}, f32[1,4,40,640]{3,2,1,0:T(8,128)S(1)}, u32[]{:S(2)}, u32[]{:S(2)}) collective-permute-start(f32[1,4,40,640]{3,2,1,0:T(8,128)S(1)} %pad_maximum_fusion.7), channel_id=1, source_target_pairs={{0,1},{1,0},{2,3},{3,2},{4,5},{5,4},{6,7},{7,6},{8,9},{9,8},{10,11... | collective-permute-start | bytes 1228808 | tf_op jit(solution)/shard_map/ppermute | solution.py:31
  203.9 2.4 %collective-permute-start.22 = (f32[2,4,40,640]{3,2,1,0:T(8,128)S(1)}, f32[2,4,40,640]{3,2,1,0:T(8,128)S(1)}, u32[]{:S(2)}, u32[]{:S(2)}) collective-permute-start(f32[2,4,40,640]{3,2,1,0:T(8,128)S(1)} %pad_maximum_fusion.2), channel_id=1, source_target_pairs={{0,1},{1,0},{2,3},{3,2},{4,5},{5,4},{6,7},{7,6},{8,9},{9,8},{10,11... | collective-permute-start | bytes 2457608 | tf_op jit(solution)/shard_map/ppermute | solution.py:31
  206.6 1.2 copy-start.8
Sparse Core Ops, SparseCore 0:
  11.6 77.0 all-gather.3
Sparse Core Ops, SparseCore 1:
  127.8 58.6 all-gather.5

commit v7 on v6

--- a/solution.py
+++ b/solution.py
@@ -620,9 +620,10 @@
     downsampled = temporal_forward(after(hidden, first, out_b), before, temporal_full)
     chain_b.land(downsampled)
     chain_c.land(downsampled)
-    rows = jnp.stack([first, chain_b.finish()])
-    out_c = chain_c.launch(rows)
-    rows = join_x(rows)
+    rows = join_x(first[None], downsampled)
+    second = chain_b.finish()[None]
+    out_c = chain_c.launch(second)
+    rows = jnp.concatenate([rows, join_x(second)])
     last_rows = join_core(join_x(chain_c.finish()[None]))[0]
     rows = join_core(rows)
     downsampled = downsampled.reshape(1, out_count, height, breadth, channels)

time: 216 us -> 213 us (0.986)
  waiting for transfers between devices: 37.5 us -> 34.6 us
    ppermute x25 -> x26, waiting for transfers between devices: 33.7 us -> 30.9 us  [flip(): return lax.ppermute(x, axis, [(i, i ^ mask) for i in range(count)])]
    ppermute x25 -> x26, starting transfers between devices: 40 us -> 40.4 us  [flip(): return lax.ppermute(x, axis, [(i, i ^ mask) for i in range(count)])]
  transfers between devices with their start and end apart: 29 -> 30, of which waited for: 12 -> 12; matrix products, arithmetic and copies ran while one was open for 9% -> 9% of each run, Pallas kernels for 41% -> 42%
where the time goes in v7:
time: 213 us
  Pallas kernels  88.4 us (42%)
  starting transfers between devices  44.8 us (21%)
  waiting for transfers between devices  34.6 us (16%)
  other arithmetic  16.7 us (8%)
  between operations  16.5 us (8%)
  local copies, waits for them, and re-layouts  9.2 us (4%)
  matrix products  2.35 us (1%)
    ppermute x26, starting transfers between devices, flip(): return lax.ppermute(x, axis, [(i, i ^ mask) for i in range(count)])  40.4 us
    ppermute x26, waiting for transfers between devices, flip(): return lax.ppermute(x, axis, [(i, i ^ mask) for i in range(count)])  30.9 us
    pallas_call x2, Pallas kernels, weight_grad(): pl.pallas_call(weight_grad_kernel, grid=(2,), in_specs=[pl.BlockSpec(memo...  17.1 us
    pallas_call x1, Pallas kernels, conv_forward(): pl.pallas_call(conv_forward_kernel, grid=(3,), in_specs=[whole(views.shap...  15.2 us
    pallas_call x1, Pallas kernels, conv_back_end(): pl.pallas_call(lambda *refs: conv_back_end_kernel(pixels * (channels // G...  12.1 us
    pallas_call x1, Pallas kernels, conv_back_start(): pl.pallas_call(conv_back_kernel, grid=(2,), in_specs=[whole(views.shape),...  11.7 us
    pallas_call x1, Pallas kernels, last_grad(): pl.pallas_call(last_grad_kernel, grid=(1,), in_specs=[pl.BlockSpec(memory...  8.84 us
    pallas_call x1, Pallas kernels, turned_columns(): pl.pallas_call(turn_kernel, grid=(3,), in_specs=[whole(views.shape)], out...  8.38 us
  transfers between devices with their start and end apart: 30, of which 12 were waited for; matrix products, arithmetic and copies ran while one was open for 9% of the time, Pallas kernels for 42%

profile of v7, /device:TPU:0, one launch (start us, length us, event | category | flops | bytes accessed | tf_op | source)
XLA Modules:
  0.0 212.6 jit_solution(7073041179068959561)
XLA Ops:
  8.1 1.9 fusion.1
  10.0 4.1 %collective-permute-start = (bf16[1,1,1,40,1280]{4,3,2,1,0:T(8,128)(2,1)S(1)}, bf16[1,1,1,40,1280]{4,3,2,1,0:T(8,128)(2,1)S(1)}, u32[]{:S(2)}, u32[]{:S(2)}) collective-permute-start(bf16[1,1,1,40,1280]{4,3,2,1,0:T(8,128)(2,1)S(1)} %dynamic-slice_bitcast_fusion), channel_id=1, source_target_pairs={{0,16},{4,20},{8,24},{12,28},{16,0},{20,4},{24,8},{28,12},{1,17},{... | collective-permute-start | bytes 307208 | tf_op jit(solution)/shard_map/ppermute | solution.py:31
  14.2 5.1 %collective-permute-done = bf16[1,1,1,40,1280]{4,3,2,1,0:T(8,128)(2,1)S(1)} collective-permute-done((bf16[1,1,1,40,1280]{4,3,2,1,0:T(8,128)(2,1)S(1)}, bf16[1,1,1,40,1280]{4,3,2,1,0:T(8,128)(2,1)S(1)}, u32[]{:S(2)}, u32[]{:S(2)}) %collective-permute-start) | collective-permute-done | bytes 102432 | tf_op jit(solution)/shard_map/ppermute | solution.py:31
  20.1 1.5 fusion.refs_1_.refs_6_
  21.6 5.3 %collective-permute-done.1 = bf16[2,1,1,40,1280]{4,3,2,1,0:T(8,128)(2,1)S(1)} collective-permute-done((bf16[2,1,1,40,1280]{4,3,2,1,0:T(8,128)(2,1)S(1)}, bf16[2,1,1,40,1280]{4,3,2,1,0:T(8,128)(2,1)S(1)}, u32[]{:S(2)}, u32[]{:S(2)}) %collective-permute-start.1) | collective-permute-done | bytes 204832 | tf_op jit(solution)/shard_map/ppermute | solution.py:31
  26.9 1.4 collective-permute-start.2
  28.3 7.7 %norm.1 = (bf16[4,18,16,1920]{3,2,1,0:T(8,128)(2,1)}, f32[4,1,640]{2,1,0:T(1,128)}, f32[4,1,640]{2,1,0:T(1,128)}) custom-call(bf16[4,256,640]{2,1,0:T(8,128)(2,1)} %bitcast.103, f32[640,640]{1,0:T(8,128)} %fusion.refs_1_.refs_6_), custom_call_target="tpu_custom_call" | custom-call | flops 8739999744 | bytes 760000 | tf_op jit(solution)/shard_map/norm/pallas_call | solution.py:210
  36.0 3.0 %collective-permute-done.2 = bf16[2,2,1,40,1280]{4,3,2,1,0:T(8,128)(2,1)S(1)} collective-permute-done((bf16[2,2,1,40,1280]{4,3,2,1,0:T(8,128)(2,1)S(1)}, bf16[2,2,1,40,1280]{4,3,2,1,0:T(8,128)(2,1)S(1)}, u32[]{:S(2)}, u32[]{:S(2)}) %collective-permute-start.2) | collective-permute-done | bytes 409632 | tf_op jit(solution)/shard_map/ppermute | solution.py:31
  39.2 1.5 collective-permute-start.4
  40.7 8.4 %turn.1 = bf16[3,1920,1024]{2,1,0:T(8,128)(2,1)} custom-call(bf16[4,18,16,1920]{3,2,1,0:T(8,128)(2,1)} %get-tuple-element.68.views_ref), custom_call_target="tpu_custom_call" | custom-call | flops 9774999552 | bytes 850000 | tf_op jit(solution)/shard_map/turn/pallas_call | solution.py:230
  49.8 1.1 pad_maximum_fusion.1
  51.9 1.5 collective-permute-start.3
  55.6 2.2 %hidden_grad.1 = (bf16[4,256,640]{2,1,0:T(8,128)(2,1)S(1)}, bf16[4,18,16,1920]{3,2,1,0:T(8,128)(2,1)S(1)}, f32[1,640]{1,0:T(1,128)S(1)}) custom-call(bf16[2,256,640]{2,1,0:T(8,128)(2,1)S(1)} %bitcast.91, bf16[256,640]{1,0:T(8,128)(2,1)S(1)} %collective-permute-done.3.refs_1_, bf16[640,1920]{1,0:T(8,128)(2,1)S(1)} %bitcast.88), custom_call_target="tpu_custom_call" | custom-call | flops 7474999808 | bytes 650000 | tf_op jit(solution)/shard_map/hidden_grad/pallas_call | solution.py:261
  57.8 1.0 copy-done.2
  58.9 2.0 copy-done.3
  60.9 8.5 %weight_grad.2 = (f32[8,4,40,640]{3,2,1,0:T(8,128)}, bf16[8,4,40,640]{3,2,1,0:T(8,128)(2,1)}) custom-call(s32[1]{0:T(128)} %bitcast.4.core_ref, bf16[9,640,1024]{2,1,0:T(8,128)(2,1)} %bitcast.105, bf16[1024,640]{1,0:T(8,128)(2,1)} %bitcast.92), custom_call_target="tpu_custom_call" | custom-call | flops 9774999552 | bytes 850000 | tf_op jit(solution)/shard_map/weight_grad/pallas_call | solution.py:302
  69.4 5.7 %collective-permute-start.6 = (bf16[8,4,40,640]{3,2,1,0:T(8,128)(2,1)}, bf16[8,4,40,640]{3,2,1,0:T(8,128)(2,1)S(1)}, u32[]{:S(2)}, u32[]{:S(2)}) collective-permute-start(bf16[8,4,40,640]{3,2,1,0:T(8,128)(2,1)} %get-tuple-element.72), channel_id=1, source_target_pairs={{0,1},{1,0},{2,3},{3,2},{4,5},{5,4},{6,7},{7,6},{8,9},{9,8},{10,11... | collective-permute-start | bytes 4915208 | tf_op jit(solution)/shard_map/ppermute | solution.py:31
  75.8 8.6 %weight_grad.3 = (f32[8,4,40,640]{3,2,1,0:T(8,128)}, bf16[8,4,40,640]{3,2,1,0:T(8,128)(2,1)}) custom-call(s32[1]{0:T(128)} %bitcast.4.core_ref, bf16[9,640,1024]{2,1,0:T(8,128)(2,1)} %bitcast.106, bf16[1024,640]{1,0:T(8,128)(2,1)} %bitcast.93), custom_call_target="tpu_custom_call" | custom-call | flops 9774999552 | bytes 850000 | tf_op jit(solution)/shard_map/weight_grad/pallas_call | solution.py:302
  84.4 1.4 convert_add_fusion.1
  85.8 2.8 %all-gather.4.cloned.1.call-done.w_ref.refs_1_ = bf16[640,6016]{1,0:T(8,128)(2,1)} async-done(((bf16[40,6016]{1,0:T(8,128)(2,1)}), bf16[640,6016]{1,0:T(8,128)(2,1)}) %all-gather.4.cloned.1.call-update) | async-done | bytes 7700496 | tf_op jit(solution)/shard_map/all_gather | solution.py:554
  88.7 1.4 convolution_reduce_fusion
  90.6 15.2 %conv_forward.1 = (bf16[4,256,640]{2,1,0:T(8,128)(2,1)}, bf16[256,640]{1,0:T(8,128)(2,1)}) custom-call(bf16[4,18,16,1920]{3,2,1,0:T(8,128)(2,1)} %get-tuple-element.68.views_ref, bf16[640,6016]{1,0:T(8,128)(2,1)} %all-gather.4.cloned.1.call-done.w_ref.refs_1_, f32[1,640]{1,0:T(1,128)} %broadcast_in_dim.10.shift_ref), custom_call_target="tpu_custom_call" | custom-call | flops 17250000896 | bytes 1500000 | tf_op jit(solution)/shard_map/conv_forward/pallas_call | solution.py:416
  105.8 2.9 %collective-permute-start.8 = (bf16[256,640]{1,0:T(8,128)(2,1)}, bf16[256,640]{1,0:T(8,128)(2,1)}, u32[]{:S(2)}, u32[]{:S(2)}) collective-permute-start(bf16[256,640]{1,0:T(8,128)(2,1)} %get-tuple-element.81), channel_id=1, source_target_pairs={{0,1},{1,2},{2,3},{4,5},{5,6},{6,7},{8,9},{9,10},{10,11},{12,13},{... | collective-permute-start | bytes 983048 | tf_op jit(solution)/shard_map/ppermute | solution.py:592
  108.7 1.0 convert_add_fusion.5
  110.8 2.8 %add_convert_fusion.1 = (bf16[2,2,2,1,2,40,640]{6,5,4,3,2,1,0:T(8,128)(2,1)}, f32[2,2,2,1,2,40,640]{6,5,4,3,2,1,0:T(8,128)S(1)}) fusion(f32[2,2,2,2,2,40,640]{6,5,4,3,2,1,0:T(8,128)S(1)} %bitcast.95, s32[]{:T(128)S(6)} %select_n.247, bf16[2,2,2,2,2,40,640]{6,5,4,3,2,1,0:T(8,128)(2,1)} %bitcast.13, s32[]{:T(128)S(6)} %select_n.248), kind=kLoop, calls=%fused_computation.18 | loop fusion | flops 2048000 | bytes 7372808 | tf_op jit(solution)/shard_map/convert_element_type | solution.py:122
  113.6 3.9 %collective-permute-start.9 = (bf16[2,2,2,1,2,40,640]{6,5,4,3,2,1,0:T(8,128)(2,1)}, bf16[2,2,2,1,2,40,640]{6,5,4,3,2,1,0:T(8,128)(2,1)S(1)}, u32[]{:S(2)}, u32[]{:S(2)}) collective-permute-start(bf16[2,2,2,1,2,40,640]{6,5,4,3,2,1,0:T(8,128)(2,1)} %get-tuple-element.127), channel_id=1, source_target_pairs={{0,2},{2,0},{1,3},{3,1},{4,6},{6,4},{5,7},{7,5},{8,10},{10,8},{9,1... | collective-permute-start | bytes 2457608 | tf_op jit(solution)/shard_map/ppermute | solution.py:31
  117.4 8.8 %last_grad.1 = (f32[8,4,40,640]{3,2,1,0:T(8,128)}, bf16[8,2,40,640]{3,2,1,0:T(8,128)(2,1)}, bf16[8,2,40,640]{3,2,1,0:T(8,128)(2,1)}) custom-call(s32[1]{0:T(128)} %bitcast.4.core_ref, bf16[9,640,1024]{2,1,0:T(8,128)(2,1)} %bitcast.107, bf16[1024,640]{1,0:T(8,128)(2,1)} %bitcast.94, bf16[4,256,640]{2,1,0:T(8,128)(2,1)} %get-tuple-element.112.hidden_ref, ...), custom_call_target="tpu_custom_call" | custom-call | flops 11845000192 | bytes 1030000 | tf_op jit(solution)/shard_map/last_grad/pallas_call | solution.py:345
  127.5 1.1 convert_add_fusion.8
  128.6 1.2 collective-permute-start.15
  129.8 5.6 %collective-permute-done.9 = bf16[2,2,2,1,2,40,640]{6,5,4,3,2,1,0:T(8,128)(2,1)S(1)} collective-permute-done((bf16[2,2,2,1,2,40,640]{6,5,4,3,2,1,0:T(8,128)(2,1)}, bf16[2,2,2,1,2,40,640]{6,5,4,3,2,1,0:T(8,128)(2,1)S(1)}, u32[]{:S(2)}, u32[]{:S(2)}) %collective-permute-start.9) | collective-permute-done | bytes 819232 | tf_op jit(solution)/shard_map/ppermute | solution.py:31
  136.1 1.3 copy-done.5
  137.4 1.9 convert_add_fusion
  139.6 11.7 %conv_back_start.1.refs_2_ = f32[1024,640]{1,0:T(8,128)} custom-call(bf16[4,18,16,1920]{3,2,1,0:T(8,128)(2,1)} %copy-done.3, bf16[640,6016]{1,0:T(8,128)(2,1)} %all-gather.4.cloned.1.call-done.w_ref.refs_1_), custom_call_target="tpu_custom_call" | custom-call | flops 13799999488 | bytes 1200000 | tf_op jit(solution)/shard_map/conv_back_start/pallas_call | solution.py:465
  151.4 4.3 %collective-permute-start.19 = (bf16[1,1,1,1,2,40,640]{6,5,4,3,2,1,0:T(8,128)(2,1)S(1)}, bf16[1,1,1,1,2,40,640]{6,5,4,3,2,1,0:T(8,128)(2,1)S(1)}, u32[]{:S(2)}, u32[]{:S(2)}) collective-permute-start(bf16[1,1,1,1,2,40,640]{6,5,4,3,2,1,0:T(8,128)(2,1)S(1)} %get-tuple-element.156), channel_id=1, source_target_pairs={{0,16},{4,20},{8,24},{12,28},{16,0},{20,4},{24,8},{28,12},{1,17},{... | collective-permute-start | bytes 307208 | tf_op jit(solution)/shard_map/ppermute | solution.py:31
  155.8 3.8 %collective-permute-start.16 = (bf16[2,1,1,1,2,40,640]{6,5,4,3,2,1,0:T(8,128)(2,1)S(1)}, bf16[2,1,1,1,2,40,640]{6,5,4,3,2,1,0:T(8,128)(2,1)S(1)}, u32[]{:S(2)}, u32[]{:S(2)}) collective-permute-start(bf16[2,1,1,1,2,40,640]{6,5,4,3,2,1,0:T(8,128)(2,1)S(1)} %get-tuple-element.141), channel_id=1, source_target_pairs={{0,8},{4,12},{8,0},{12,4},{16,24},{20,28},{24,16},{28,20},{1,9},{5... | collective-permute-start | bytes 614408 | tf_op jit(solution)/shard_map/ppermute | solution.py:31
  159.8 0.9 collective-permute-start.18
  160.7 12.1 %conv_back_end.1 = f32[4,256,640]{2,1,0:T(8,128)} custom-call(bf16[4,18,16,1920]{3,2,1,0:T(8,128)(2,1)} %copy-done.3, bf16[640,6016]{1,0:T(8,128)(2,1)} %all-gather.4.cloned.1.call-done.w_ref.refs_1_, f32[1024,640]{1,0:T(8,128)} %conv_back_start.1.refs_2_, bf16[4,256,640]{2,1,0:T(8,128)(2,1)} %bitcast.104, f32[4,1,640]{2,1,0:T(1,128)} %get-tuple-element.66.refs_4_, ...), custom_call_target="tpu_custom_call" | custom-call | flops 13799999488 | bytes 1200000 | tf_op jit(solution)/shard_map/conv_back_end/pallas_call | solution.py:510
  172.8 1.8 collective-permute-start.20
  174.9 6.2 %collective-permute-start.21 = (bf16[1,1,1,1,2,40,640]{6,5,4,3,2,1,0:T(8,128)(2,1)S(1)}, bf16[1,1,1,1,2,40,640]{6,5,4,3,2,1,0:T(8,128)(2,1)S(1)}, u32[]{:S(2)}, u32[]{:S(2)}) collective-permute-start(bf16[1,1,1,1,2,40,640]{6,5,4,3,2,1,0:T(8,128)(2,1)S(1)} %get-tuple-element.158), channel_id=1, source_target_pairs={{0,16},{4,20},{8,24},{12,28},{16,0},{20,4},{24,8},{28,12},{1,17},{... | collective-permute-start | bytes 307208 | tf_op jit(solution)/shard_map/ppermute | solution.py:31
  181.1 5.2 %temporal.1 = f32[2,256,640]{2,1,0:T(8,128)} custom-call(bf16[4,256,640]{2,1,0:T(8,128)(2,1)} %get-tuple-element.112.hidden_ref, bf16[256,640]{1,0:T(8,128)(2,1)} %collective-permute-done.8.before_ref, bf16[640,1920]{1,0:T(8,128)(2,1)} %bitcast.89), custom_call_target="tpu_custom_call" | custom-call | flops 5980000256 | bytes 520000 | tf_op jit(solution)/shard_map/temporal/pallas_call | solution.py:381
  187.0 1.3 copy.21
  188.4 4.7 %collective-permute-done.25 = bf16[1,1,1,1,2,40,640]{6,5,4,3,2,1,0:T(8,128)(2,1)S(1)} collective-permute-done((bf16[1,1,1,1,2,40,640]{6,5,4,3,2,1,0:T(8,128)(2,1)S(1)}, bf16[1,1,1,1,2,40,640]{6,5,4,3,2,1,0:T(8,128)(2,1)S(1)}, u32[]{:S(2)}, u32[]{:S(2)}) %collective-permute-start.25) | collective-permute-done | bytes 102432 | tf_op jit(solution)/shard_map/ppermute | solution.py:31
  193.1 1.8 collective-permute-start.26
  195.3 3.6 %collective-permute-done.26 = f32[1,2,40,640]{3,2,1,0:T(8,128)S(1)} collective-permute-done((f32[1,2,40,640]{3,2,1,0:T(8,128)S(1)}, f32[1,2,40,640]{3,2,1,0:T(8,128)S(1)}, u32[]{:S(2)}, u32[]{:S(2)}) %collective-permute-start.26) | collective-permute-done | bytes 204832 | tf_op jit(solution)/shard_map/ppermute | solution.py:31
  199.0 2.0 collective-permute-done.22
  201.3 1.0 fusion.37
  202.4 0.9 pad_maximum_fusion.2
  203.9 1.2 copy-done.8
  (99 shorter events, 11.9 us)
Async XLA Ops:
  8.0 2.0 copy-start.7
  8.0 80.7 %all-gather.4.cloned.1.call-start = ((), (), s32[]{:S(2)}) async-start(), calls=%async_computation | async-start | bytes 8181760 | tf_op jit(solution)/shard_map/all_gather | solution.py:554
  10.0 177.1 %all-gather.6.cloned.1.call-start = ((), (), s32[]{:S(2)}) async-start(), calls=%async_computation.1 | async-start | bytes 1182720 | tf_op jit(solution)/shard_map/all_gather | solution.py:578
  10.0 9.2 %collective-permute-start = (bf16[1,1,1,40,1280]{4,3,2,1,0:T(8,128)(2,1)S(1)}, bf16[1,1,1,40,1280]{4,3,2,1,0:T(8,128)(2,1)S(1)}, u32[]{:S(2)}, u32[]{:S(2)}) collective-permute-start(bf16[1,1,1,40,1280]{4,3,2,1,0:T(8,128)(2,1)S(1)} %dynamic-slice_bitcast_fusion), channel_id=1, source_target_pairs={{0,16},{4,20},{8,24},{12,28},{16,0},{20,4},{24,8},{28,12},{1,17},{... | collective-permute-start | bytes 307208 | tf_op jit(solution)/shard_map/ppermute | solution.py:31
  19.3 7.6 %collective-permute-start.1 = (bf16[2,1,1,40,1280]{4,3,2,1,0:T(8,128)(2,1)S(1)}, bf16[2,1,1,40,1280]{4,3,2,1,0:T(8,128)(2,1)S(1)}, u32[]{:S(2)}, u32[]{:S(2)}) collective-permute-start(bf16[2,1,1,40,1280]{4,3,2,1,0:T(8,128)(2,1)S(1)} %pad_maximum_fusion.8), channel_id=1, source_target_pairs={{0,8},{4,12},{8,0},{12,4},{16,24},{20,28},{24,16},{28,20},{1,9},{5... | collective-permute-start | bytes 614408 | tf_op jit(solution)/shard_map/ppermute | solution.py:31
  26.9 12.1 %collective-permute-start.2 = (bf16[2,2,1,40,1280]{4,3,2,1,0:T(8,128)(2,1)S(1)}, bf16[2,2,1,40,1280]{4,3,2,1,0:T(8,128)(2,1)S(1)}, u32[]{:S(2)}, u32[]{:S(2)}) collective-permute-start(bf16[2,2,1,40,1280]{4,3,2,1,0:T(8,128)(2,1)S(1)} %pad_maximum_fusion.4), channel_id=1, source_target_pairs={{0,4},{4,0},{8,12},{12,8},{16,20},{20,16},{24,28},{28,24},{1,5},{5... | collective-permute-start | bytes 1228808 | tf_op jit(solution)/shard_map/ppermute | solution.py:31
  39.2 10.4 %collective-permute-start.4 = (bf16[2,2,2,40,640]{4,3,2,1,0:T(8,128)(2,1)S(1)}, bf16[2,2,2,40,640]{4,3,2,1,0:T(8,128)(2,1)S(1)}, u32[]{:S(2)}, u32[]{:S(2)}) collective-permute-start(bf16[2,2,2,40,640]{4,3,2,1,0:T(8,128)(2,1)S(1)} %broadcast_select_fusion.9), channel_id=1, source_target_pairs={{0,2},{2,0},{1,3},{3,1},{4,6},{6,4},{5,7},{7,5},{8,10},{10,8},{9,1... | collective-permute-start | bytes 1228808 | tf_op jit(solution)/shard_map/ppermute | solution.py:31
  49.8 1.3 copy-start.1
  51.0 3.1 %collective-permute-start.5 = (bf16[2,2,2,40,1920]{4,3,2,1,0:T(8,128)(2,1)}, bf16[2,2,2,40,1920]{4,3,2,1,0:T(8,128)(2,1)S(1)}, u32[]{:S(2)}, u32[]{:S(2)}) collective-permute-start(bf16[2,2,2,40,1920]{4,3,2,1,0:T(8,128)(2,1)} %pad_maximum_fusion.1), channel_id=1, source_target_pairs={{0,1},{1,0},{2,3},{3,2},{4,5},{5,4},{6,7},{7,6},{8,9},{9,8},{10,11... | collective-permute-start | bytes 3686408 | tf_op jit(solution)/shard_map/ppermute | solution.py:31
  51.9 3.7 %collective-permute-start.3 = (bf16[256,640]{1,0:T(8,128)(2,1)}, bf16[256,640]{1,0:T(8,128)(2,1)S(1)}, u32[]{:S(2)}, u32[]{:S(2)}) collective-permute-start(bf16[256,640]{1,0:T(8,128)(2,1)} %bitcast.7), channel_id=1, source_target_pairs={{1,0},{2,1},{3,2},{5,4},{6,5},{7,6},{9,8},{10,9},{11,10},{13,12},{... | collective-permute-start | bytes 983048 | tf_op jit(solution)/shard_map/ppermute | solution.py:550
  54.7 3.1 %copy-start = (bf16[2,2,2,80,1920]{4,3,2,1,0:T(8,128)(2,1)}, bf16[2,2,2,80,1920]{4,3,2,1,0:T(8,128)(2,1)S(1)}, u32[]{:S(2)}) copy-start(bf16[2,2,2,80,1920]{4,3,2,1,0:T(8,128)(2,1)S(1)} %pad_maximum_fusion) | copy-start | bytes 7372804
  57.8 1.1 copy-start.2
  58.8 2.0 copy-start.3
  69.4 15.1 %collective-permute-start.6 = (bf16[8,4,40,640]{3,2,1,0:T(8,128)(2,1)}, bf16[8,4,40,640]{3,2,1,0:T(8,128)(2,1)S(1)}, u32[]{:S(2)}, u32[]{:S(2)}) collective-permute-start(bf16[8,4,40,640]{3,2,1,0:T(8,128)(2,1)} %get-tuple-element.72), channel_id=1, source_target_pairs={{0,1},{1,0},{2,3},{3,2},{4,5},{5,4},{6,7},{7,6},{8,9},{9,8},{10,11... | collective-permute-start | bytes 4915208 | tf_op jit(solution)/shard_map/ppermute | solution.py:31
  75.8 8.7 %copy-start.6 = (f32[8,4,40,640]{3,2,1,0:T(8,128)S(1)}, f32[8,4,40,640]{3,2,1,0:T(8,128)}, u32[]{:S(2)}) copy-start(f32[8,4,40,640]{3,2,1,0:T(8,128)} %get-tuple-element.71) | copy-start | bytes 9830404
  84.3 24.4 %collective-permute-start.7 = (bf16[8,4,40,640]{3,2,1,0:T(8,128)(2,1)}, bf16[8,4,40,640]{3,2,1,0:T(8,128)(2,1)}, u32[]{:S(2)}, u32[]{:S(2)}) collective-permute-start(bf16[8,4,40,640]{3,2,1,0:T(8,128)(2,1)} %get-tuple-element.73), channel_id=1, source_target_pairs={{0,1},{1,0},{2,3},{3,2},{4,5},{5,4},{6,7},{7,6},{8,9},{9,8},{10,11... | collective-permute-start | bytes 4915208 | tf_op jit(solution)/shard_map/ppermute | solution.py:31
  85.8 22.9 %collective-permute-start.10 = (bf16[2,2,2,1,2,40,640]{6,5,4,3,2,1,0:T(8,128)(2,1)}, bf16[2,2,2,1,2,40,640]{6,5,4,3,2,1,0:T(8,128)(2,1)S(1)}, u32[]{:S(2)}, u32[]{:S(2)}) collective-permute-start(bf16[2,2,2,1,2,40,640]{6,5,4,3,2,1,0:T(8,128)(2,1)} %get-tuple-element.126), channel_id=1, source_target_pairs={{0,2},{2,0},{1,3},{3,1},{4,6},{6,4},{5,7},{7,5},{8,10},{10,8},{9,1... | collective-permute-start | bytes 2457608 | tf_op jit(solution)/shard_map/ppermute | solution.py:31
  105.8 4.2 %collective-permute-start.8 = (bf16[256,640]{1,0:T(8,128)(2,1)}, bf16[256,640]{1,0:T(8,128)(2,1)}, u32[]{:S(2)}, u32[]{:S(2)}) collective-permute-start(bf16[256,640]{1,0:T(8,128)(2,1)} %get-tuple-element.81), channel_id=1, source_target_pairs={{0,1},{1,2},{2,3},{4,5},{5,6},{6,7},{8,9},{9,10},{10,11},{12,13},{... | collective-permute-start | bytes 983048 | tf_op jit(solution)/shard_map/ppermute | solution.py:592
  108.7 2.1 copy-start.4
  109.7 17.8 %collective-permute-start.11 = (bf16[2,2,1,1,2,40,640]{6,5,4,3,2,1,0:T(8,128)(2,1)}, bf16[2,2,1,1,2,40,640]{6,5,4,3,2,1,0:T(8,128)(2,1)}, u32[]{:S(2)}, u32[]{:S(2)}) collective-permute-start(bf16[2,2,1,1,2,40,640]{6,5,4,3,2,1,0:T(8,128)(2,1)} %get-tuple-element.134), channel_id=1, source_target_pairs={{0,4},{4,0},{8,12},{12,8},{16,20},{20,16},{24,28},{28,24},{1,5},{5... | collective-permute-start | bytes 1228808 | tf_op jit(solution)/shard_map/ppermute | solution.py:31
  113.6 21.9 %collective-permute-start.9 = (bf16[2,2,2,1,2,40,640]{6,5,4,3,2,1,0:T(8,128)(2,1)}, bf16[2,2,2,1,2,40,640]{6,5,4,3,2,1,0:T(8,128)(2,1)S(1)}, u32[]{:S(2)}, u32[]{:S(2)}) collective-permute-start(bf16[2,2,2,1,2,40,640]{6,5,4,3,2,1,0:T(8,128)(2,1)} %get-tuple-element.127), channel_id=1, source_target_pairs={{0,2},{2,0},{1,3},{3,1},{4,6},{6,4},{5,7},{7,5},{8,10},{10,8},{9,1... | collective-permute-start | bytes 2457608 | tf_op jit(solution)/shard_map/ppermute | solution.py:31
  126.3 9.8 %collective-permute-start.14 = (bf16[8,2,40,640]{3,2,1,0:T(8,128)(2,1)}, bf16[8,2,40,640]{3,2,1,0:T(8,128)(2,1)}, u32[]{:S(2)}, u32[]{:S(2)}) collective-permute-start(bf16[8,2,40,640]{3,2,1,0:T(8,128)(2,1)} %get-tuple-element.86), channel_id=1, source_target_pairs={{0,1},{1,0},{2,3},{3,2},{4,5},{5,4},{6,7},{7,6},{8,9},{9,8},{10,11... | collective-permute-start | bytes 2457608 | tf_op jit(solution)/shard_map/ppermute | solution.py:31
  126.3 9.8 %collective-permute-start.13 = (bf16[8,2,40,640]{3,2,1,0:T(8,128)(2,1)}, bf16[8,2,40,640]{3,2,1,0:T(8,128)(2,1)}, u32[]{:S(2)}, u32[]{:S(2)}) collective-permute-start(bf16[8,2,40,640]{3,2,1,0:T(8,128)(2,1)} %get-tuple-element.94), channel_id=1, source_target_pairs={{0,1},{1,0},{2,3},{3,2},{4,5},{5,4},{6,7},{7,6},{8,9},{9,8},{10,11... | collective-permute-start | bytes 2457608 | tf_op jit(solution)/shard_map/ppermute | solution.py:31
  128.6 22.7 %collective-permute-start.15 = (bf16[2,1,1,1,2,40,640]{6,5,4,3,2,1,0:T(8,128)(2,1)S(1)}, bf16[2,1,1,1,2,40,640]{6,5,4,3,2,1,0:T(8,128)(2,1)S(1)}, u32[]{:S(2)}, u32[]{:S(2)}) collective-permute-start(bf16[2,1,1,1,2,40,640]{6,5,4,3,2,1,0:T(8,128)(2,1)S(1)} %get-tuple-element.144), channel_id=1, source_target_pairs={{0,8},{4,12},{8,0},{12,4},{16,24},{20,28},{24,16},{28,20},{1,9},{5... | collective-permute-start | bytes 614408 | tf_op jit(solution)/shard_map/ppermute | solution.py:31
  135.4 1.9 copy-start.5
  135.6 20.0 %collective-permute-start.12 = (bf16[2,2,1,1,2,40,640]{6,5,4,3,2,1,0:T(8,128)(2,1)S(1)}, bf16[2,2,1,1,2,40,640]{6,5,4,3,2,1,0:T(8,128)(2,1)S(1)}, u32[]{:S(2)}, u32[]{:S(2)}) collective-permute-start(bf16[2,2,1,1,2,40,640]{6,5,4,3,2,1,0:T(8,128)(2,1)S(1)} %get-tuple-element.131), channel_id=1, source_target_pairs={{0,4},{4,0},{8,12},{12,8},{16,20},{20,16},{24,28},{28,24},{1,5},{5... | collective-permute-start | bytes 1228808 | tf_op jit(solution)/shard_map/ppermute | solution.py:31
  139.3 20.3 %collective-permute-start.17 = (bf16[2,2,2,1,2,40,640]{6,5,4,3,2,1,0:T(8,128)(2,1)S(1)}, bf16[2,2,2,1,2,40,640]{6,5,4,3,2,1,0:T(8,128)(2,1)S(1)}, u32[]{:S(2)}, u32[]{:S(2)}) collective-permute-start(bf16[2,2,2,1,2,40,640]{6,5,4,3,2,1,0:T(8,128)(2,1)S(1)} %get-tuple-element.124), channel_id=1, source_target_pairs={{0,2},{2,0},{1,3},{3,1},{4,6},{6,4},{5,7},{7,5},{8,10},{10,8},{9,1... | collective-permute-start | bytes 2457608 | tf_op jit(solution)/shard_map/ppermute | solution.py:31
  151.4 21.4 %collective-permute-start.19 = (bf16[1,1,1,1,2,40,640]{6,5,4,3,2,1,0:T(8,128)(2,1)S(1)}, bf16[1,1,1,1,2,40,640]{6,5,4,3,2,1,0:T(8,128)(2,1)S(1)}, u32[]{:S(2)}, u32[]{:S(2)}) collective-permute-start(bf16[1,1,1,1,2,40,640]{6,5,4,3,2,1,0:T(8,128)(2,1)S(1)} %get-tuple-element.156), channel_id=1, source_target_pairs={{0,16},{4,20},{8,24},{12,28},{16,0},{20,4},{24,8},{28,12},{1,17},{... | collective-permute-start | bytes 307208 | tf_op jit(solution)/shard_map/ppermute | solution.py:31
  155.8 17.0 %collective-permute-start.16 = (bf16[2,1,1,1,2,40,640]{6,5,4,3,2,1,0:T(8,128)(2,1)S(1)}, bf16[2,1,1,1,2,40,640]{6,5,4,3,2,1,0:T(8,128)(2,1)S(1)}, u32[]{:S(2)}, u32[]{:S(2)}) collective-permute-start(bf16[2,1,1,1,2,40,640]{6,5,4,3,2,1,0:T(8,128)(2,1)S(1)} %get-tuple-element.141), channel_id=1, source_target_pairs={{0,8},{4,12},{8,0},{12,4},{16,24},{20,28},{24,16},{28,20},{1,9},{5... | collective-permute-start | bytes 614408 | tf_op jit(solution)/shard_map/ppermute | solution.py:31
  159.8 14.9 %collective-permute-start.18 = (bf16[2,2,1,1,2,40,640]{6,5,4,3,2,1,0:T(8,128)(2,1)S(1)}, bf16[2,2,1,1,2,40,640]{6,5,4,3,2,1,0:T(8,128)(2,1)S(1)}, u32[]{:S(2)}, u32[]{:S(2)}) collective-permute-start(bf16[2,2,1,1,2,40,640]{6,5,4,3,2,1,0:T(8,128)(2,1)S(1)} %get-tuple-element.130), channel_id=1, source_target_pairs={{0,4},{4,0},{8,12},{12,8},{16,20},{20,16},{24,28},{28,24},{1,5},{5... | collective-permute-start | bytes 1228808 | tf_op jit(solution)/shard_map/ppermute | solution.py:31
  172.8 15.6 %collective-permute-start.20 = (f32[1,2,40,640]{3,2,1,0:T(8,128)S(1)}, f32[1,2,40,640]{3,2,1,0:T(8,128)S(1)}, u32[]{:S(2)}, u32[]{:S(2)}) collective-permute-start(f32[1,2,40,640]{3,2,1,0:T(8,128)S(1)} %add_bitcast_fusion.2), channel_id=1, source_target_pairs={{0,2},{2,0},{1,3},{3,1},{4,6},{6,4},{5,7},{7,5},{8,10},{10,8},{9,1... | collective-permute-start | bytes 614408 | tf_op jit(solution)/shard_map/ppermute | solution.py:31
  174.7 11.5 %collective-permute-start.24 = (bf16[2,1,1,1,2,40,640]{6,5,4,3,2,1,0:T(8,128)(2,1)S(1)}, bf16[2,1,1,1,2,40,640]{6,5,4,3,2,1,0:T(8,128)(2,1)S(1)}, u32[]{:S(2)}, u32[]{:S(2)}) collective-permute-start(bf16[2,1,1,1,2,40,640]{6,5,4,3,2,1,0:T(8,128)(2,1)S(1)} %get-tuple-element.140), channel_id=1, source_target_pairs={{0,8},{4,12},{8,0},{12,4},{16,24},{20,28},{24,16},{28,20},{1,9},{5... | collective-permute-start | bytes 614408 | tf_op jit(solution)/shard_map/ppermute | solution.py:31
  174.9 11.4 %collective-permute-start.21 = (bf16[1,1,1,1,2,40,640]{6,5,4,3,2,1,0:T(8,128)(2,1)S(1)}, bf16[1,1,1,1,2,40,640]{6,5,4,3,2,1,0:T(8,128)(2,1)S(1)}, u32[]{:S(2)}, u32[]{:S(2)}) collective-permute-start(bf16[1,1,1,1,2,40,640]{6,5,4,3,2,1,0:T(8,128)(2,1)S(1)} %get-tuple-element.158), channel_id=1, source_target_pairs={{0,16},{4,20},{8,24},{12,28},{16,0},{20,4},{24,8},{28,12},{1,17},{... | collective-permute-start | bytes 307208 | tf_op jit(solution)/shard_map/ppermute | solution.py:31
  186.3 6.7 %collective-permute-start.25 = (bf16[1,1,1,1,2,40,640]{6,5,4,3,2,1,0:T(8,128)(2,1)S(1)}, bf16[1,1,1,1,2,40,640]{6,5,4,3,2,1,0:T(8,128)(2,1)S(1)}, u32[]{:S(2)}, u32[]{:S(2)}) collective-permute-start(bf16[1,1,1,1,2,40,640]{6,5,4,3,2,1,0:T(8,128)(2,1)S(1)} %add_convert_fusion.9), channel_id=1, source_target_pairs={{0,16},{4,20},{8,24},{12,28},{16,0},{20,4},{24,8},{28,12},{1,17},{... | collective-permute-start | bytes 307208 | tf_op jit(solution)/shard_map/ppermute | solution.py:31
  193.1 5.8 %collective-permute-start.26 = (f32[1,2,40,640]{3,2,1,0:T(8,128)S(1)}, f32[1,2,40,640]{3,2,1,0:T(8,128)S(1)}, u32[]{:S(2)}, u32[]{:S(2)}) collective-permute-start(f32[1,2,40,640]{3,2,1,0:T(8,128)S(1)} %add_bitcast_fusion), channel_id=1, source_target_pairs={{0,2},{2,0},{1,3},{3,1},{4,6},{6,4},{5,7},{7,5},{8,10},{10,8},{9,1... | collective-permute-start | bytes 614408 | tf_op jit(solution)/shard_map/ppermute | solution.py:31
  194.9 6.2 %collective-permute-start.22 = (f32[1,2,40,640]{3,2,1,0:T(8,128)S(1)}, f32[1,2,40,640]{3,2,1,0:T(8,128)S(1)}, u32[]{:S(2)}, u32[]{:S(2)}) collective-permute-start(f32[1,2,40,640]{3,2,1,0:T(8,128)S(1)} %add_bitcast_fusion.1), channel_id=1, source_target_pairs={{0,2},{2,0},{1,3},{3,1},{4,6},{6,4},{5,7},{7,5},{8,10},{10,8},{9,1... | collective-permute-start | bytes 614408 | tf_op jit(solution)/shard_map/ppermute | solution.py:31
  199.0 3.3 %collective-permute-start.27 = (f32[1,4,40,640]{3,2,1,0:T(8,128)S(1)}, f32[1,4,40,640]{3,2,1,0:T(8,128)S(1)}, u32[]{:S(2)}, u32[]{:S(2)}) collective-permute-start(f32[1,4,40,640]{3,2,1,0:T(8,128)S(1)} %pad_maximum_fusion.5), channel_id=1, source_target_pairs={{0,1},{1,0},{2,3},{3,2},{4,5},{5,4},{6,7},{7,6},{8,9},{9,8},{10,11... | collective-permute-start | bytes 1228808 | tf_op jit(solution)/shard_map/ppermute | solution.py:31
  201.2 2.4 %collective-permute-start.23 = (f32[2,4,40,640]{3,2,1,0:T(8,128)S(1)}, f32[2,4,40,640]{3,2,1,0:T(8,128)S(1)}, u32[]{:S(2)}, u32[]{:S(2)}) collective-permute-start(f32[2,4,40,640]{3,2,1,0:T(8,128)S(1)} %maximum_maximum_fusion), channel_id=1, source_target_pairs={{0,1},{1,0},{2,3},{3,2},{4,5},{5,4},{6,7},{7,6},{8,9},{9,8},{10,11... | collective-permute-start | bytes 2457608 | tf_op jit(solution)/shard_map/ppermute | solution.py:31
  203.9 1.2 copy-start.8
Sparse Core Ops, SparseCore 0:
  11.6 77.0 all-gather.3
Sparse Core Ops, SparseCore 1:
  127.5 58.7 all-gather.5
